TPU v7x, 512 devices: a whole 4x4x16 slice. The times are simulated.
512 devices in a mesh: gx: 32 (over y, z_lo), gy: 16 (over x, z_hi, core).
Axes of the slice: x: 4, y: 4, z: 16 (z_hi: 2, z_lo: 8; z = z_hi * 8 + z_lo), core: 2. Of those that a mesh axis runs over, the one named last changes fastest.
Arguments:
- latent: bfloat16 [128, 2048, 128], P('gx', 'gy'), may hold values from -6 to 6
- corr_kernel: bfloat16 [128, 128], replicated, may hold values from -0.5 to 0.5
- first_conv_weight: bfloat16 [3, 3, 128, 128], replicated, may hold values from -0.1875 to 0.1875
- first_conv_bias: float32 [128], replicated, may hold values from -3 to 3
- second_conv_weight: bfloat16 [3, 3, 128, 128], replicated, may hold values from -0.1875 to 0.1875
- second_conv_bias: float32 [128], replicated, may hold values from -3 to 3
- cotangent: bfloat16 [128, 2048, 128], P('gx', 'gy'), may hold values from -0.01171875 to 0.01171875
Outputs:
- prediction: bfloat16 [128, 2048, 128], P('gx', 'gy')
- conv1_weight_grad: float32 [3, 3, 128, 128], replicated
- conv1_bias_grad: float32 [128], replicated
- conv2_weight_grad: float32 [3, 3, 128, 128], replicated
- conv2_bias_grad: float32 [128], replicated
- kernel_grad: float32 [128, 128], replicated
All inputs are finite; a program needn't handle non-finite values.
Results may differ from a plain program's by a relative error of at most 0.0095.
Values may be sent and summed in bfloat16 or wider, within the bound.
No kernel may reach another device: no remote copies, remote signals or barrier semaphores. Data moves between devices by JAX's collectives and lax.ppermute only.
A program may use at most 64 MiB of HBM per device.

v0:
```python
import math

import jax
import jax.numpy as jnp
from jax import lax
from jax.sharding import PartitionSpec as P

DILATION_FIRST = 1
DILATION_SECOND = 2


def padded_2(array, sides, width):
    for axis, dim in sides:
        size, length = (lax.axis_size(axis), array.shape[dim])
        up = [(i, (i + 1) % size) for i in range(size)]
        down = [(j, i) for i, j in up]
        last = lax.slice_in_dim(array, length - width, length, axis=dim)
        leading = lax.slice_in_dim(array, 0, width, axis=dim)
        before = lax.ppermute(last, axis, up)
        after = lax.ppermute(leading, axis, down)
        array = jnp.concatenate([before, array, after], axis=dim)
    return array


def silu_slope(preact):
    logistic = jax.nn.sigmoid(preact)
    return logistic * (1.0 + preact * (1.0 - logistic))


def spectral_tables(length):
    positions = jnp.arange(length, dtype=jnp.int32)
    phases = positions[:, None] * positions[None, :] % length
    angles = phases.astype(jnp.float32) * (2.0 * math.pi / length)
    return (jnp.cos(angles), jnp.sin(angles))


def transform(table_mat, operand):
    return jnp.dot(
        table_mat, operand, precision=lax.Precision.HIGHEST, preferred_element_type=jnp.float32
    )


def to_columns(field):
    return lax.all_to_all(field, "gx", split_axis=1, concat_axis=0, tiled=True)


def surround(field, dilation):
    return padded_2(field, (("gx", 0), ("gy", 1)), dilation)


def forward_taps(padded, dilation, row_count, col_count, channels):
    windows = []
    for row_off in (-1, 0, 1):
        for col_off in (-1, 0, 1):
            row_at = dilation + row_off * dilation
            col_at = dilation + col_off * dilation
            windows.append(padded[row_at : row_at + row_count, col_at : col_at + col_count])
    return jnp.concatenate(windows, axis=-1).reshape(-1, 9 * channels)


def backward_taps(padded, dilation, row_count, col_count, channels):
    windows = []
    for row_off in (-1, 0, 1):
        for col_off in (-1, 0, 1):
            row_at = dilation - row_off * dilation
            col_at = dilation - col_off * dilation
            windows.append(padded[row_at : row_at + row_count, col_at : col_at + col_count])
    return jnp.concatenate(windows, axis=-1).reshape(-1, 9 * channels)


def layer_back(stored_item, gradient, row_count, col_count, channels):
    stacked, preact, weight, dilation = stored_item
    slope = (gradient * silu_slope(preact)).astype(jnp.bfloat16)
    flat_slope = slope.reshape(-1, channels)
    weight_grad = lax.dot_general(
        stacked, flat_slope, (((0,), (0,)), ((), ())), preferred_element_type=jnp.float32
    ).reshape(3, 3, channels, channels)
    bias_grad = jnp.sum(flat_slope.astype(jnp.float32), axis=0)
    stacked_back = backward_taps(
        surround(slope, dilation), dilation, row_count, col_count, channels
    )
    flipped = jnp.transpose(weight, (0, 1, 3, 2)).reshape(9 * channels, channels)
    carried = gradient + jnp.dot(stacked_back, flipped, preferred_element_type=jnp.float32).reshape(
        gradient.shape
    )
    return (weight_grad, bias_grad, carried)


def per_device(
    latent,
    corr_kernel,
    first_conv_weight,
    first_conv_bias,
    second_conv_weight,
    second_conv_bias,
    cotangent,
):
    row_count, col_count, channels = latent.shape
    full_rows = row_count * lax.axis_size("gx")
    columns = to_columns(latent)
    col_shape = columns.shape
    cosines, sines = spectral_tables(full_rows)
    flattened = columns.reshape(full_rows, -1).astype(jnp.float32)
    lat_real = transform(cosines, flattened).reshape(col_shape)
    lat_imag = (-transform(sines, flattened)).reshape(col_shape)
    kernel_f = corr_kernel.astype(jnp.float32)
    ker_real = transform(cosines, kernel_f)[:, None, :]
    ker_imag = (-transform(sines, kernel_f))[:, None, :]
    prod_real = (lat_real * ker_real + lat_imag * ker_imag).reshape(full_rows, -1)
    prod_imag = (lat_imag * ker_real - lat_real * ker_imag).reshape(full_rows, -1)
    correlated = (transform(cosines, prod_real) - transform(sines, prod_imag)) / full_rows
    mixed_cols = (columns.astype(jnp.float32) + correlated.reshape(col_shape)).astype(jnp.bfloat16)
    mixed_field = lax.all_to_all(mixed_cols, "gx", split_axis=0, concat_axis=1, tiled=True)
    stored = []
    current = mixed_field
    for weight, bias_vec, dilation in (
        (first_conv_weight, first_conv_bias, DILATION_FIRST),
        (second_conv_weight, second_conv_bias, DILATION_SECOND),
    ):
        stacked = forward_taps(
            surround(current, dilation), dilation, row_count, col_count, channels
        )
        preact = (
            jnp.dot(
                stacked, weight.reshape(9 * channels, channels), preferred_element_type=jnp.float32
            )
            + bias_vec
        )
        preact = preact.reshape(current.shape)
        stored.append((stacked, preact, weight, dilation))
        current = (current.astype(jnp.float32) + jax.nn.silu(preact)).astype(jnp.bfloat16)
    gradient = cotangent.astype(jnp.float32)
    second_weight_matrix, bias_two, gradient = layer_back(
        stored[1], gradient, row_count, col_count, channels
    )
    first_weight_matrix, bias_one, gradient = layer_back(
        stored[0], gradient, row_count, col_count, channels
    )
    mixed_gradient = gradient.astype(jnp.bfloat16)
    grad_cols = to_columns(mixed_gradient).reshape(full_rows, -1).astype(jnp.float32)
    grad_real = transform(cosines, grad_cols).reshape(col_shape)
    grad_imag = (-transform(sines, grad_cols)).reshape(col_shape)
    cross_real = jnp.sum(grad_real * lat_real + grad_imag * lat_imag, axis=1)
    cross_imag = jnp.sum(grad_real * lat_imag - grad_imag * lat_real, axis=1)
    kernel_grad = (transform(cosines, cross_real) - transform(sines, cross_imag)) / full_rows
    second_weight_matrix, bias_two, first_weight_matrix, bias_one, kernel_grad = lax.psum(
        (second_weight_matrix, bias_two, first_weight_matrix, bias_one, kernel_grad), ("gx", "gy")
    )
    return (current, first_weight_matrix, bias_one, second_weight_matrix, bias_two, kernel_grad)


def solution(mesh):
    in_specs = (P("gx", "gy", None), P(), P(), P(), P(), P(), P("gx", "gy", None))
    out_specs = (P("gx", "gy", None), P(), P(), P(), P(), P())
    return jax.shard_map(
        per_device, mesh=mesh, in_specs=in_specs, out_specs=out_specs, check_vma=False
    )
```

profile of v0, /device:TPU:1, one launch (start us, length us, event | category | flops | bytes accessed | tf_op | source)
XLA Modules:
  0.0 713.9 jit_solution(14996200767274391868)
XLA Ops:
  7.2 1.7 copy.39
  8.8 16.1 %all-to-all-start = ((bf16[4,128,128]{2,0,1:T(4,128)(2,1)}), bf16[4,128,128]{2,0,1:T(4,128)(2,1)S(1)}, u32[]{:S(2)}, u32[]{:S(2)}) async-start(bf16[4,128,128]{2,0,1:T(4,128)(2,1)} %copy.39), calls=%async_computation | async-start | bytes 262144 | tf_op jit(solution)/shard_map/all_to_all | solution.py:44
  25.9 10.8 %all-to-all-done = bf16[4,128,128]{2,0,1:T(4,128)(2,1)S(1)} async-done(((bf16[4,128,128]{2,0,1:T(4,128)(2,1)}), bf16[4,128,128]{2,0,1:T(4,128)(2,1)S(1)}, u32[]{:S(2)}, u32[]{:S(2)}) %all-to-all-start) | async-done | bytes 131104 | tf_op jit(solution)/shard_map/all_to_all | solution.py:44
  37.6 1.2 multiply_subtract_fusion
  38.8 0.6 fusion.30
  39.5 0.7 fusion
  40.3 18.6 %all_to_all.48 = bf16[128,4,128]{2,1,0:T(4,128)(2,1)S(1)} all-to-all(bf16[128,4,128]{2,1,0:T(4,128)(2,1)S(1)} %fusion.4), channel_id=1, replica_groups=mesh['gx'=32,'gy'=16] {'gx'}, dimensions={0} | all-to-all | bytes 262144 | tf_op jit(solution)/shard_map/all_to_all | solution.py:113
  59.0 2.6 collective-permute-start
  61.6 11.4 %collective-permute-start.1 = (bf16[1,128,128]{2,1,0:T(8,128)(2,1)S(1)}, bf16[1,128,128]{2,1,0:T(8,128)(2,1)S(1)}, u32[]{:S(2)}, u32[]{:S(2)}) collective-permute-start(bf16[1,128,128]{2,1,0:T(8,128)(2,1)S(1)} %bitcast.165), channel_id=1, source_target_pairs={{16,0},{32,16},{48,32},{64,48},{80,64},{96,80},{112,96},{128,112},... | collective-permute-start | bytes 98312 | tf_op jit(solution)/shard_map/ppermute | solution.py:20
  73.0 1.0 collective-permute-done.1
  74.0 12.6 %collective-permute-start.2 = (bf16[6,1,128]{2,1,0:T(2,128)(2,1)S(1)}, bf16[6,1,128]{2,1,0:T(2,128)(2,1)S(1)}, u32[]{:S(2)}, u32[]{:S(2)}) collective-permute-start(bf16[6,1,128]{2,1,0:T(2,128)(2,1)S(1)} %get-tuple-element.41), channel_id=1, source_target_pairs={{0,1},{1,2},{2,3},{3,4},{4,5},{5,6},{6,7},{7,8},{8,9},{9,10},{10,1... | collective-permute-start | bytes 4616 | tf_op jit(solution)/shard_map/ppermute | solution.py:19
  86.6 1.9 collective-permute-start.3
  88.6 11.7 %collective-permute-done.3 = bf16[6,1,128]{2,1,0:T(2,128)(2,1)S(1)} collective-permute-done((bf16[6,1,128]{2,1,0:T(2,128)(2,1)S(1)}, bf16[6,1,128]{2,1,0:T(2,128)(2,1)S(1)}, u32[]{:S(2)}, u32[]{:S(2)}) %collective-permute-start.3) | collective-permute-done | bytes 1568 | tf_op jit(solution)/shard_map/ppermute | solution.py:20
  100.8 0.6 copy-done.2
  102.0 1.9 collective-permute-start.4
  103.9 12.7 %collective-permute-start.5 = (bf16[2,128,128]{2,1,0:T(8,128)(2,1)S(1)}, bf16[2,128,128]{2,1,0:T(8,128)(2,1)S(1)}, u32[]{:S(2)}, u32[]{:S(2)}) collective-permute-start(bf16[2,128,128]{2,1,0:T(8,128)(2,1)S(1)} %get-tuple-element.47), channel_id=1, source_target_pairs={{16,0},{32,16},{48,32},{64,48},{80,64},{96,80},{112,96},{128,112},... | collective-permute-start | bytes 196616 | tf_op jit(solution)/shard_map/ppermute | solution.py:20
  116.7 1.2 collective-permute-done.5
  117.9 2.8 collective-permute-start.6
  120.7 1.9 collective-permute-start.7
  122.7 11.7 %collective-permute-done.7 = bf16[8,2,128]{2,1,0:T(2,128)(2,1)S(1)} collective-permute-done((bf16[8,2,128]{2,1,0:T(2,128)(2,1)S(1)}, bf16[8,2,128]{2,1,0:T(2,128)(2,1)S(1)}, u32[]{:S(2)}, u32[]{:S(2)}) %collective-permute-start.7) | collective-permute-done | bytes 4128 | tf_op jit(solution)/shard_map/ppermute | solution.py:20
  135.5 1.3 convert_reduce_fusion
  136.8 1.9 collective-permute-start.8
  138.7 12.8 %collective-permute-start.9 = (bf16[2,128,128]{2,1,0:T(8,128)(2,1)S(1)}, bf16[2,128,128]{2,1,0:T(8,128)(2,1)S(1)}, u32[]{:S(2)}, u32[]{:S(2)}) collective-permute-start(bf16[2,128,128]{2,1,0:T(8,128)(2,1)S(1)} %get-tuple-element.45), channel_id=1, source_target_pairs={{16,0},{32,16},{48,32},{64,48},{80,64},{96,80},{112,96},{128,112},... | collective-permute-start | bytes 196616 | tf_op jit(solution)/shard_map/ppermute | solution.py:20
  151.5 1.3 collective-permute-done.9
  152.9 1.9 collective-permute-start.10
  154.8 12.4 %collective-permute-start.11 = (bf16[8,2,128]{2,1,0:T(2,128)(2,1)S(1)}, bf16[8,2,128]{2,1,0:T(2,128)(2,1)S(1)}, u32[]{:S(2)}, u32[]{:S(2)}) collective-permute-start(bf16[8,2,128]{2,1,0:T(2,128)(2,1)S(1)} %get-tuple-element.21), channel_id=1, source_target_pairs={{0,1},{1,2},{2,3},{3,4},{4,5},{5,6},{6,7},{7,8},{8,9},{9,10},{10,1... | collective-permute-start | bytes 12296 | tf_op jit(solution)/shard_map/ppermute | solution.py:19
  167.4 0.8 collective-permute-done.11
  168.8 1.2 convert_reduce_fusion.1
  170.0 1.9 collective-permute-start.12
  171.9 12.4 %collective-permute-start.13 = (bf16[1,128,128]{2,1,0:T(8,128)(2,1)S(1)}, bf16[1,128,128]{2,1,0:T(8,128)(2,1)S(1)}, u32[]{:S(2)}, u32[]{:S(2)}) collective-permute-start(bf16[1,128,128]{2,1,0:T(8,128)(2,1)S(1)} %get-tuple-element.43), channel_id=1, source_target_pairs={{16,0},{32,16},{48,32},{64,48},{80,64},{96,80},{112,96},{128,112},... | collective-permute-start | bytes 98312 | tf_op jit(solution)/shard_map/ppermute | solution.py:20
  184.3 1.0 collective-permute-done.13
  185.3 15.9 %collective-permute-start.14 = (bf16[6,1,128]{2,1,0:T(2,128)(2,1)S(1)}, bf16[6,1,128]{2,1,0:T(2,128)(2,1)S(1)}, u32[]{:S(2)}, u32[]{:S(2)}) collective-permute-start(bf16[6,1,128]{2,1,0:T(2,128)(2,1)S(1)} %get-tuple-element.37), channel_id=1, source_target_pairs={{1,0},{2,1},{3,2},{4,3},{5,4},{6,5},{7,6},{8,7},{9,8},{10,9},{11,1... | collective-permute-start | bytes 4616 | tf_op jit(solution)/shard_map/ppermute | solution.py:20
  201.3 1.9 collective-permute-start.15
  203.4 0.6 copy.46
  204.0 1.6 copy.48
  206.2 0.5 copy-done.6
  207.2 0.8 copy.50
  207.9 12.4 %all-to-all-start.2 = ((bf16[4,128,128]{2,0,1:T(4,128)(2,1)}), bf16[4,128,128]{2,0,1:T(4,128)(2,1)S(1)}, u32[]{:S(2)}, u32[]{:S(2)}) async-start(bf16[4,128,128]{2,0,1:T(4,128)(2,1)} %copy.50), calls=%async_computation.2 | async-start | bytes 262144 | tf_op jit(solution)/shard_map/all_to_all | solution.py:44
  220.6 1.3 fusion.89
  221.9 1.3 fusion.88
  223.2 9.0 %all-to-all-done.2 = bf16[4,128,128]{2,0,1:T(4,128)(2,1)S(1)} async-done(((bf16[4,128,128]{2,0,1:T(4,128)(2,1)}), bf16[4,128,128]{2,0,1:T(4,128)(2,1)S(1)}, u32[]{:S(2)}, u32[]{:S(2)}) %all-to-all-start.2) | async-done | bytes 131104 | tf_op jit(solution)/shard_map/all_to_all | solution.py:44
  233.0 0.5 subtract_reduce_fusion
  234.0 1.1 fusion.2
  235.1 110.6 %all-reduce = (f32[128]{0:T(128)}, f32[128]{0:T(128)}) all-reduce(f32[128]{0:T(128)S(1)} %get-tuple-element.15, f32[128]{0:T(128)S(1)} %get-tuple-element.13), channel_id=1, replica_groups=mesh['gx'=32,'gy'=16] {'gx','gy'}, use_global_device_ids=true, to_apply=%region_2.3 | all-reduce | flops 256 | bytes 2048 | tf_op jit(solution)/shard_map/psum | solution.py:146
  345.7 357.9 %all-reduce.4.cloned.1.call-done = (f32[3,3,128,128]{3,2,1,0:T(8,128)}, f32[3,3,128,128]{3,2,1,0:T(8,128)}, f32[128,128]{1,0:T(8,128)}) async-done(((f32[3,3,128,128]{3,2,1,0:T(8,128)}, f32[3,3,128,128]{3,2,1,0:T(8,128)}, f32[128,128]{1,0:T(8,128)}), (f32[3,3,128,128]{3,2,1,0:T(8,128)}, f32[3,3,128,128]{3,2,1,0:T(8,128)}, f32[128,128]{1,0:T(8,128)})) %all-reduce.4.cloned.1.call-update) | async-done | bytes 1245200 | tf_op jit(solution)/shard_map/psum | solution.py:146
  703.6 2.0 copy.112
  705.6 0.8 copy.113
  706.4 0.6 copy.114
  (103 shorter events, 7.7 us)
Async XLA Ops:
  7.2 17.8 %copy-start = (bf16[128,128]{1,0:T(8,128)(2,1)S(1)}, bf16[128,128]{1,0:T(8,128)(2,1)}, u32[]{:S(2)}) copy-start(bf16[128,128]{1,0:T(8,128)(2,1)} %param.8) | copy-start | bytes 98308
  8.8 27.9 %all-to-all-start = ((bf16[4,128,128]{2,0,1:T(4,128)(2,1)}), bf16[4,128,128]{2,0,1:T(4,128)(2,1)S(1)}, u32[]{:S(2)}, u32[]{:S(2)}) async-start(bf16[4,128,128]{2,0,1:T(4,128)(2,1)} %copy.39), calls=%async_computation | async-start | bytes 262144 | tf_op jit(solution)/shard_map/all_to_all | solution.py:44
  59.0 14.0 %collective-permute-start = (bf16[1,128,128]{2,1,0:T(8,128)(2,1)S(1)}, bf16[1,128,128]{2,1,0:T(8,128)(2,1)S(1)}, u32[]{:S(2)}, u32[]{:S(2)}) collective-permute-start(bf16[1,128,128]{2,1,0:T(8,128)(2,1)S(1)} %bitcast.166), channel_id=1, source_target_pairs={{0,16},{16,32},{32,48},{48,64},{64,80},{80,96},{96,112},{112,128},... | collective-permute-start | bytes 98312 | tf_op jit(solution)/shard_map/ppermute | solution.py:19
  61.6 12.4 %collective-permute-start.1 = (bf16[1,128,128]{2,1,0:T(8,128)(2,1)S(1)}, bf16[1,128,128]{2,1,0:T(8,128)(2,1)S(1)}, u32[]{:S(2)}, u32[]{:S(2)}) collective-permute-start(bf16[1,128,128]{2,1,0:T(8,128)(2,1)S(1)} %bitcast.165), channel_id=1, source_target_pairs={{16,0},{32,16},{48,32},{64,48},{80,64},{96,80},{112,96},{128,112},... | collective-permute-start | bytes 98312 | tf_op jit(solution)/shard_map/ppermute | solution.py:20
  74.0 14.5 %collective-permute-start.2 = (bf16[6,1,128]{2,1,0:T(2,128)(2,1)S(1)}, bf16[6,1,128]{2,1,0:T(2,128)(2,1)S(1)}, u32[]{:S(2)}, u32[]{:S(2)}) collective-permute-start(bf16[6,1,128]{2,1,0:T(2,128)(2,1)S(1)} %get-tuple-element.41), channel_id=1, source_target_pairs={{0,1},{1,2},{2,3},{3,4},{4,5},{5,6},{6,7},{7,8},{8,9},{9,10},{10,1... | collective-permute-start | bytes 4616 | tf_op jit(solution)/shard_map/ppermute | solution.py:19
  86.6 13.6 %collective-permute-start.3 = (bf16[6,1,128]{2,1,0:T(2,128)(2,1)S(1)}, bf16[6,1,128]{2,1,0:T(2,128)(2,1)S(1)}, u32[]{:S(2)}, u32[]{:S(2)}) collective-permute-start(bf16[6,1,128]{2,1,0:T(2,128)(2,1)S(1)} %get-tuple-element.40), channel_id=1, source_target_pairs={{1,0},{2,1},{3,2},{4,3},{5,4},{6,5},{7,6},{8,7},{9,8},{10,9},{11,1... | collective-permute-start | bytes 4616 | tf_op jit(solution)/shard_map/ppermute | solution.py:20
  100.4 1.0 copy-start.2
  100.4 1.0 copy-start.8
  102.0 14.8 %collective-permute-start.4 = (bf16[2,128,128]{2,1,0:T(8,128)(2,1)S(1)}, bf16[2,128,128]{2,1,0:T(8,128)(2,1)S(1)}, u32[]{:S(2)}, u32[]{:S(2)}) collective-permute-start(bf16[2,128,128]{2,1,0:T(8,128)(2,1)S(1)} %get-tuple-element.46), channel_id=1, source_target_pairs={{0,16},{16,32},{32,48},{48,64},{64,80},{80,96},{96,112},{112,128},... | collective-permute-start | bytes 196616 | tf_op jit(solution)/shard_map/ppermute | solution.py:19
  103.9 14.0 %collective-permute-start.5 = (bf16[2,128,128]{2,1,0:T(8,128)(2,1)S(1)}, bf16[2,128,128]{2,1,0:T(8,128)(2,1)S(1)}, u32[]{:S(2)}, u32[]{:S(2)}) collective-permute-start(bf16[2,128,128]{2,1,0:T(8,128)(2,1)S(1)} %get-tuple-element.47), channel_id=1, source_target_pairs={{16,0},{32,16},{48,32},{64,48},{80,64},{96,80},{112,96},{128,112},... | collective-permute-start | bytes 196616 | tf_op jit(solution)/shard_map/ppermute | solution.py:20
  117.9 4.7 collective-permute-start.6
  120.7 13.6 %collective-permute-start.7 = (bf16[8,2,128]{2,1,0:T(2,128)(2,1)S(1)}, bf16[8,2,128]{2,1,0:T(2,128)(2,1)S(1)}, u32[]{:S(2)}, u32[]{:S(2)}) collective-permute-start(bf16[8,2,128]{2,1,0:T(2,128)(2,1)S(1)} %get-tuple-element.26), channel_id=1, source_target_pairs={{1,0},{2,1},{3,2},{4,3},{5,4},{6,5},{7,6},{8,7},{9,8},{10,9},{11,1... | collective-permute-start | bytes 12296 | tf_op jit(solution)/shard_map/ppermute | solution.py:20
  134.5 1.0 copy-start.5
  134.5 1.0 copy-start.9
  134.5 1.0 copy-start.10
  135.0 1.8 copy-start.1
  136.8 14.7 %collective-permute-start.8 = (bf16[2,128,128]{2,1,0:T(8,128)(2,1)S(1)}, bf16[2,128,128]{2,1,0:T(8,128)(2,1)S(1)}, u32[]{:S(2)}, u32[]{:S(2)}) collective-permute-start(bf16[2,128,128]{2,1,0:T(8,128)(2,1)S(1)} %get-tuple-element.44), channel_id=1, source_target_pairs={{0,16},{16,32},{32,48},{48,64},{64,80},{80,96},{96,112},{112,128},... | collective-permute-start | bytes 196616 | tf_op jit(solution)/shard_map/ppermute | solution.py:19
  138.7 14.1 %collective-permute-start.9 = (bf16[2,128,128]{2,1,0:T(8,128)(2,1)S(1)}, bf16[2,128,128]{2,1,0:T(8,128)(2,1)S(1)}, u32[]{:S(2)}, u32[]{:S(2)}) collective-permute-start(bf16[2,128,128]{2,1,0:T(8,128)(2,1)S(1)} %get-tuple-element.45), channel_id=1, source_target_pairs={{16,0},{32,16},{48,32},{64,48},{80,64},{96,80},{112,96},{128,112},... | collective-permute-start | bytes 196616 | tf_op jit(solution)/shard_map/ppermute | solution.py:20
  152.9 14.5 %collective-permute-start.10 = (bf16[8,2,128]{2,1,0:T(2,128)(2,1)S(1)}, bf16[8,2,128]{2,1,0:T(2,128)(2,1)S(1)}, u32[]{:S(2)}, u32[]{:S(2)}) collective-permute-start(bf16[8,2,128]{2,1,0:T(2,128)(2,1)S(1)} %get-tuple-element.22), channel_id=1, source_target_pairs={{1,0},{2,1},{3,2},{4,3},{5,4},{6,5},{7,6},{8,7},{9,8},{10,9},{11,1... | collective-permute-start | bytes 12296 | tf_op jit(solution)/shard_map/ppermute | solution.py:20
  154.8 13.4 %collective-permute-start.11 = (bf16[8,2,128]{2,1,0:T(2,128)(2,1)S(1)}, bf16[8,2,128]{2,1,0:T(2,128)(2,1)S(1)}, u32[]{:S(2)}, u32[]{:S(2)}) collective-permute-start(bf16[8,2,128]{2,1,0:T(2,128)(2,1)S(1)} %get-tuple-element.21), channel_id=1, source_target_pairs={{0,1},{1,2},{2,3},{3,4},{4,5},{5,6},{6,7},{7,8},{8,9},{9,10},{10,1... | collective-permute-start | bytes 12296 | tf_op jit(solution)/shard_map/ppermute | solution.py:19
  170.0 14.4 %collective-permute-start.12 = (bf16[1,128,128]{2,1,0:T(8,128)(2,1)S(1)}, bf16[1,128,128]{2,1,0:T(8,128)(2,1)S(1)}, u32[]{:S(2)}, u32[]{:S(2)}) collective-permute-start(bf16[1,128,128]{2,1,0:T(8,128)(2,1)S(1)} %get-tuple-element.42), channel_id=1, source_target_pairs={{0,16},{16,32},{32,48},{48,64},{64,80},{80,96},{96,112},{112,128},... | collective-permute-start | bytes 98312 | tf_op jit(solution)/shard_map/ppermute | solution.py:19
  171.9 13.4 %collective-permute-start.13 = (bf16[1,128,128]{2,1,0:T(8,128)(2,1)S(1)}, bf16[1,128,128]{2,1,0:T(8,128)(2,1)S(1)}, u32[]{:S(2)}, u32[]{:S(2)}) collective-permute-start(bf16[1,128,128]{2,1,0:T(8,128)(2,1)S(1)} %get-tuple-element.43), channel_id=1, source_target_pairs={{16,0},{32,16},{48,32},{64,48},{80,64},{96,80},{112,96},{128,112},... | collective-permute-start | bytes 98312 | tf_op jit(solution)/shard_map/ppermute | solution.py:20
  185.3 20.3 %collective-permute-start.14 = (bf16[6,1,128]{2,1,0:T(2,128)(2,1)S(1)}, bf16[6,1,128]{2,1,0:T(2,128)(2,1)S(1)}, u32[]{:S(2)}, u32[]{:S(2)}) collective-permute-start(bf16[6,1,128]{2,1,0:T(2,128)(2,1)S(1)} %get-tuple-element.37), channel_id=1, source_target_pairs={{1,0},{2,1},{3,2},{4,3},{5,4},{6,5},{7,6},{8,7},{9,8},{10,9},{11,1... | collective-permute-start | bytes 4616 | tf_op jit(solution)/shard_map/ppermute | solution.py:20
  201.3 4.4 collective-permute-start.15
  205.7 1.0 copy-start.6
  207.9 24.2 %all-to-all-start.2 = ((bf16[4,128,128]{2,0,1:T(4,128)(2,1)}), bf16[4,128,128]{2,0,1:T(4,128)(2,1)S(1)}, u32[]{:S(2)}, u32[]{:S(2)}) async-start(bf16[4,128,128]{2,0,1:T(4,128)(2,1)} %copy.50), calls=%async_computation.2 | async-start | bytes 262144 | tf_op jit(solution)/shard_map/all_to_all | solution.py:44
  220.4 483.2 %all-reduce.4.cloned.1.call-start = ((), (), s32[]{:S(2)}) async-start(), calls=%async_computation.3 | async-start | bytes 2490368 | tf_op jit(solution)/shard_map/psum | solution.py:146
  223.2 9.8 %copy-start.3 = (f32[128,4,128]{0,2,1:T(8,128)S(1)}, f32[128,4,128]{0,2,1:T(8,128)}, u32[]{:S(2)}) copy-start(f32[128,4,128]{0,2,1:T(8,128)} %get-tuple-element.54) | copy-start | bytes 786436
  703.6 2.0 copy-start.4
  703.6 2.8 copy-start.7
Sparse Core Ops, SparseCore 0:
  235.3 468.3 all-reduce.3
where the time goes:
time: 715 us; the launch traced here: 714 us
  waiting for transfers between devices  406 us (57%)
  starting transfers between devices  138 us (19%)
  blocking collectives  129 us (18%)
  between operations  14.8 us (2%)
  matrix products  12.5 us (2%)
  local copies, waits for them, and re-layouts  12.3 us (2%)
    psum x1, waiting for transfers between devices, per_device(): lax.psum((second_weight_matrix, bias_two, first_weight_matrix, bias_one,...  358 us
    psum x1, blocking collectives, per_device(): lax.psum((second_weight_matrix, bias_two, first_weight_matrix, bias_one,...  111 us
    ppermute x8, starting transfers between devices, padded_2(): after = lax.ppermute(leading, axis, down)  71 us
    ppermute x8, starting transfers between devices, padded_2(): before = lax.ppermute(last, axis, up)  38 us
    all_to_all x2, starting transfers between devices, to_columns(): return lax.all_to_all(field, 'gx', split_axis=1, concat_axis=0, tiled=True)  28.5 us
    ppermute x8, waiting for transfers between devices, padded_2(): after = lax.ppermute(leading, axis, down)  27.8 us
    all_to_all x2, waiting for transfers between devices, to_columns(): return lax.all_to_all(field, 'gx', split_axis=1, concat_axis=0, tiled=True)  19.8 us
    all_to_all x1, blocking collectives, per_device(): lax.all_to_all(mixed_cols, 'gx', split_axis=0, concat_axis=1, tiled=True)  18.6 us
  transfers between devices with their start and end apart: 19, of which 11 were waited for; matrix products, arithmetic and copies ran while one was open for 1% of the time, Pallas kernels for 0%

commit v1 on v0

v1 whole, which is shorter than its diff:
```python
import jax
import jax.numpy as jnp
import numpy as np
from jax import lax
from jax.sharding import Mesh, PartitionSpec as P

ROWS_AXES = ("y", "zl")
COLS_AXES = ("x", "zh", "c")
PLANE_AXES = ("y", "x", "c")
DEPTH_AXES = ("zl", "zh")
N_ROWS = 128
OWN = 4
HALO_LAT = 5
HALO_COT = 2
GRAD_ROWS = 2560


def real_transform(order):
    freq = np.arange(64)
    angle = 2.0 * np.pi * ((freq[:, None] * order[None, :]) % N_ROWS) / N_ROWS
    sines = np.sin(angle)
    sines[0] = np.cos(np.pi * order)
    return np.concatenate([np.cos(angle), sines])


def split_two(table):
    high = table.astype(jnp.bfloat16)
    low = (table - high.astype(np.float64)).astype(jnp.bfloat16)
    return high, low


def silu_slope(preact):
    logistic = jax.nn.sigmoid(preact)
    return logistic * (1.0 + preact * (1.0 - logistic))


def shift_rows(x, step):
    width, _, channels = x.shape
    x = x.reshape(width, 4, 32, channels)
    if step > 0:
        out = jnp.concatenate([x[:, step:], jnp.roll(x[:, :step], -1, axis=2)], axis=1)
    elif step < 0:
        out = jnp.concatenate([jnp.roll(x[:, step:], 1, axis=2), x[:, :step]], axis=1)
    else:
        out = x
    return out.reshape(width, 128, channels)


def taps(x, dilation, sign):
    rows = jnp.concatenate([shift_rows(x, sign * p * dilation) for p in (-1, 0, 1)], axis=-1)
    width = x.shape[0]
    kept = width - 2 * dilation
    cols = [rows[dilation + sign * q * dilation :][:kept] for q in (-1, 0, 1)]
    return jnp.concatenate(cols, axis=-1)


def matmul(a, b):
    return jnp.dot(a, b, preferred_element_type=jnp.float32)


def spectrum(table_hi, table_lo, field):
    def one(table):
        return jnp.einsum("fr,jrc->jfc", table, field, preferred_element_type=jnp.float32)

    return one(table_hi) + one(table_lo)


def cross(first, second):
    fc, fs = first[..., :64, :], first[..., 64:, :]
    sc, ss = second[..., :64, :], second[..., 64:, :]
    real_row = lax.broadcasted_iota(jnp.int32, (64, 1), 0) == 0
    out_c = sc * fc + jnp.where(real_row, 0.0, ss * fs)
    out_s = jnp.where(real_row, ss * fs, ss * fc - sc * fs)
    return jnp.concatenate([out_c, out_s], axis=-2)


def per_device(latent, corr_kernel, w1, b1, w2, b2, cotangent):
    bf, f4 = jnp.bfloat16, jnp.float32
    row_count, col_count, channels = latent.shape
    n_rows_dev = lax.axis_size(ROWS_AXES)
    n_cols_dev = lax.axis_size(COLS_AXES)
    up = [(i, (i + 1) % n_cols_dev) for i in range(n_cols_dev)]
    down = [(j, i) for i, j in up]
    edge_hi = jnp.concatenate([latent[:, -HALO_LAT:], cotangent[:, -HALO_COT:]], axis=1)
    edge_lo = jnp.concatenate([latent[:, :HALO_LAT], cotangent[:, :HALO_COT]], axis=1)
    left = lax.ppermute(edge_hi, COLS_AXES, up)
    right = lax.ppermute(edge_lo, COLS_AXES, down)
    pad = jnp.zeros((row_count, 2, channels), bf)
    lat_ext = jnp.concatenate([left[:, :HALO_LAT], latent, right[:, :HALO_LAT], pad], axis=1)
    cot_ext = jnp.concatenate([left[:, HALO_LAT:], cotangent, right[:, HALO_LAT:]], axis=1)
    lat_blocks = lat_ext.transpose(1, 0, 2).reshape(-1, 4, row_count, channels)
    cot_blocks = cot_ext.transpose(1, 0, 2).reshape(-1, 4, row_count, channels)
    n = n_rows_dev
    send = jnp.concatenate(
        [lat_blocks[0:n], lat_blocks[1 : n + 1], lat_blocks[2 : n + 2], lat_blocks[3 : n + 3, :2],
         cot_blocks[0:n], cot_blocks[1 : n + 1]],
        axis=1,
    )
    got = lax.all_to_all(send, ROWS_AXES, 0, 0, tiled=True)
    cells = got.transpose(1, 2, 0, 3).reshape(22, N_ROWS, channels)
    lat, cot = cells[:14], cells[14:].astype(f4)

    place = np.arange(N_ROWS)
    order = 4 * (place % 32) + place // 32
    t_hi, t_lo = split_two(real_transform(order))
    n_hi, n_lo = split_two(real_transform(place))
    weight = np.full((N_ROWS, 1), 2.0 / N_ROWS)
    weight[0] = weight[64] = 1.0 / N_ROWS
    inv_perm = jnp.asarray((real_transform(order) * weight).T, f4)
    inv_nat = jnp.asarray((real_transform(place) * weight).T, f4)

    lat_spec = spectrum(t_hi, t_lo, lat)
    ker_spec = spectrum(n_hi, n_lo, corr_kernel[None])[0]
    prod = cross(ker_spec[None], lat_spec)
    correlated = jnp.einsum("rf,jfc->jrc", inv_perm, prod, precision=lax.Precision.HIGHEST, preferred_element_type=f4)
    mixed = (lat.astype(f4) + correlated).astype(bf)

    w1_flat = w1.transpose(1, 0, 2, 3).reshape(9 * channels, channels)
    w2_flat = w2.transpose(1, 0, 2, 3).reshape(9 * channels, channels)
    w1_back = w1.transpose(1, 0, 3, 2).reshape(9 * channels, channels)
    w2_back = w2.transpose(1, 0, 3, 2).reshape(9 * channels, channels)

    mixed_taps = taps(mixed, 1, 1)
    pre1 = matmul(mixed_taps, w1_flat) + b1
    hidden = (mixed[1:13].astype(f4) + jax.nn.silu(pre1)).astype(bf)
    hidden_taps = taps(hidden, 2, 1)
    pre2 = matmul(hidden_taps, w2_flat) + b2
    prediction = (hidden[4:8].astype(f4) + jax.nn.silu(pre2[2:6])).astype(bf)
    pred_send = prediction.reshape(OWN, 4, n, channels).transpose(2, 0, 1, 3)
    pred_got = lax.all_to_all(pred_send, ROWS_AXES, 0, 0, tiled=True)
    pred_out = pred_got.transpose(2, 0, 1, 3).reshape(row_count, col_count, channels)

    slope2 = (cot * silu_slope(pre2)).astype(bf)
    own2 = slope2[2:6].reshape(-1, channels)
    dot_t = lambda a, b: lax.dot_general(a, b, (((0,), (0,)), ((), ())), preferred_element_type=f4)
    dw2 = dot_t(hidden_taps[2:6].reshape(-1, 9 * channels), own2)
    db2 = jnp.sum(own2.astype(f4), axis=0)
    grad_hidden = cot[2:6] + matmul(taps(slope2, 2, -1), w2_back)
    slope1 = (grad_hidden * silu_slope(pre1[4:8])).astype(bf)
    own1 = slope1.reshape(-1, channels)
    dw1 = dot_t(mixed_taps[4:8].reshape(-1, 9 * channels), own1)
    db1 = jnp.sum(own1.astype(f4), axis=0)
    spread = matmul(taps(jnp.pad(slope1, ((2, 2), (0, 0), (0, 0))), 1, -1), w1_back)
    grad_mixed = (spread + jnp.pad(grad_hidden, ((1, 1), (0, 0), (0, 0)))).astype(bf)
    grad_spec = spectrum(t_hi, t_lo, grad_mixed)
    both = jnp.sum(cross(grad_spec, lat_spec[4:10]), axis=0)
    dk = jnp.dot(inv_nat, both, precision=lax.Precision.HIGHEST, preferred_element_type=f4)

    biases = jnp.stack([db1, db2])
    high = biases.astype(bf)
    low = (biases - high.astype(f4)).astype(bf)
    grads = jnp.concatenate(
        [dw1.astype(bf), dw2.astype(bf), dk.astype(bf), high, low, jnp.zeros((GRAD_ROWS - 2436, channels), bf)]
    )
    n_plane, n_depth = lax.axis_size(PLANE_AXES), lax.axis_size(DEPTH_AXES)
    share = GRAD_ROWS // n_plane
    part = lax.all_to_all(grads.reshape(n_plane, share, channels), PLANE_AXES, 0, 0, tiled=True)
    part = jnp.sum(part.astype(f4), axis=0).astype(bf)
    part = lax.all_to_all(jnp.broadcast_to(part, (n_depth, share, channels)), DEPTH_AXES, 0, 0, tiled=True)
    part = jnp.sum(part.astype(f4), axis=0).astype(bf)
    whole = lax.all_to_all(jnp.broadcast_to(part, (n_plane, share, channels)), PLANE_AXES, 0, 0, tiled=True)
    whole = whole.reshape(GRAD_ROWS, channels).astype(f4)
    dw1, dw2 = (whole[a : a + 1152].reshape(3, 3, channels, channels).transpose(1, 0, 2, 3) for a in (0, 1152))
    return pred_out, dw1, whole[2432] + whole[2434], dw2, whole[2433] + whole[2435], whole[2304:2432]


def solution(mesh):
    axes = ROWS_AXES + COLS_AXES
    split = Mesh(mesh.devices.reshape(4, 8, 4, 2, 2), axes)
    grid = P(ROWS_AXES, COLS_AXES, None)
    return jax.shard_map(
        per_device, mesh=split, in_specs=(grid, P(), P(), P(), P(), P(), grid),
        out_specs=(grid, P(), P(), P(), P(), P()), check_vma=False,
    )
```

time: 715 us -> 185 us (0.26)
  waiting for transfers between devices: 406 us -> 78.4 us
  blocking collectives: 129 us -> 21 us
  starting transfers between devices: 138 us -> 55.5 us
  between operations: 14.8 us -> 1.34 us
    psum x1 -> x0, waiting for transfers between devices: 358 us -> none  [per_device(): lax.psum((second_weight_matrix, bias_two, first_weight_matrix, bias_one,...]
    psum x1 -> x0, blocking collectives: 111 us -> none  [per_device(): lax.psum((second_weight_matrix, bias_two, first_weight_matrix, bias_one,...]
    ppermute x16 -> x2, starting transfers between devices: 109 us -> 18.8 us  [the longest x1 9.97 us: per_device(): left = lax.ppermute(edge_hi, COLS_AXES, up)]
    all_to_all x2 -> x4, waiting for transfers between devices: 19.8 us -> 75.9 us  [the longest x1 34.3 us: per_device(): got = lax.all_to_all(send, ROWS_AXES, 0, 0, tiled=True)]
    ppermute x16 -> x2, waiting for transfers between devices: 28.8 us -> 2.58 us  [the longest x1 2.58 us: per_device(): left = lax.ppermute(edge_hi, COLS_AXES, up)]
    all_to_all x2 -> x4, starting transfers between devices: 28.5 us -> 36.8 us  [the longest x1 10 us: per_device(): lax.all_to_all(jnp.broadcast_to(part, (n_depth, share, channels)), DEPTH_...]
  transfers between devices with their start and end apart: 19 -> 6, of which waited for: 11 -> 5; matrix products, arithmetic and copies ran while one was open for 1% -> 1% of each run, Pallas kernels for 0% -> 0%
where the time goes in v1:
time: 185 us
  waiting for transfers between devices  78.4 us (42%)
  starting transfers between devices  55.5 us (30%)
  blocking collectives  21 us (11%)
  local copies, waits for them, and re-layouts  18 us (10%)
  matrix products  6.61 us (4%)
  other arithmetic  3.62 us (2%)
    all_to_all x1, waiting for transfers between devices, per_device(): got = lax.all_to_all(send, ROWS_AXES, 0, 0, tiled=True)  34.3 us
    all_to_all x1, blocking collectives, per_device(): lax.all_to_all(grads.reshape(n_plane, share, channels), PLANE_AXES, 0, 0,...  21 us
    all_to_all x1, waiting for transfers between devices, per_device(): lax.all_to_all(jnp.broadcast_to(part, (n_depth, share, channels)), DEPTH_...  17.5 us
    all_to_all x1, waiting for transfers between devices, per_device(): lax.all_to_all(jnp.broadcast_to(part, (n_plane, share, channels)), PLANE_...  12.3 us
    all_to_all x1, waiting for transfers between devices, per_device(): pred_got = lax.all_to_all(pred_send, ROWS_AXES, 0, 0, tiled=True)  11.7 us
    all_to_all x1, starting transfers between devices, per_device(): lax.all_to_all(jnp.broadcast_to(part, (n_depth, share, channels)), DEPTH_...  10 us
    ppermute x1, starting transfers between devices, per_device(): left = lax.ppermute(edge_hi, COLS_AXES, up)  9.97 us
    all_to_all x1, starting transfers between devices, per_device(): pred_got = lax.all_to_all(pred_send, ROWS_AXES, 0, 0, tiled=True)  9.91 us
  transfers between devices with their start and end apart: 6, of which 5 were waited for; matrix products, arithmetic and copies ran while one was open for 1% of the time, Pallas kernels for 0%

profile of v1, /device:TPU:1, one launch (start us, length us, event | category | flops | bytes accessed | tf_op | source)
XLA Modules:
  0.0 184.6 jit_solution(13417890547104468097)
XLA Ops:
  0.7 0.8 fusion.66
  1.4 0.7 fusion.65
  2.2 8.8 %collective-permute-start.1 = (bf16[4,7,128]{2,1,0:T(8,128)(2,1)S(1)}, bf16[4,7,128]{2,1,0:T(8,128)(2,1)S(1)}, u32[]{:S(2)}, u32[]{:S(2)}) collective-permute-start(bf16[4,7,128]{2,1,0:T(8,128)(2,1)S(1)} %pad_maximum_fusion.17), channel_id=1, source_target_pairs={{1,0},{2,1},{3,2},{4,3},{5,4},{6,5},{7,6},{8,7},{9,8},{10,9},{11,1... | collective-permute-start | bytes 21512 | tf_op jit(solution)/shard_map/ppermute | solution.py:87
  11.0 10.0 %collective-permute-start = (bf16[4,7,128]{2,1,0:T(8,128)(2,1)S(1)}, bf16[4,7,128]{2,1,0:T(8,128)(2,1)S(1)}, u32[]{:S(2)}, u32[]{:S(2)}) collective-permute-start(bf16[4,7,128]{2,1,0:T(8,128)(2,1)S(1)} %pad_maximum_fusion.16), channel_id=1, source_target_pairs={{0,1},{1,2},{2,3},{3,4},{4,5},{5,6},{6,7},{7,8},{8,9},{9,10},{10,1... | collective-permute-start | bytes 21512 | tf_op jit(solution)/shard_map/ppermute | solution.py:86
  21.0 2.6 %collective-permute-done = bf16[4,7,128]{2,1,0:T(8,128)(2,1)S(1)} collective-permute-done((bf16[4,7,128]{2,1,0:T(8,128)(2,1)S(1)}, bf16[4,7,128]{2,1,0:T(8,128)(2,1)S(1)}, u32[]{:S(2)}, u32[]{:S(2)}) %collective-permute-start) | collective-permute-done | bytes 7200 | tf_op jit(solution)/shard_map/ppermute | solution.py:86
  23.6 1.0 maximum_bitcast_fusion
  24.9 0.7 constant_dynamic-update-slice_fusion.4
  26.2 0.7 constant_dynamic-update-slice_fusion.3
  26.9 0.7 constant_dynamic-update-slice_fusion.2
  27.6 0.7 slice_dynamic-update-slice_fusion
  28.3 0.7 constant_dynamic-update-slice_fusion.1
  29.0 0.7 constant_dynamic-update-slice_fusion
  29.7 9.9 %all-to-all-start = ((bf16[32,22,4,128]{3,2,1,0:T(4,128)(2,1)}), bf16[32,22,4,128]{3,2,1,0:T(4,128)(2,1)S(1)}, u32[]{:S(2)}, u32[]{:S(2)}) async-start(bf16[32,22,4,128]{3,2,1,0:T(4,128)(2,1)} %constant_dynamic-update-slice_fusion), calls=%async_computation | async-start | bytes 1441792 | tf_op jit(solution)/shard_map/all_to_all | solution.py:99
  40.7 34.3 %all-to-all-done = bf16[32,22,4,128]{3,2,1,0:T(4,128)(2,1)S(1)} async-done(((bf16[32,22,4,128]{3,2,1,0:T(4,128)(2,1)}), bf16[32,22,4,128]{3,2,1,0:T(4,128)(2,1)S(1)}, u32[]{:S(2)}, u32[]{:S(2)}) %all-to-all-start) | async-done | bytes 720928 | tf_op jit(solution)/shard_map/all_to_all | solution.py:99
  75.3 0.3 fusion.68
  75.6 0.4 copy-done.5
  75.9 0.3 fusion.10
  76.2 0.2 select_add_fusion
  76.5 0.6 copy-done.8
  77.1 0.9 fusion.12
  78.7 0.6 fusion.46
  79.3 1.2 add_convert_fusion
  80.6 0.3 copy.78
  81.3 0.4 fusion.48
  81.7 0.3 copy-done.12
  81.9 0.9 fusion.34
  83.0 0.5 fusion.1
  83.5 0.4 slice-done
  84.4 0.5 convert_reduce_fusion.1
  84.9 0.5 fusion
  86.1 0.6 fusion.23
  87.3 0.5 copy-done.7
  88.0 0.6 concatenate.135
  88.5 21.0 %all_to_all.25 = bf16[32,80,128]{2,1,0:T(8,128)(2,1)S(1)} all-to-all(bf16[32,80,128]{2,1,0:T(8,128)(2,1)S(1)} %bitcast.146), channel_id=1, replica_groups=mesh['y'=4,'zl'=8,'x'=4,'zh'=2,'c'=2] {'y','x','c'}, dimensions={0} | all-to-all | bytes 1310720 | tf_op jit(solution)/shard_map/all_to_all | solution.py:157
  109.7 0.8 broadcast_in_dim.61
  110.5 10.0 %all-to-all-start.3 = ((bf16[16,80,128]{2,1,0:T(8,128)(2,1)}), bf16[16,80,128]{2,1,0:T(8,128)(2,1)S(1)}, u32[]{:S(2)}, u32[]{:S(2)}) async-start(bf16[16,80,128]{2,1,0:T(8,128)(2,1)} %broadcast_in_dim.61), calls=%async_computation.3 | async-start | bytes 655360 | tf_op jit(solution)/shard_map/all_to_all | solution.py:159
  120.5 0.7 copy.93
  121.3 17.5 %all-to-all-done.3 = bf16[16,80,128]{2,1,0:T(8,128)(2,1)S(1)} async-done(((bf16[16,80,128]{2,1,0:T(8,128)(2,1)}), bf16[16,80,128]{2,1,0:T(8,128)(2,1)S(1)}, u32[]{:S(2)}, u32[]{:S(2)}) %all-to-all-start.3) | async-done | bytes 327712 | tf_op jit(solution)/shard_map/all_to_all | solution.py:159
  138.8 9.9 %all-to-all-start.1 = ((bf16[32,4,4,128]{3,2,1,0:T(4,128)(2,1)}), bf16[32,4,4,128]{3,2,1,0:T(4,128)(2,1)S(1)}, u32[]{:S(2)}, u32[]{:S(2)}) async-start(bf16[32,4,4,128]{3,2,1,0:T(4,128)(2,1)} %bitcast.126), calls=%async_computation.1 | async-start | bytes 262144 | tf_op jit(solution)/shard_map/all_to_all | solution.py:130
  148.8 11.7 %all-to-all-done.1 = bf16[32,4,4,128]{3,2,1,0:T(4,128)(2,1)S(1)} async-done(((bf16[32,4,4,128]{3,2,1,0:T(4,128)(2,1)}), bf16[32,4,4,128]{3,2,1,0:T(4,128)(2,1)S(1)}, u32[]{:S(2)}, u32[]{:S(2)}) %all-to-all-start.1) | async-done | bytes 131104 | tf_op jit(solution)/shard_map/all_to_all | solution.py:130
  160.5 0.9 broadcast_in_dim.62
  161.4 7.0 %all-to-all-start.4 = ((bf16[32,80,128]{2,1,0:T(8,128)(2,1)}), bf16[32,80,128]{2,1,0:T(8,128)(2,1)S(1)}, u32[]{:S(2)}, u32[]{:S(2)}) async-start(bf16[32,80,128]{2,1,0:T(8,128)(2,1)} %broadcast_in_dim.62), calls=%async_computation.4 | async-start | bytes 1310720 | tf_op jit(solution)/shard_map/all_to_all | solution.py:161
  168.5 0.7 copy.85
  169.1 12.3 %all-to-all-done.4 = bf16[32,80,128]{2,1,0:T(8,128)(2,1)S(1)} async-done(((bf16[32,80,128]{2,1,0:T(8,128)(2,1)}), bf16[32,80,128]{2,1,0:T(8,128)(2,1)S(1)}, u32[]{:S(2)}, u32[]{:S(2)}) %all-to-all-start.4) | async-done | bytes 655392 | tf_op jit(solution)/shard_map/all_to_all | solution.py:161
  181.7 0.5 fusion.36
  182.2 0.6 slice.448
  182.9 0.9 copy.92
  183.7 0.9 copy.91
  (91 shorter events, 5.5 us)
Async XLA Ops:
  0.6 39.5 %copy-start = (bf16[128,128]{1,0:T(8,128)(2,1)S(1)}, bf16[128,128]{1,0:T(8,128)(2,1)}, u32[]{:S(2)}) copy-start(bf16[128,128]{1,0:T(8,128)(2,1)} %param.16) | copy-start | bytes 98308
  0.6 25.2 %copy-start.4 = (bf16[4,128,128]{2,1,0:T(8,128)(2,1)S(1)}, bf16[4,128,128]{2,1,0:T(8,128)(2,1)}, u32[]{:S(2)}) copy-start(bf16[4,128,128]{2,1,0:T(8,128)(2,1)} %param.21) | copy-start | bytes 393220
  2.2 18.9 %collective-permute-start.1 = (bf16[4,7,128]{2,1,0:T(8,128)(2,1)S(1)}, bf16[4,7,128]{2,1,0:T(8,128)(2,1)S(1)}, u32[]{:S(2)}, u32[]{:S(2)}) collective-permute-start(bf16[4,7,128]{2,1,0:T(8,128)(2,1)S(1)} %pad_maximum_fusion.17), channel_id=1, source_target_pairs={{1,0},{2,1},{3,2},{4,3},{5,4},{6,5},{7,6},{8,7},{9,8},{10,9},{11,1... | collective-permute-start | bytes 21512 | tf_op jit(solution)/shard_map/ppermute | solution.py:87
  11.0 12.6 %collective-permute-start = (bf16[4,7,128]{2,1,0:T(8,128)(2,1)S(1)}, bf16[4,7,128]{2,1,0:T(8,128)(2,1)S(1)}, u32[]{:S(2)}, u32[]{:S(2)}) collective-permute-start(bf16[4,7,128]{2,1,0:T(8,128)(2,1)S(1)} %pad_maximum_fusion.16), channel_id=1, source_target_pairs={{0,1},{1,2},{2,3},{3,4},{4,5},{5,6},{6,7},{7,8},{8,9},{9,10},{10,1... | collective-permute-start | bytes 21512 | tf_op jit(solution)/shard_map/ppermute | solution.py:86
  26.2 13.4 %copy-start.2 = (bf16[3,3,128,128]{3,2,1,0:T(8,128)(2,1)S(1)}, bf16[3,3,128,128]{3,2,1,0:T(8,128)(2,1)}, u32[]{:S(2)}) copy-start(bf16[3,3,128,128]{3,2,1,0:T(8,128)(2,1)} %param.19) | copy-start | bytes 884740
  29.7 10.1 %copy-start.3 = (bf16[3,3,128,128]{3,2,1,0:T(8,128)(2,1)S(1)}, bf16[3,3,128,128]{3,2,1,0:T(8,128)(2,1)}, u32[]{:S(2)}) copy-start(bf16[3,3,128,128]{3,2,1,0:T(8,128)(2,1)} %param.17) | copy-start | bytes 884740
  29.7 45.2 %all-to-all-start = ((bf16[32,22,4,128]{3,2,1,0:T(4,128)(2,1)}), bf16[32,22,4,128]{3,2,1,0:T(4,128)(2,1)S(1)}, u32[]{:S(2)}, u32[]{:S(2)}) async-start(bf16[32,22,4,128]{3,2,1,0:T(4,128)(2,1)} %constant_dynamic-update-slice_fusion), calls=%async_computation | async-start | bytes 1441792 | tf_op jit(solution)/shard_map/all_to_all | solution.py:99
  39.6 0.8 copy-start.10
  39.6 0.9 copy-start.9
  40.6 34.6 %copy-start.6 = (bf16[128,128,1]{1,0,2:T(8,128)(2,1)S(1)}, bf16[128,128,1]{1,0,2:T(8,128)(2,1)}, u32[]{:S(2)}) copy-start(bf16[128,128,1]{1,0,2:T(8,128)(2,1)} %constant.43) | copy-start | bytes 98308
  75.0 6.0 %copy-start.1 = (f32[8,4,32,128]{3,1,0,2:T(4,128)}, f32[8,4,32,128]{3,1,0,2:T(4,128)S(1)}, u32[]{:S(2)}) copy-start(f32[8,4,32,128]{3,1,0,2:T(4,128)S(1)} %slice_convert_fusion) | copy-start | bytes 1572868
  75.2 0.8 copy-start.5
  76.2 0.8 copy-start.8
  78.6 0.7 copy-start.11
  81.3 0.7 copy-start.12
  82.9 1.0 slice-start
  86.9 0.8 copy-start.7
  110.5 28.3 %all-to-all-start.3 = ((bf16[16,80,128]{2,1,0:T(8,128)(2,1)}), bf16[16,80,128]{2,1,0:T(8,128)(2,1)S(1)}, u32[]{:S(2)}, u32[]{:S(2)}) async-start(bf16[16,80,128]{2,1,0:T(8,128)(2,1)} %broadcast_in_dim.61), calls=%async_computation.3 | async-start | bytes 655360 | tf_op jit(solution)/shard_map/all_to_all | solution.py:159
  138.8 21.7 %all-to-all-start.1 = ((bf16[32,4,4,128]{3,2,1,0:T(4,128)(2,1)}), bf16[32,4,4,128]{3,2,1,0:T(4,128)(2,1)S(1)}, u32[]{:S(2)}, u32[]{:S(2)}) async-start(bf16[32,4,4,128]{3,2,1,0:T(4,128)(2,1)} %bitcast.126), calls=%async_computation.1 | async-start | bytes 262144 | tf_op jit(solution)/shard_map/all_to_all | solution.py:130
  161.4 20.1 %all-to-all-start.4 = ((bf16[32,80,128]{2,1,0:T(8,128)(2,1)}), bf16[32,80,128]{2,1,0:T(8,128)(2,1)S(1)}, u32[]{:S(2)}, u32[]{:S(2)}) async-start(bf16[32,80,128]{2,1,0:T(8,128)(2,1)} %broadcast_in_dim.62), calls=%async_computation.4 | async-start | bytes 1310720 | tf_op jit(solution)/shard_map/all_to_all | solution.py:161

commit v2 on v1

v2 whole, which is shorter than its diff:
```python
import jax
import jax.numpy as jnp
import numpy as np
from jax import lax
from jax.experimental import pallas as pl
from jax.experimental.pallas import tpu as pltpu
from jax.sharding import Mesh, PartitionSpec as P

ROWS_AXES = ("y", "zl")
COLS_AXES = ("x", "zh", "c")
PLANE_AXES = ("y", "x", "c")
DEPTH_AXES = ("zl", "zh")
SIZES = {"y": 4, "zl": 8, "x": 4, "zh": 2, "c": 2}
N_ROWS = 128
CH = 128
PEERS = 32
GRAD_ROWS = 2560
BF, F4 = jnp.bfloat16, jnp.float32
VMEM = pl.BlockSpec(memory_space=pltpu.VMEM)


def real_transform(order):
    freq = np.arange(64)
    angle = 2.0 * np.pi * ((freq[:, None] * order[None, :]) % N_ROWS) / N_ROWS
    sines = np.sin(angle)
    sines[0] = np.cos(np.pi * order)
    return np.concatenate([np.cos(angle), sines])


def split_two(table):
    high = table.astype(jnp.bfloat16)
    low = (table - high.astype(np.float64)).astype(jnp.bfloat16)
    return high, low


def tables():
    place = np.arange(N_ROWS)
    order = 4 * (place % 32) + place // 32
    weight = np.full((N_ROWS, 1), 2.0 / N_ROWS)
    weight[0] = weight[64] = 1.0 / N_ROWS
    made = []
    for rows in (order, place):
        made.append(np.concatenate(split_two(real_transform(rows)), axis=1))
        high, low = split_two((real_transform(rows) * weight).T)
        made.append(np.concatenate([high, high, low], axis=1))
    return made


def window_of(y, zl, flip):
    snake = zl * 4 + jnp.where(zl % 2 == 0, y, 3 - y)
    return jnp.where(flip, 31 - snake, snake)


def flipped(zh, c):
    return zh == c


def device_ring():
    ring = []
    for x in range(4):
        for zh in range(2):
            for c in range(2):
                block = [0] * 32
                for y in range(4):
                    for zl in range(8):
                        snake = zl * 4 + (y if zl % 2 == 0 else 3 - y)
                        block[31 - snake if flipped(zh, c) else snake] = (((y * 8 + zl) * 4 + x) * 2 + zh) * 2 + c
                ring += block
    return ring


def dot(a, b):
    return jnp.dot(a, b, preferred_element_type=F4)


def dot_t(a, b):
    return lax.dot_general(a, b, (((0,), (0,)), ((), ())), preferred_element_type=F4)


def turned(x, step):
    blocks = [x[32 * i : 32 * i + 32] for i in range(4)]
    if step > 0:
        moved = [pltpu.roll(b, 31, axis=0) for b in blocks[:step]]
        return jnp.concatenate(blocks[step:] + moved, axis=0)
    if step < 0:
        moved = [pltpu.roll(b, 1, axis=0) for b in blocks[step:]]
        return jnp.concatenate(moved + blocks[:step], axis=0)
    return x


def put_turned(ref, col, x, steps):
    for i, step in enumerate(steps):
        ref[col, :, i * CH : (i + 1) * CH] = turned(x, step).astype(BF)


def cross(first, second):
    fc, fs = first[:64], first[64:]
    sc, ss = second[:64], second[64:]
    real_row = lax.broadcasted_iota(jnp.int32, sc.shape, 0) == 0
    out_c = sc * fc + jnp.where(real_row, 0.0, ss * fs)
    out_s = jnp.where(real_row, ss * fs, ss * fc - sc * fs)
    return jnp.concatenate([out_c, out_s], axis=0)


def three_parts(x):
    high = x.astype(BF)
    low = (x - high.astype(F4)).astype(BF)
    return jnp.concatenate([high, low, high], axis=0)


def send_kernel(lat, cot, out, wide, packed):
    y, zl, zh, c = (lax.axis_index(a) for a in ("y", "zl", "zh", "c"))
    flip = flipped(zh, c)
    for t, ref in enumerate((lat, cot)):
        wide[t * 512 : t * 512 + 512, :] = ref[...].reshape(512, CH).astype(F4)
    for k in range(PEERS):
        start = pl.multiple_of(4 * window_of(k // 8, jnp.int32(k % 8), flip), 4)
        for t in range(2):
            for rr in range(4):
                piece = wide[pl.ds(t * 512 + rr * 128 + start, 4), :]
                packed[pl.ds(k * 32 + t * 16 + rr, 4, stride=4), :] = piece
    out[...] = packed[...].astype(BF).reshape(PEERS, 32, CH)


def column(ref, start, stride):
    return jnp.concatenate([ref[pl.ds(start + rr, 32, stride=stride), :] for rr in range(4)], axis=0)


def forward_kernel(far_left, left, own, right, far_right, ker, w1, b1, w2, b2, fwd, inv, fwd_nat,
                   pred, spec, m3, h3, rise1, slope2, cot_own,
                   gl, go, gr, gl2, gr2, latf, xw, parts, cots, hid, placed):
    for ref, wide in ((left, gl), (own, go), (right, gr), (far_left, gl2), (far_right, gr2)):
        wide[...] = ref[...].reshape(wide.shape).astype(F4)
    lat_from = ([(gl2, 4, 8)] + [(gl, 4 * j, 32) for j in range(4)] + [(go, 4 * j, 32) for j in range(4)]
                + [(gr, 4 * j, 32) for j in range(4)] + [(gr2, 0, 8)])
    for j, (ref, start, stride) in enumerate(lat_from):
        x = column(ref, start, stride)
        latf[j] = x
        xb = x.astype(BF)
        xw[0:128, j * CH : (j + 1) * CH] = xb
        xw[128:256, j * CH : (j + 1) * CH] = xb
    cot_from = [(gl, 24), (gl, 28)] + [(go, 16 + 4 * j) for j in range(4)] + [(gr, 16), (gr, 20)]
    for u, (ref, start) in enumerate(cot_from):
        cots[u] = column(ref, start, 32)
    cot_own[...] = cots[2:6]
    ker_two = jnp.concatenate([ker[...], ker[...]], axis=0)
    ker_spec = dot(fwd_nat[...], ker_two)
    for j in range(0, 14, 2):
        lanes = slice(j * CH, (j + 2) * CH)
        s = dot(fwd[...], xw[:, lanes])
        if 4 <= j < 10:
            spec[:, (j - 4) * CH : (j - 2) * CH] = s
        for i in range(2):
            part = s[:, i * CH : (i + 1) * CH]
            parts[:, i * CH : (i + 1) * CH] = three_parts(cross(ker_spec, part))
        corr = dot(inv[...], parts[...])
        for i in range(2):
            mixed = (latf[j + i] + corr[:, i * CH : (i + 1) * CH]).astype(BF).astype(F4)
            latf[j + i] = mixed
            put_turned(m3, j + i, mixed, (-1, 0, 1))
    for j in range(0, 12, 4):
        v = b1[...]
        for q in range(3):
            v = v + dot(m3[j + q : j + q + 4].reshape(512, 384), w1[q])
        g = jax.nn.sigmoid(v)
        if j == 4:
            rise1[...] = (g * (1.0 + v * (1.0 - g))).reshape(4, N_ROWS, CH)
        vg = v * g
        for i in range(4):
            h = (latf[j + i + 1] + vg[i * 128 : i * 128 + 128]).astype(BF).astype(F4)
            hid[j + i] = h
            put_turned(h3, j + i, h, (-2, 0, 2))
    for j in range(0, 8, 4):
        v = b2[...]
        for q in range(3):
            v = v + dot(h3[j + 2 * q : j + 2 * q + 4].reshape(512, 384), w2[q])
        g = jax.nn.sigmoid(v)
        vg = v * g
        rise = g * (1.0 + v * (1.0 - g))
        for i in range(4):
            u = j + i
            slope2[u] = (cots[u] * rise[i * 128 : i * 128 + 128]).astype(BF)
            if 2 <= u < 6:
                p = hid[u + 2] + vg[i * 128 : i * 128 + 128]
                for rr in range(4):
                    placed[pl.ds((u - 2) * 4 + rr, 32, stride=16), :] = p[rr * 32 : rr * 32 + 32]
    pred[...] = placed[...].astype(BF).reshape(PEERS, 16, CH)


def backward_kernel(spec, m3, h3, rise1, slope2, cot_own, w1b, w2b, fwd, inv_nat, out, s3, z3, gm):
    own2 = slope2[2:6].reshape(512, CH)
    for q in range(3):
        d = dot_t(h3[2 + 2 * q : 6 + 2 * q].reshape(512, 384), own2)
        for p in range(3):
            out[1152 + (p * 3 + q) * 128 : 1280 + (p * 3 + q) * 128, :] = d[p * 128 : p * 128 + 128].astype(BF)
    for u in range(8):
        put_turned(s3, u, slope2[u].astype(F4), (2, 0, -2))
    gh = cot_own[...].reshape(512, CH)
    for q in range(3):
        gh = gh + dot(s3[4 - 2 * q : 8 - 2 * q].reshape(512, 384), w2b[q])
    slope1 = (gh * rise1[...].reshape(512, CH)).astype(BF)
    slope1_wide = slope1.astype(F4)
    for i in range(4):
        put_turned(z3, i, slope1_wide[i * 128 : i * 128 + 128], (1, 0, -1))
    gm[0] = jnp.zeros((N_ROWS, CH), F4)
    gm[5] = jnp.zeros((N_ROWS, CH), F4)
    gm[1:5] = gh.reshape(4, N_ROWS, CH)
    for q in range(3):
        gm[q : q + 4] += dot(z3[...].reshape(512, 384), w1b[q]).reshape(4, N_ROWS, CH)
    for q in range(3):
        d = dot_t(m3[4 + q : 8 + q].reshape(512, 384), slope1)
        for p in range(3):
            out[(p * 3 + q) * 128 : (p * 3 + q) * 128 + 128, :] = d[p * 128 : p * 128 + 128].astype(BF)
    both = jnp.zeros((N_ROWS, CH), F4)
    for j in range(0, 6, 2):
        two = jnp.concatenate([gm[j], gm[j + 1]], axis=1).astype(BF)
        s = dot(fwd[...], jnp.concatenate([two, two], axis=0))
        for i in range(2):
            both = both + cross(s[:, i * CH : (i + 1) * CH], spec[:, (j + i) * CH : (j + i + 1) * CH])
    dk = dot(inv_nat[...], three_parts(both))
    out[2304:2432, :] = dk.astype(BF)
    db1 = jnp.sum(slope1_wide, axis=0, keepdims=True)
    db2 = jnp.sum(own2.astype(F4), axis=0, keepdims=True)
    rows = []
    for b in (db1, db2):
        high = b.astype(BF).astype(F4)
        rows += [high, b - high]
    tail = jnp.concatenate(rows + [jnp.zeros((GRAD_ROWS - 2436, CH), F4)], axis=0)
    out[2432:GRAD_ROWS, :] = tail.astype(BF)


def call(kernel, outs, scratch, flops, *args):
    return pl.pallas_call(
        kernel,
        out_shape=[jax.ShapeDtypeStruct(s, d) for s, d in outs],
        in_specs=[VMEM] * len(args),
        out_specs=[VMEM] * len(outs),
        scratch_shapes=[pltpu.VMEM(s, d) for s, d in scratch],
        compiler_params=pltpu.CompilerParams(vmem_limit_bytes=40 << 20),
        cost_estimate=pl.CostEstimate(flops=flops, bytes_accessed=4 << 20, transcendentals=0),
    )(*args)


def forward(far_left, left, own, right, far_right, ker, w1, b1, w2, b2):
    fwd, inv, fwd_nat, _ = (jnp.asarray(t, BF) for t in tables())
    w1q = w1.transpose(1, 0, 2, 3).reshape(3, 384, CH)
    w2q = w2.transpose(1, 0, 2, 3).reshape(3, 384, CH)
    outs = [((PEERS, 16, CH), BF), ((128, 6 * CH), F4), ((14, 128, 384), BF), ((12, 128, 384), BF),
            ((4, 128, CH), F4), ((8, 128, CH), BF), ((4, 128, CH), F4)]
    scratch = [((1024, CH), F4)] * 3 + [((256, CH), F4)] * 2 + [
        ((14, 128, CH), F4), ((256, 14 * CH), BF), ((384, 2 * CH), BF), ((8, 128, CH), F4), ((12, 128, CH), F4),
        ((512, CH), F4)]
    return call(forward_kernel, outs, scratch, 1 << 30, far_left, left, own, right, far_right, ker,
                w1q, b1.reshape(1, CH), w2q, b2.reshape(1, CH), fwd, inv, fwd_nat)


def backward(w1, w2, spec, m3, h3, rise1, slope2, cot_own):
    fwd, _, _, inv_nat = (jnp.asarray(t, BF) for t in tables())
    w1b = w1.transpose(1, 0, 3, 2).reshape(3, 384, CH)
    w2b = w2.transpose(1, 0, 3, 2).reshape(3, 384, CH)
    outs = [((GRAD_ROWS, CH), BF)]
    scratch = [((8, 128, 384), BF), ((4, 128, 384), BF), ((6, 128, CH), F4)]
    return call(backward_kernel, outs, scratch, 1 << 31, spec, m3, h3, rise1, slope2, cot_own, w1b, w2b, fwd, inv_nat)[0]


def per_device(latent, corr_kernel, w1, b1, w2, b2, cotangent):
    row_count, col_count, _ = latent.shape
    flip = flipped(lax.axis_index("zh"), lax.axis_index("c"))
    (send,) = call(send_kernel, [((PEERS, 32, CH), BF)], [((1024, CH), F4), ((1024, CH), F4)], 1 << 20, latent, cotangent)
    own = lax.all_to_all(send, ROWS_AXES, 0, 0, tiled=True)
    ring = device_ring()
    n = len(ring)
    everywhere = ROWS_AXES + COLS_AXES

    def shifted(block, by):
        return lax.ppermute(block, everywhere, [(ring[i], ring[(i + by) % n]) for i in range(n)])

    left, right = shifted(own, 1), shifted(own, -1)
    far_left, far_right = shifted(own[:, 8:16], 2), shifted(own[:, 0:8], -2)
    pred_send, *kept = forward(far_left, left, own, right, far_right, corr_kernel, w1, b1, w2, b2)
    pred_got = lax.all_to_all(pred_send, ROWS_AXES, 0, 0, tiled=True)
    grads = backward(w1, w2, *kept)
    grads, pred_got = lax.optimization_barrier((grads, pred_got))

    got = pred_got.reshape(4, 8, 4, row_count, CH)
    even, odd = got[:, 0::2], got[::-1, 1::2]
    got = jnp.stack([even, odd], axis=2).reshape(4, 8, 4, row_count, CH).transpose(1, 0, 2, 3, 4)
    got = got.reshape(PEERS, 4, row_count, CH)
    got = jnp.where(flip, got[::-1], got)
    pred_out = got.transpose(2, 0, 1, 3).reshape(row_count, col_count, CH)

    n_plane, n_depth = lax.axis_size(PLANE_AXES), lax.axis_size(DEPTH_AXES)
    share = GRAD_ROWS // n_plane
    part = lax.all_to_all(grads.reshape(n_plane, share, CH), PLANE_AXES, 0, 0, tiled=True)
    part = jnp.sum(part.astype(F4), axis=0).astype(BF)
    part = lax.all_to_all(jnp.broadcast_to(part, (n_depth, share, CH)), DEPTH_AXES, 0, 0, tiled=True)
    part = jnp.sum(part.astype(F4), axis=0).astype(BF)
    whole = lax.all_to_all(jnp.broadcast_to(part, (n_plane, share, CH)), PLANE_AXES, 0, 0, tiled=True)
    whole = whole.reshape(GRAD_ROWS, CH).astype(F4)
    dw1, dw2 = (whole[a : a + 1152].reshape(3, 3, CH, CH) for a in (0, 1152))
    return pred_out, dw1, whole[2432] + whole[2433], dw2, whole[2434] + whole[2435], whole[2304:2432]


def solution(mesh):
    split = Mesh(mesh.devices.reshape(tuple(SIZES[a] for a in ROWS_AXES + COLS_AXES)), ROWS_AXES + COLS_AXES)
    grid = P(ROWS_AXES, COLS_AXES, None)
    return jax.shard_map(
        per_device, mesh=split, in_specs=(grid, P(), P(), P(), P(), P(), grid),
        out_specs=(grid, P(), P(), P(), P(), P()), check_vma=False,
    )
```

time: 185 us -> 154 us (0.83)
  waiting for transfers between devices: 78.4 us -> 43.1 us
  blocking collectives: 21 us -> 50.7 us
  starting transfers between devices: 55.5 us -> 36.3 us
  matrix products: 6.61 us -> 0 us
  Pallas kernels: 0 us -> 6.4 us
  local copies, waits for them, and re-layouts: 18 us -> 13.4 us
  other arithmetic: 3.62 us -> 0.91 us
    all_to_all x3 -> x2, waiting for transfers between devices: 64.1 us -> 29.1 us  [the longest x1 18.3 us: per_device(): lax.all_to_all(jnp.broadcast_to(part, (n_depth, share, CH)), DEPTH_AXES,...]
    all_to_all x1 -> x2, blocking collectives: 21 us -> 50.7 us  [the longest x1 34.6 us: per_device(): own = lax.all_to_all(send, ROWS_AXES, 0, 0, tiled=True)]
    all_to_all x3 -> x2, starting transfers between devices: 26.9 us -> 13.9 us  [the longest x1 8.09 us: per_device(): lax.all_to_all(jnp.broadcast_to(part, (n_plane, share, CH)), PLANE_AXES,...]
    ppermute x2 -> x4, starting transfers between devices: 18.8 us -> 11.1 us  [shifted(): lax.ppermute(block, everywhere, [(ring[i], ring[(i + by) % n]) for i in r...]
    dot_general x14 -> x0, matrix products: 6.61 us -> none  [the longest x4 3.22 us: matmul(): return jnp.dot(a, b, preferred_element_type=jnp.float32)]
    pallas_call x0 -> x3, Pallas kernels: none -> 6.4 us  [call(): pl.pallas_call(kernel, out_shape=[jax.ShapeDtypeStruct(s, d) for s, d in...]
    slice x33 -> x2, local copies, waits for them, and re-layouts: 4.71 us -> 1.1 us  [the longest x1 1.09 us: per_device(): dw1, dw2 = (whole[a:a + 1152].reshape(3, 3, CH, CH) for a in (0, 1152))]
    reshape x3 -> x0, local copies, waits for them, and re-layouts: 2.44 us -> none  [the longest x2 1.71 us: per_device(): whole[a:a + 1152].reshape(3, 3, channels, channels).transpose(1, 0, 2, 3)]
  transfers between devices with their start and end apart: 6 -> 7, of which waited for: 5 -> 5; matrix products, arithmetic and copies ran while one was open for 1% -> 2% of each run, Pallas kernels for 0% -> 1%
where the time goes in v2:
time: 154 us; the launch traced here: 152 us
  blocking collectives  50.7 us (33%)
  waiting for transfers between devices  43.1 us (28%)
  starting transfers between devices  36.3 us (24%)
  local copies, waits for them, and re-layouts  13.4 us (9%)
  Pallas kernels  6.4 us (4%)
    all_to_all x1, blocking collectives, per_device(): own = lax.all_to_all(send, ROWS_AXES, 0, 0, tiled=True)  34.6 us
    all_to_all x1, waiting for transfers between devices, per_device(): lax.all_to_all(jnp.broadcast_to(part, (n_depth, share, CH)), DEPTH_AXES,...  18.3 us
    all_to_all x1, blocking collectives, per_device(): lax.all_to_all(grads.reshape(n_plane, share, CH), PLANE_AXES, 0, 0, tiled...  16.1 us
    all_to_all x1, starting transfers between devices, per_device(): pred_got = lax.all_to_all(pred_send, ROWS_AXES, 0, 0, tiled=True)  11.3 us
    ppermute x4, starting transfers between devices, shifted(): lax.ppermute(block, everywhere, [(ring[i], ring[(i + by) % n]) for i in r...  11.1 us
    all_to_all x1, waiting for transfers between devices, per_device(): lax.all_to_all(jnp.broadcast_to(part, (n_plane, share, CH)), PLANE_AXES,...  10.7 us
    all_to_all x1, waiting for transfers between devices, per_device(): pred_got = lax.all_to_all(pred_send, ROWS_AXES, 0, 0, tiled=True)  9.35 us
    all_to_all x1, starting transfers between devices, per_device(): lax.all_to_all(jnp.broadcast_to(part, (n_plane, share, CH)), PLANE_AXES,...  8.09 us
  transfers between devices with their start and end apart: 7, of which 5 were waited for; matrix products, arithmetic and copies ran while one was open for 2% of the time, Pallas kernels for 1%

profile of v2, /device:TPU:1, one launch (start us, length us, event | category | flops | bytes accessed | tf_op | source)
XLA Modules:
  0.0 151.8 jit_solution(2296490671226189932)
XLA Ops:
  0.6 0.9 copy-done
  1.5 0.9 copy-done.1
  2.5 0.0 copy-start.6
  2.5 0.0 copy-start.7
  2.5 0.0 copy-start.8
  2.5 0.3 shard_map.163
  2.8 34.6 %all_to_all.25.own = bf16[32,32,128]{2,1,0:T(8,128)(2,1)S(1)} all-to-all(bf16[32,32,128]{2,1,0:T(8,128)(2,1)S(1)} %shard_map.163), channel_id=1, replica_groups=mesh['y'=4,'zl'=8,'x'=4,'zh'=2,'c'=2] {'y','zl'}, dimensions={0} | all-to-all | bytes 524288 | tf_op jit(solution)/shard_map/all_to_all | solution.py:270
  37.4 1.9 %collective-permute-start.1 = (bf16[32,32,128]{2,1,0:T(8,128)(2,1)S(1)}, bf16[32,32,128]{2,1,0:T(8,128)(2,1)S(1)}, u32[]{:S(2)}, u32[]{:S(2)}) collective-permute-start(bf16[32,32,128]{2,1,0:T(8,128)(2,1)S(1)} %all_to_all.25.own), channel_id=1, source_target_pairs={{112,240},{240,368},{368,496},{496,480},{480,352},{352,224},{224,9... | collective-permute-start | bytes 786440 | tf_op jit(solution)/shard_map/ppermute | solution.py:276
  39.3 3.7 %collective-permute-start.2 = (bf16[32,32,128]{2,1,0:T(8,128)(2,1)S(1)}, bf16[32,32,128]{2,1,0:T(8,128)(2,1)S(1)}, u32[]{:S(2)}, u32[]{:S(2)}) collective-permute-start(bf16[32,32,128]{2,1,0:T(8,128)(2,1)S(1)} %all_to_all.25.own), channel_id=1, source_target_pairs={{112,15},{240,112},{368,240},{496,368},{480,496},{352,480},{224,35... | collective-permute-start | bytes 786440 | tf_op jit(solution)/shard_map/ppermute | solution.py:276
  43.0 2.4 %collective-permute-start = (bf16[32,8,128]{2,1,0:T(8,128)(2,1)S(1)}, bf16[32,8,128]{2,1,0:T(8,128)(2,1)S(1)}, u32[]{:S(2)}, u32[]{:S(2)}) collective-permute-start(bf16[32,8,128]{2,1,0:T(8,128)(2,1)S(1)} %get-tuple-element.29), channel_id=1, source_target_pairs={{112,368},{240,496},{368,480},{496,352},{480,224},{352,96},{224,80... | collective-permute-start | bytes 196616 | tf_op jit(solution)/shard_map/ppermute | solution.py:276
  45.4 3.1 %collective-permute-start.3 = (bf16[32,8,128]{2,1,0:T(8,128)(2,1)S(1)}, bf16[32,8,128]{2,1,0:T(8,128)(2,1)S(1)}, u32[]{:S(2)}, u32[]{:S(2)}) collective-permute-start(bf16[32,8,128]{2,1,0:T(8,128)(2,1)S(1)} %get-tuple-element.28), channel_id=1, source_target_pairs={{112,143},{240,15},{368,112},{496,240},{480,368},{352,496},{224,48... | collective-permute-start | bytes 196616 | tf_op jit(solution)/shard_map/ppermute | solution.py:276
  48.7 2.0 %collective-permute-done.far_left = bf16[32,8,128]{2,1,0:T(8,128)(2,1)S(1)} collective-permute-done((bf16[32,8,128]{2,1,0:T(8,128)(2,1)S(1)}, bf16[32,8,128]{2,1,0:T(8,128)(2,1)S(1)}, u32[]{:S(2)}, u32[]{:S(2)}) %collective-permute-start) | collective-permute-done | bytes 65568 | tf_op jit(solution)/shard_map/ppermute | solution.py:276
  50.7 2.7 %collective-permute-done.3.far_right = bf16[32,8,128]{2,1,0:T(8,128)(2,1)S(1)} collective-permute-done((bf16[32,8,128]{2,1,0:T(8,128)(2,1)S(1)}, bf16[32,8,128]{2,1,0:T(8,128)(2,1)S(1)}, u32[]{:S(2)}, u32[]{:S(2)}) %collective-permute-start.3) | collective-permute-done | bytes 65568 | tf_op jit(solution)/shard_map/ppermute | solution.py:276
  53.3 0.0 collective-permute-done.1.left
  53.3 0.0 collective-permute-done.2.right
  53.3 0.0 copy-done.2
  53.4 4.4 %shard_map.164 = (bf16[32,16,128]{2,1,0:T(8,128)(2,1)}, f32[128,768]{1,0:T(8,128)S(1)}, bf16[14,128,384]{2,1,0:T(8,128)(2,1)S(1)}, bf16[12,128,384]{2,1,0:T(8,12...) custom-call(bf16[32,8,128]{2,1,0:T(8,128)(2,1)S(1)} %collective-permute-done.f, ...), custom_call_target="tpu_custom_call" | custom-call | flops 1073741824 | bytes 4194304 | tf_op jit(solution)/shard_map/pallas_call | solution.py:233
  57.7 1.1 copy-done.9
  58.8 0.7 copy-done.11
  59.5 0.7 copy-done.13
  60.2 11.3 %all-to-all-start.1 = ((bf16[32,16,128]{2,1,0:T(8,128)(2,1)}), bf16[32,16,128]{2,1,0:T(8,128)(2,1)}, u32[]{:S(2)}, u32[]{:S(2)}) async-start(bf16[32,16,128]{2,1,0:T(8,128)(2,1)} %get-tuple-element.21), calls=%async_computation.1 | async-start | bytes 262144 | tf_op jit(solution)/shard_map/all_to_all | solution.py:281
  71.5 0.2 copy.43
  71.7 0.2 copy.44
  71.9 0.0 copy-start.10
  71.9 1.3 copy-done.10
  73.2 0.9 copy-done.12
  74.2 0.9 copy-done.14
  75.1 1.8 %shard_map.165 = bf16[2560,128]{1,0:T(8,128)(2,1)S(1)} custom-call(f32[128,768]{1,0:T(8,128)S(1)} %get-tuple-element.15.spec, bf16[14,128,384]{2,1,0:T(8,128)(2,1)S(1)} %get-tuple-element.16.m3, bf16[12,128,384]{2,1,0:T(8,128)(2,1)S(1)} %copy-done.10, f32[4,128,128]{2,1,0:T(8,128)S(1)} %get-tuple-element.18.rise1, bf16[8,128,128]{2,1,0:T(8,128)(2,1)S(1)} %copy-done.12, ...), custom_call_target="tpu_custom_call" | custom-call | flops 2147483648 | bytes 4194304 | tf_op jit(solution)/shard_map/pallas_call | solution.py:233
  76.9 9.3 %all-to-all-done.1 = bf16[32,16,128]{2,1,0:T(8,128)(2,1)} async-done(((bf16[32,16,128]{2,1,0:T(8,128)(2,1)}), bf16[32,16,128]{2,1,0:T(8,128)(2,1)}, u32[]{:S(2)}, u32[]{:S(2)}) %all-to-all-start.1) | async-done | bytes 131104 | tf_op jit(solution)/shard_map/all_to_all | solution.py:281
  86.2 16.1 %all_to_all.26 = bf16[32,80,128]{2,1,0:T(8,128)(2,1)S(1)} all-to-all(bf16[32,80,128]{2,1,0:T(8,128)(2,1)S(1)} %bitcast.32), channel_id=1, replica_groups=mesh['y'=4,'zl'=8,'x'=4,'zh'=2,'c'=2] {'y','x','c'}, dimensions={0} | all-to-all | bytes 1310720 | tf_op jit(solution)/shard_map/all_to_all | solution.py:294
  102.3 0.1 reduce_sum.24
  102.4 0.8 broadcast_in_dim.6
  103.2 5.8 %all-to-all-start.3 = ((bf16[16,80,128]{2,1,0:T(8,128)(2,1)}), bf16[16,80,128]{2,1,0:T(8,128)(2,1)S(1)}, u32[]{:S(2)}, u32[]{:S(2)}) async-start(bf16[16,80,128]{2,1,0:T(8,128)(2,1)} %broadcast_in_dim.6), calls=%async_computation.3 | async-start | bytes 655360 | tf_op jit(solution)/shard_map/all_to_all | solution.py:296
  109.1 18.3 %all-to-all-done.3 = bf16[16,80,128]{2,1,0:T(8,128)(2,1)S(1)} async-done(((bf16[16,80,128]{2,1,0:T(8,128)(2,1)}), bf16[16,80,128]{2,1,0:T(8,128)(2,1)S(1)}, u32[]{:S(2)}, u32[]{:S(2)}) %all-to-all-start.3) | async-done | bytes 327712 | tf_op jit(solution)/shard_map/all_to_all | solution.py:296
  127.4 0.1 reduce_sum.25
  127.5 0.9 broadcast_in_dim.7
  128.4 8.1 %all-to-all-start.4 = ((bf16[32,80,128]{2,1,0:T(8,128)(2,1)}), bf16[32,80,128]{2,1,0:T(8,128)(2,1)S(1)}, u32[]{:S(2)}, u32[]{:S(2)}) async-start(bf16[32,80,128]{2,1,0:T(8,128)(2,1)} %broadcast_in_dim.7), calls=%async_computation.4 | async-start | bytes 1310720 | tf_op jit(solution)/shard_map/all_to_all | solution.py:298
  136.5 0.9 slice_bitcast_fusion
  137.5 0.1 pad_maximum_fusion
  137.6 0.1 copy.45
  137.7 0.1 copy.46
  137.8 0.1 rev.7
  137.9 0.8 copy.47
  138.7 10.7 %all-to-all-done.4 = bf16[32,80,128]{2,1,0:T(8,128)(2,1)S(1)} async-done(((bf16[32,80,128]{2,1,0:T(8,128)(2,1)}), bf16[32,80,128]{2,1,0:T(8,128)(2,1)S(1)}, u32[]{:S(2)}, u32[]{:S(2)}) %all-to-all-start.4) | async-done | bytes 655392 | tf_op jit(solution)/shard_map/all_to_all | solution.py:298
  149.4 0.1 bitcast_convert_fusion
  149.5 1.1 fusion.2
  150.6 0.6 slice.52
  151.3 0.5 fusion
  (26 shorter events, 0.1 us)
Async XLA Ops:
  0.6 0.9 copy-start
  1.5 0.9 copy-start.1
  2.4 46.1 %copy-start.15 = (bf16[3,3,128,128]{3,2,1,0:T(8,128)(2,1)S(1)}, bf16[3,3,128,128]{3,2,1,0:T(8,128)(2,1)}, u32[]{:S(2)}) copy-start(bf16[3,3,128,128]{3,2,1,0:T(8,128)(2,1)} %param.14) | copy-start | bytes 884740
  2.4 46.2 %copy-start.16 = (bf16[3,3,128,128]{3,2,1,0:T(8,128)(2,1)S(1)}, bf16[3,3,128,128]{3,2,1,0:T(8,128)(2,1)}, u32[]{:S(2)}) copy-start(bf16[3,3,128,128]{3,2,1,0:T(8,128)(2,1)} %param.16) | copy-start | bytes 884740
  2.4 50.9 %copy-start.2 = (bf16[128,128]{1,0:T(8,128)(2,1)S(1)}, bf16[128,128]{1,0:T(8,128)(2,1)}, u32[]{:S(2)}) copy-start(bf16[128,128]{1,0:T(8,128)(2,1)} %ker.1) | copy-start | bytes 98308
  2.5 50.9 %copy-start.3 = (f32[128]{0:T(128)S(1)}, f32[128]{0:T(128)}, u32[]{:S(2)}) copy-start(f32[128]{0:T(128)} %param.15) | copy-start | bytes 1540
  2.5 50.9 %copy-start.4 = (f32[128]{0:T(128)S(1)}, f32[128]{0:T(128)}, u32[]{:S(2)}) copy-start(f32[128]{0:T(128)} %param.17) | copy-start | bytes 1540
  2.5 50.9 %copy-start.6 = (bf16[128,384]{1,0:T(8,128)(2,1)S(1)}, bf16[128,384]{1,0:T(8,128)(2,1)}, u32[]{:S(2)}) copy-start(bf16[128,384]{1,0:T(8,128)(2,1)} %constant.19.clone.inv) | copy-start | bytes 294916
  2.5 50.9 %copy-start.7 = (bf16[128,256]{1,0:T(8,128)(2,1)S(1)}, bf16[128,256]{1,0:T(8,128)(2,1)}, u32[]{:S(2)}) copy-start(bf16[128,256]{1,0:T(8,128)(2,1)} %constant.18.clone.fwd) | copy-start | bytes 196612
  2.5 50.9 %copy-start.8 = (bf16[128,256]{1,0:T(8,128)(2,1)S(1)}, bf16[128,256]{1,0:T(8,128)(2,1)}, u32[]{:S(2)}) copy-start(bf16[128,256]{1,0:T(8,128)(2,1)} %constant.20.clone.fwd_nat) | copy-start | bytes 196612
  37.4 15.9 %collective-permute-start.1 = (bf16[32,32,128]{2,1,0:T(8,128)(2,1)S(1)}, bf16[32,32,128]{2,1,0:T(8,128)(2,1)S(1)}, u32[]{:S(2)}, u32[]{:S(2)}) collective-permute-start(bf16[32,32,128]{2,1,0:T(8,128)(2,1)S(1)} %all_to_all.25.own), channel_id=1, source_target_pairs={{112,240},{240,368},{368,496},{496,480},{480,352},{352,224},{224,9... | collective-permute-start | bytes 786440 | tf_op jit(solution)/shard_map/ppermute | solution.py:276
  39.3 14.0 %collective-permute-start.2 = (bf16[32,32,128]{2,1,0:T(8,128)(2,1)S(1)}, bf16[32,32,128]{2,1,0:T(8,128)(2,1)S(1)}, u32[]{:S(2)}, u32[]{:S(2)}) collective-permute-start(bf16[32,32,128]{2,1,0:T(8,128)(2,1)S(1)} %all_to_all.25.own), channel_id=1, source_target_pairs={{112,15},{240,112},{368,240},{496,368},{480,496},{352,480},{224,35... | collective-permute-start | bytes 786440 | tf_op jit(solution)/shard_map/ppermute | solution.py:276
  43.0 7.6 %collective-permute-start = (bf16[32,8,128]{2,1,0:T(8,128)(2,1)S(1)}, bf16[32,8,128]{2,1,0:T(8,128)(2,1)S(1)}, u32[]{:S(2)}, u32[]{:S(2)}) collective-permute-start(bf16[32,8,128]{2,1,0:T(8,128)(2,1)S(1)} %get-tuple-element.29), channel_id=1, source_target_pairs={{112,368},{240,496},{368,480},{496,352},{480,224},{352,96},{224,80... | collective-permute-start | bytes 196616 | tf_op jit(solution)/shard_map/ppermute | solution.py:276
  45.4 7.9 %collective-permute-start.3 = (bf16[32,8,128]{2,1,0:T(8,128)(2,1)S(1)}, bf16[32,8,128]{2,1,0:T(8,128)(2,1)S(1)}, u32[]{:S(2)}, u32[]{:S(2)}) collective-permute-start(bf16[32,8,128]{2,1,0:T(8,128)(2,1)S(1)} %get-tuple-element.28), channel_id=1, source_target_pairs={{112,143},{240,15},{368,112},{496,240},{480,368},{352,496},{224,48... | collective-permute-start | bytes 196616 | tf_op jit(solution)/shard_map/ppermute | solution.py:276
  57.7 1.1 copy-start.9
  58.8 0.7 copy-start.11
  59.5 0.7 copy-start.13
  60.2 11.7 %copy-start.5 = (bf16[128,384]{1,0:T(8,128)(2,1)S(1)}, bf16[128,384]{1,0:T(8,128)(2,1)}, u32[]{:S(2)}) copy-start(bf16[128,384]{1,0:T(8,128)(2,1)} %constant.21.clone.inv_nat) | copy-start | bytes 294916
  60.2 26.0 %all-to-all-start.1 = ((bf16[32,16,128]{2,1,0:T(8,128)(2,1)}), bf16[32,16,128]{2,1,0:T(8,128)(2,1)}, u32[]{:S(2)}, u32[]{:S(2)}) async-start(bf16[32,16,128]{2,1,0:T(8,128)(2,1)} %get-tuple-element.21), calls=%async_computation.1 | async-start | bytes 262144 | tf_op jit(solution)/shard_map/all_to_all | solution.py:281
  71.9 1.3 copy-start.10
  73.2 0.9 copy-start.12
  74.1 0.9 copy-start.14
  103.2 24.2 %all-to-all-start.3 = ((bf16[16,80,128]{2,1,0:T(8,128)(2,1)}), bf16[16,80,128]{2,1,0:T(8,128)(2,1)S(1)}, u32[]{:S(2)}, u32[]{:S(2)}) async-start(bf16[16,80,128]{2,1,0:T(8,128)(2,1)} %broadcast_in_dim.6), calls=%async_computation.3 | async-start | bytes 655360 | tf_op jit(solution)/shard_map/all_to_all | solution.py:296
  128.4 21.0 %all-to-all-start.4 = ((bf16[32,80,128]{2,1,0:T(8,128)(2,1)}), bf16[32,80,128]{2,1,0:T(8,128)(2,1)S(1)}, u32[]{:S(2)}, u32[]{:S(2)}) async-start(bf16[32,80,128]{2,1,0:T(8,128)(2,1)} %broadcast_in_dim.7), calls=%async_computation.4 | async-start | bytes 1310720 | tf_op jit(solution)/shard_map/all_to_all | solution.py:298

commit v3 on v2

--- a/solution.py
+++ b/solution.py
@@ -126,9 +126,9 @@
     return jnp.concatenate([ref[pl.ds(start + rr, 32, stride=stride), :] for rr in range(4)], axis=0)
 
 
-def forward_kernel(far_left, left, own, right, far_right, ker, w1, b1, w2, b2, fwd, inv, fwd_nat,
-                   pred, spec, m3, h3, rise1, slope2, cot_own,
-                   gl, go, gr, gl2, gr2, latf, xw, parts, cots, hid, placed):
+def step_kernel(far_left, left, own, right, far_right, ker, w1, b1, w2, b2, w1b, w2b, fwd, inv, fwd_nat, inv_nat,
+                pred, out,
+                gl, go, gr, gl2, gr2, latf, xw, parts, cots, hid, placed, spec, m3, h3, rise1, slope2, s3, z3, gm):
     for ref, wide in ((left, gl), (own, go), (right, gr), (far_left, gl2), (far_right, gr2)):
         wide[...] = ref[...].reshape(wide.shape).astype(F4)
     lat_from = ([(gl2, 4, 8)] + [(gl, 4 * j, 32) for j in range(4)] + [(go, 4 * j, 32) for j in range(4)]
@@ -142,7 +142,6 @@
     cot_from = [(gl, 24), (gl, 28)] + [(go, 16 + 4 * j) for j in range(4)] + [(gr, 16), (gr, 20)]
     for u, (ref, start) in enumerate(cot_from):
         cots[u] = column(ref, start, 32)
-    cot_own[...] = cots[2:6]
     ker_two = jnp.concatenate([ker[...], ker[...]], axis=0)
     ker_spec = dot(fwd_nat[...], ker_two)
     for j in range(0, 14, 2):
@@ -186,8 +185,6 @@
                     placed[pl.ds((u - 2) * 4 + rr, 32, stride=16), :] = p[rr * 32 : rr * 32 + 32]
     pred[...] = placed[...].astype(BF).reshape(PEERS, 16, CH)
 
-
-def backward_kernel(spec, m3, h3, rise1, slope2, cot_own, w1b, w2b, fwd, inv_nat, out, s3, z3, gm):
     own2 = slope2[2:6].reshape(512, CH)
     for q in range(3):
         d = dot_t(h3[2 + 2 * q : 6 + 2 * q].reshape(512, 384), own2)
@@ -195,7 +192,7 @@
             out[1152 + (p * 3 + q) * 128 : 1280 + (p * 3 + q) * 128, :] = d[p * 128 : p * 128 + 128].astype(BF)
     for u in range(8):
         put_turned(s3, u, slope2[u].astype(F4), (2, 0, -2))
-    gh = cot_own[...].reshape(512, CH)
+    gh = cots[2:6].reshape(512, CH)
     for q in range(3):
         gh = gh + dot(s3[4 - 2 * q : 8 - 2 * q].reshape(512, 384), w2b[q])
     slope1 = (gh * rise1[...].reshape(512, CH)).astype(BF)
@@ -229,44 +226,57 @@
     out[2432:GRAD_ROWS, :] = tail.astype(BF)
 
 
-def call(kernel, outs, scratch, flops, *args):
+def finish_kernel(whole, dw1, dw2, dk, db1, db2):
+    rows = whole[...].reshape(GRAD_ROWS, CH)
+    dw1[...] = rows[0:1152].astype(F4)
+    dw2[...] = rows[1152:2304].astype(F4)
+    dk[...] = rows[2304:2432].astype(F4)
+    tail = rows[2432:2448].astype(F4)
+    db1[...] = tail[0:1] + tail[1:2]
+    db2[...] = tail[2:3] + tail[3:4]
+
+
+def call(kernel, outs, scratch, flops, mib, *args):
     return pl.pallas_call(
         kernel,
         out_shape=[jax.ShapeDtypeStruct(s, d) for s, d in outs],
         in_specs=[VMEM] * len(args),
         out_specs=[VMEM] * len(outs),
         scratch_shapes=[pltpu.VMEM(s, d) for s, d in scratch],
-        compiler_params=pltpu.CompilerParams(vmem_limit_bytes=40 << 20),
+        compiler_params=pltpu.CompilerParams(vmem_limit_bytes=mib << 20),
         cost_estimate=pl.CostEstimate(flops=flops, bytes_accessed=4 << 20, transcendentals=0),
     )(*args)
 
 
-def forward(far_left, left, own, right, far_right, ker, w1, b1, w2, b2):
-    fwd, inv, fwd_nat, _ = (jnp.asarray(t, BF) for t in tables())
-    w1q = w1.transpose(1, 0, 2, 3).reshape(3, 384, CH)
-    w2q = w2.transpose(1, 0, 2, 3).reshape(3, 384, CH)
-    outs = [((PEERS, 16, CH), BF), ((128, 6 * CH), F4), ((14, 128, 384), BF), ((12, 128, 384), BF),
-            ((4, 128, CH), F4), ((8, 128, CH), BF), ((4, 128, CH), F4)]
+def local_step(far_left, left, own, right, far_right, ker, w1, b1, w2, b2):
+    fwd, inv, fwd_nat, inv_nat = (jnp.asarray(t, BF) for t in tables())
+    w1q, w2q = (w.transpose(1, 0, 2, 3).reshape(3, 384, CH) for w in (w1, w2))
+    w1b, w2b = (w.transpose(1, 0, 3, 2).reshape(3, 384, CH) for w in (w1, w2))
+    outs = [((PEERS, 16, CH), BF), ((GRAD_ROWS, CH), BF)]
     scratch = [((1024, CH), F4)] * 3 + [((256, CH), F4)] * 2 + [
         ((14, 128, CH), F4), ((256, 14 * CH), BF), ((384, 2 * CH), BF), ((8, 128, CH), F4), ((12, 128, CH), F4),
-        ((512, CH), F4)]
-    return call(forward_kernel, outs, scratch, 1 << 30, far_left, left, own, right, far_right, ker,
-                w1q, b1.reshape(1, CH), w2q, b2.reshape(1, CH), fwd, inv, fwd_nat)
-
-
-def backward(w1, w2, spec, m3, h3, rise1, slope2, cot_own):
-    fwd, _, _, inv_nat = (jnp.asarray(t, BF) for t in tables())
-    w1b = w1.transpose(1, 0, 3, 2).reshape(3, 384, CH)
-    w2b = w2.transpose(1, 0, 3, 2).reshape(3, 384, CH)
-    outs = [((GRAD_ROWS, CH), BF)]
-    scratch = [((8, 128, 384), BF), ((4, 128, 384), BF), ((6, 128, CH), F4)]
-    return call(backward_kernel, outs, scratch, 1 << 31, spec, m3, h3, rise1, slope2, cot_own, w1b, w2b, fwd, inv_nat)[0]
+        ((512, CH), F4),
+        ((128, 6 * CH), F4), ((14, 128, 384), BF), ((12, 128, 384), BF), ((4, 128, CH), F4), ((8, 128, CH), BF),
+        ((8, 128, 384), BF), ((4, 128, 384), BF), ((6, 128, CH), F4)]
+    return call(step_kernel, outs, scratch, 3 << 30, 24, far_left, left, own, right, far_right, ker,
+                w1q, b1.reshape(1, CH), w2q, b2.reshape(1, CH), w1b, w2b, fwd, inv, fwd_nat, inv_nat)
+
+
+def depth_sum(part):
+    def moved(x, target):
+        flat = [(z % 8) * 2 + z // 8 for z in range(16)]
+        return lax.ppermute(x, DEPTH_AXES, [(flat[z], flat[target(z)]) for z in range(16)])
+
+    opposite, ahead, behind = (moved(part, lambda z, d=d: (z + d) % 16) for d in (8, 4, 12))
+    part = (part + opposite) + (ahead + behind)
+    one, two, three = (moved(part, lambda z, d=d: z ^ d) for d in (1, 2, 3))
+    return (part + one) + (two + three)
 
 
 def per_device(latent, corr_kernel, w1, b1, w2, b2, cotangent):
     row_count, col_count, _ = latent.shape
     flip = flipped(lax.axis_index("zh"), lax.axis_index("c"))
-    (send,) = call(send_kernel, [((PEERS, 32, CH), BF)], [((1024, CH), F4), ((1024, CH), F4)], 1 << 20, latent, cotangent)
+    (send,) = call(send_kernel, [((PEERS, 32, CH), BF)], [((1024, CH), F4), ((1024, CH), F4)], 1 << 20, 4, latent, cotangent)
     own = lax.all_to_all(send, ROWS_AXES, 0, 0, tiled=True)
     ring = device_ring()
     n = len(ring)
@@ -277,10 +287,15 @@
 
     left, right = shifted(own, 1), shifted(own, -1)
     far_left, far_right = shifted(own[:, 8:16], 2), shifted(own[:, 0:8], -2)
-    pred_send, *kept = forward(far_left, left, own, right, far_right, corr_kernel, w1, b1, w2, b2)
+    pred_send, grads = local_step(far_left, left, own, right, far_right, corr_kernel, w1, b1, w2, b2)
+    n_plane = lax.axis_size(PLANE_AXES)
+    share = GRAD_ROWS // n_plane
+    part = lax.all_to_all(grads.reshape(n_plane, share, CH), PLANE_AXES, 0, 0, tiled=True)
+    part, pred_send = lax.optimization_barrier((part, pred_send))
     pred_got = lax.all_to_all(pred_send, ROWS_AXES, 0, 0, tiled=True)
-    grads = backward(w1, w2, *kept)
-    grads, pred_got = lax.optimization_barrier((grads, pred_got))
+    part = depth_sum(jnp.sum(part.astype(F4), axis=0)).astype(BF)
+    part, pred_got = lax.optimization_barrier((part, pred_got))
+    whole = lax.all_to_all(jnp.broadcast_to(part, (n_plane, share, CH)), PLANE_AXES, 0, 0, tiled=True)
 
     got = pred_got.reshape(4, 8, 4, row_count, CH)
     even, odd = got[:, 0::2], got[::-1, 1::2]
@@ -289,16 +304,10 @@
     got = jnp.where(flip, got[::-1], got)
     pred_out = got.transpose(2, 0, 1, 3).reshape(row_count, col_count, CH)
 
-    n_plane, n_depth = lax.axis_size(PLANE_AXES), lax.axis_size(DEPTH_AXES)
-    share = GRAD_ROWS // n_plane
-    part = lax.all_to_all(grads.reshape(n_plane, share, CH), PLANE_AXES, 0, 0, tiled=True)
-    part = jnp.sum(part.astype(F4), axis=0).astype(BF)
-    part = lax.all_to_all(jnp.broadcast_to(part, (n_depth, share, CH)), DEPTH_AXES, 0, 0, tiled=True)
-    part = jnp.sum(part.astype(F4), axis=0).astype(BF)
-    whole = lax.all_to_all(jnp.broadcast_to(part, (n_plane, share, CH)), PLANE_AXES, 0, 0, tiled=True)
-    whole = whole.reshape(GRAD_ROWS, CH).astype(F4)
-    dw1, dw2 = (whole[a : a + 1152].reshape(3, 3, CH, CH) for a in (0, 1152))
-    return pred_out, dw1, whole[2432] + whole[2433], dw2, whole[2434] + whole[2435], whole[2304:2432]
+    shapes = [(1152, CH), (1152, CH), (CH, CH), (1, CH), (1, CH)]
+    dw1, dw2, dk, db1, db2 = call(finish_kernel, [(shape, F4) for shape in shapes], [], 1 << 20, 8, whole)
+    grad_shape = (3, 3, CH, CH)
+    return pred_out, dw1.reshape(grad_shape), db1.reshape(CH), dw2.reshape(grad_shape), db2.reshape(CH), dk
 
 
 def solution(mesh):

time: 154 us -> 140 us (0.909); the launches traced: 152 us -> 140 us
  waiting for transfers between devices: 43.1 us -> 20.3 us
  starting transfers between devices: 36.3 us -> 50.9 us
  local copies, waits for them, and re-layouts: 13.4 us -> 4.41 us
  blocking collectives: 50.7 us -> 56.2 us
    ppermute x0 -> x6, starting transfers between devices: none -> 27.7 us  [moved(): lax.ppermute(x, DEPTH_AXES, [(flat[z], flat[target(z)]) for z in range(16)])]
    all_to_all x1 -> x0, waiting for transfers between devices: 18.3 us -> none  [per_device(): lax.all_to_all(jnp.broadcast_to(part, (n_depth, share, CH)), DEPTH_AXES,...]
    all_to_all x1, waiting for transfers between devices: 9.35 us -> 0.01 us  [per_device(): pred_got = lax.all_to_all(pred_send, ROWS_AXES, 0, 0, tiled=True)]
    all_to_all x1, starting transfers between devices: 11.3 us -> 3.87 us  [per_device(): pred_got = lax.all_to_all(pred_send, ROWS_AXES, 0, 0, tiled=True)]
    all_to_all x1 -> x0, starting transfers between devices: 5.85 us -> none  [per_device(): lax.all_to_all(jnp.broadcast_to(part, (n_depth, share, CH)), DEPTH_AXES,...]
    unnamed x34 -> x22, local copies, waits for them, and re-layouts: 7.47 us -> 1.86 us
    all_to_all x1, blocking collectives: 16.1 us -> 21.4 us  [per_device(): lax.all_to_all(grads.reshape(n_plane, share, CH), PLANE_AXES, 0, 0, tiled...]
    ppermute x0 -> x6, waiting for transfers between devices: none -> 4.58 us  [moved(): lax.ppermute(x, DEPTH_AXES, [(flat[z], flat[target(z)]) for z in range(16)])]
  transfers between devices with their start and end apart: 7 -> 12, of which waited for: 5 -> 5; matrix products, arithmetic and copies ran while one was open for 2% -> 1% of each run, Pallas kernels for 1% -> 0%
where the time goes in v3:
time: 140 us
  blocking collectives  56.2 us (40%)
  starting transfers between devices  50.9 us (36%)
  waiting for transfers between devices  20.3 us (14%)
  Pallas kernels  6.68 us (5%)
  local copies, waits for them, and re-layouts  4.41 us (3%)
    all_to_all x1, blocking collectives, per_device(): own = lax.all_to_all(send, ROWS_AXES, 0, 0, tiled=True)  34.8 us
    ppermute x6, starting transfers between devices, moved(): lax.ppermute(x, DEPTH_AXES, [(flat[z], flat[target(z)]) for z in range(16)])  27.7 us
    all_to_all x1, blocking collectives, per_device(): lax.all_to_all(grads.reshape(n_plane, share, CH), PLANE_AXES, 0, 0, tiled...  21.4 us
    all_to_all x1, waiting for transfers between devices, per_device(): lax.all_to_all(jnp.broadcast_to(part, (n_plane, share, CH)), PLANE_AXES,...  11.6 us
    ppermute x4, starting transfers between devices, shifted(): lax.ppermute(block, everywhere, [(ring[i], ring[(i + by) % n]) for i in r...  11.1 us
    all_to_all x1, starting transfers between devices, per_device(): lax.all_to_all(jnp.broadcast_to(part, (n_plane, share, CH)), PLANE_AXES,...  8.19 us
    pallas_call x3, Pallas kernels, call(): pl.pallas_call(kernel, out_shape=[jax.ShapeDtypeStruct(s, d) for s, d in...  6.68 us
    ppermute x6, waiting for transfers between devices, moved(): lax.ppermute(x, DEPTH_AXES, [(flat[z], flat[target(z)]) for z in range(16)])  4.58 us
  transfers between devices with their start and end apart: 12, of which 5 were waited for; matrix products, arithmetic and copies ran while one was open for 1% of the time, Pallas kernels for 0%

profile of v3, /device:TPU:1, one launch (start us, length us, event | category | flops | bytes accessed | tf_op | source)
XLA Modules:
  0.0 139.8 jit_solution(4630775089038905805)
XLA Ops:
  0.6 0.9 copy-done
  1.5 0.9 copy-done.1
  2.4 0.3 shard_map.154
  2.7 34.8 %all_to_all.20.own = bf16[32,32,128]{2,1,0:T(8,128)(2,1)S(1)} all-to-all(bf16[32,32,128]{2,1,0:T(8,128)(2,1)S(1)} %shard_map.154), channel_id=1, replica_groups=mesh['y'=4,'zl'=8,'x'=4,'zh'=2,'c'=2] {'y','zl'}, dimensions={0} | all-to-all | bytes 524288 | tf_op jit(solution)/shard_map/all_to_all | solution.py:280
  37.5 1.9 %collective-permute-start.1 = (bf16[32,32,128]{2,1,0:T(8,128)(2,1)S(1)}, bf16[32,32,128]{2,1,0:T(8,128)(2,1)S(1)}, u32[]{:S(2)}, u32[]{:S(2)}) collective-permute-start(bf16[32,32,128]{2,1,0:T(8,128)(2,1)S(1)} %all_to_all.20.own), channel_id=1, source_target_pairs={{112,240},{240,368},{368,496},{496,480},{480,352},{352,224},{224,9... | collective-permute-start | bytes 786440 | tf_op jit(solution)/shard_map/ppermute | solution.py:286
  39.4 3.7 %collective-permute-start.2 = (bf16[32,32,128]{2,1,0:T(8,128)(2,1)S(1)}, bf16[32,32,128]{2,1,0:T(8,128)(2,1)S(1)}, u32[]{:S(2)}, u32[]{:S(2)}) collective-permute-start(bf16[32,32,128]{2,1,0:T(8,128)(2,1)S(1)} %all_to_all.20.own), channel_id=1, source_target_pairs={{112,15},{240,112},{368,240},{496,368},{480,496},{352,480},{224,35... | collective-permute-start | bytes 786440 | tf_op jit(solution)/shard_map/ppermute | solution.py:286
  43.1 2.4 %collective-permute-start = (bf16[32,8,128]{2,1,0:T(8,128)(2,1)S(1)}, bf16[32,8,128]{2,1,0:T(8,128)(2,1)S(1)}, u32[]{:S(2)}, u32[]{:S(2)}) collective-permute-start(bf16[32,8,128]{2,1,0:T(8,128)(2,1)S(1)} %get-tuple-element.29), channel_id=1, source_target_pairs={{112,368},{240,496},{368,480},{496,352},{480,224},{352,96},{224,80... | collective-permute-start | bytes 196616 | tf_op jit(solution)/shard_map/ppermute | solution.py:286
  45.5 3.1 %collective-permute-start.3 = (bf16[32,8,128]{2,1,0:T(8,128)(2,1)S(1)}, bf16[32,8,128]{2,1,0:T(8,128)(2,1)S(1)}, u32[]{:S(2)}, u32[]{:S(2)}) collective-permute-start(bf16[32,8,128]{2,1,0:T(8,128)(2,1)S(1)} %get-tuple-element.28), channel_id=1, source_target_pairs={{112,143},{240,15},{368,112},{496,240},{480,368},{352,496},{224,48... | collective-permute-start | bytes 196616 | tf_op jit(solution)/shard_map/ppermute | solution.py:286
  48.7 0.0 copy-start.2
  48.8 0.0 copy-start.3
  48.8 0.0 copy-start.4
  48.8 0.0 copy-start.5
  48.8 0.0 copy-start.6
  48.8 0.0 copy-start.7
  48.8 0.0 copy-start.8
  48.8 0.2 copy.35
  49.0 0.2 copy.36
  49.3 1.5 %collective-permute-done.far_left = bf16[32,8,128]{2,1,0:T(8,128)(2,1)S(1)} collective-permute-done((bf16[32,8,128]{2,1,0:T(8,128)(2,1)S(1)}, bf16[32,8,128]{2,1,0:T(8,128)(2,1)S(1)}, u32[]{:S(2)}, u32[]{:S(2)}) %collective-permute-start) | collective-permute-done | bytes 65568 | tf_op jit(solution)/shard_map/ppermute | solution.py:286
  50.7 2.7 %collective-permute-done.3.far_right = bf16[32,8,128]{2,1,0:T(8,128)(2,1)S(1)} collective-permute-done((bf16[32,8,128]{2,1,0:T(8,128)(2,1)S(1)}, bf16[32,8,128]{2,1,0:T(8,128)(2,1)S(1)}, u32[]{:S(2)}, u32[]{:S(2)}) %collective-permute-start.3) | collective-permute-done | bytes 65568 | tf_op jit(solution)/shard_map/ppermute | solution.py:286
  53.4 0.0 collective-permute-done.1.left
  53.4 0.0 collective-permute-done.2.right
  53.4 0.0 copy-done.3
  53.5 5.3 %shard_map.155 = (bf16[32,16,128]{2,1,0:T(8,128)(2,1)}, bf16[2560,128]{1,0:T(8,128)(2,1)S(1)}) custom-call(bf16[32,8,128]{2,1,0:T(8,128)(2,1)S(1)} %collective-permute-done.far_left, bf16[32,32,128]{2,1,0:T(8,128)(2,1)S(1)} %collective-permute-done.1.left, bf16[32,32,128]{2,1,0:T(8,128)(2,1)S(1)} %all_to_all.20.own, ...), custom_call_target="tpu_custom_call" | custom-call | flops 3221225472 | bytes 4194304 | tf_op jit(solution)/shard_map/pallas_call | solution.py:240
  58.8 21.4 %all_to_all.21 = bf16[32,80,128]{2,1,0:T(8,128)(2,1)S(1)} all-to-all(bf16[32,80,128]{2,1,0:T(8,128)(2,1)S(1)} %bitcast.27), channel_id=1, replica_groups=mesh['y'=4,'zl'=8,'x'=4,'zh'=2,'c'=2] {'y','x','c'}, dimensions={0} | all-to-all | bytes 1310720 | tf_op jit(solution)/shard_map/all_to_all | solution.py:293
  80.2 0.1 convert_reduce_fusion
  80.3 9.3 %collective-permute-start.4 = (f32[80,128]{1,0:T(8,128)S(1)}, f32[80,128]{1,0:T(8,128)S(1)}, u32[]{:S(2)}, u32[]{:S(2)}) collective-permute-start(f32[80,128]{1,0:T(8,128)S(1)} %convert_reduce_fusion), channel_id=1, source_target_pairs={{0,2},{16,18},{32,34},{48,50},{64,66},{80,82},{96,98},{112,114},{2... | collective-permute-start | bytes 122888 | tf_op jit(solution)/shard_map/ppermute | solution.py:268
  89.6 1.9 %collective-permute-start.5 = (f32[80,128]{1,0:T(8,128)S(1)}, f32[80,128]{1,0:T(8,128)S(1)}, u32[]{:S(2)}, u32[]{:S(2)}) collective-permute-start(f32[80,128]{1,0:T(8,128)S(1)} %convert_reduce_fusion), channel_id=1, source_target_pairs={{0,64},{16,80},{32,96},{48,112},{64,2},{80,18},{96,34},{112,50},{2... | collective-permute-start | bytes 122888 | tf_op jit(solution)/shard_map/ppermute | solution.py:268
  91.5 7.3 %collective-permute-start.6 = (f32[80,128]{1,0:T(8,128)S(1)}, f32[80,128]{1,0:T(8,128)S(1)}, u32[]{:S(2)}, u32[]{:S(2)}) collective-permute-start(f32[80,128]{1,0:T(8,128)S(1)} %convert_reduce_fusion), channel_id=1, source_target_pairs={{0,66},{16,82},{32,98},{48,114},{64,0},{80,16},{96,32},{112,48},{2... | collective-permute-start | bytes 122888 | tf_op jit(solution)/shard_map/ppermute | solution.py:268
  98.8 3.9 %all-to-all-start.2 = ((bf16[32,16,128]{2,1,0:T(8,128)(2,1)}), bf16[32,16,128]{2,1,0:T(8,128)(2,1)S(1)}, u32[]{:S(2)}, u32[]{:S(2)}) async-start(bf16[32,16,128]{2,1,0:T(8,128)(2,1)} %get-tuple-element.20), calls=%async_computation.2 | async-start | bytes 262144 | tf_op jit(solution)/shard_map/all_to_all | solution.py:295
  102.7 0.0 collective-permute-done.4
  102.7 0.0 collective-permute-done.5
  102.7 0.0 collective-permute-done.6
  102.8 3.0 %collective-permute-start.7 = (f32[80,128]{1,0:T(8,128)S(1)}, f32[80,128]{1,0:T(8,128)S(1)}, u32[]{:S(2)}, u32[]{:S(2)}) collective-permute-start(f32[80,128]{1,0:T(8,128)S(1)} %add_add_fusion), channel_id=1, source_target_pairs={{0,16},{16,0},{32,48},{48,32},{64,80},{80,64},{96,112},{112,96},{2... | collective-permute-start | bytes 122888 | tf_op jit(solution)/shard_map/ppermute | solution.py:268
  105.8 4.0 %collective-permute-start.8 = (f32[80,128]{1,0:T(8,128)S(1)}, f32[80,128]{1,0:T(8,128)S(1)}, u32[]{:S(2)}, u32[]{:S(2)}) collective-permute-start(f32[80,128]{1,0:T(8,128)S(1)} %add_add_fusion), channel_id=1, source_target_pairs={{0,32},{16,48},{32,0},{48,16},{64,96},{80,112},{96,64},{112,80},{2... | collective-permute-start | bytes 122888 | tf_op jit(solution)/shard_map/ppermute | solution.py:268
  109.8 2.2 %collective-permute-start.9 = (f32[80,128]{1,0:T(8,128)S(1)}, f32[80,128]{1,0:T(8,128)S(1)}, u32[]{:S(2)}, u32[]{:S(2)}) collective-permute-start(f32[80,128]{1,0:T(8,128)S(1)} %add_add_fusion), channel_id=1, source_target_pairs={{0,48},{16,32},{32,16},{48,0},{64,112},{80,96},{96,80},{112,64},{2... | collective-permute-start | bytes 122888 | tf_op jit(solution)/shard_map/ppermute | solution.py:268
  112.1 0.0 collective-permute-done.7
  112.1 0.1 collective-permute-done.8
  112.2 4.4 %collective-permute-done.9 = f32[80,128]{1,0:T(8,128)S(1)} collective-permute-done((f32[80,128]{1,0:T(8,128)S(1)}, f32[80,128]{1,0:T(8,128)S(1)}, u32[]{:S(2)}, u32[]{:S(2)}) %collective-permute-start.9) | collective-permute-done | bytes 40992 | tf_op jit(solution)/shard_map/ppermute | solution.py:268
  116.7 0.0 all-to-all-done.2
  116.7 0.9 broadcast_in_dim.3
  117.6 8.2 %all-to-all-start.3 = ((bf16[32,80,128]{2,1,0:T(8,128)(2,1)}), bf16[32,80,128]{2,1,0:T(8,128)(2,1)S(1)}, u32[]{:S(2)}, u32[]{:S(2)}) async-start(bf16[32,80,128]{2,1,0:T(8,128)(2,1)} %broadcast_in_dim.3), calls=%async_computation.3 | async-start | bytes 1310720 | tf_op jit(solution)/shard_map/all_to_all | solution.py:298
  125.9 0.1 pad_maximum_fusion
  126.0 0.1 copy.37
  126.1 0.1 copy.38
  126.3 0.1 rev.7
  126.3 0.8 copy.39
  127.1 11.6 %all-to-all-done.3.whole = bf16[32,80,128]{2,1,0:T(8,128)(2,1)S(1)} async-done(((bf16[32,80,128]{2,1,0:T(8,128)(2,1)}), bf16[32,80,128]{2,1,0:T(8,128)(2,1)S(1)}, u32[]{:S(2)}, u32[]{:S(2)}) %all-to-all-start.3) | async-done | bytes 655392 | tf_op jit(solution)/shard_map/all_to_all | solution.py:298
  138.7 1.1 shard_map.156
  (20 shorter events, 0.2 us)
Async XLA Ops:
  0.6 0.9 copy-start
  1.5 0.9 copy-start.1
  2.4 46.2 %copy-start.9 = (bf16[3,3,128,128]{3,2,1,0:T(8,128)(2,1)S(1)}, bf16[3,3,128,128]{3,2,1,0:T(8,128)(2,1)}, u32[]{:S(2)}) copy-start(bf16[3,3,128,128]{3,2,1,0:T(8,128)(2,1)} %param.13) | copy-start | bytes 884740
  2.7 46.0 %copy-start.10 = (bf16[3,3,128,128]{3,2,1,0:T(8,128)(2,1)S(1)}, bf16[3,3,128,128]{3,2,1,0:T(8,128)(2,1)}, u32[]{:S(2)}) copy-start(bf16[3,3,128,128]{3,2,1,0:T(8,128)(2,1)} %param.15) | copy-start | bytes 884740
  37.5 15.9 %collective-permute-start.1 = (bf16[32,32,128]{2,1,0:T(8,128)(2,1)S(1)}, bf16[32,32,128]{2,1,0:T(8,128)(2,1)S(1)}, u32[]{:S(2)}, u32[]{:S(2)}) collective-permute-start(bf16[32,32,128]{2,1,0:T(8,128)(2,1)S(1)} %all_to_all.20.own), channel_id=1, source_target_pairs={{112,240},{240,368},{368,496},{496,480},{480,352},{352,224},{224,9... | collective-permute-start | bytes 786440 | tf_op jit(solution)/shard_map/ppermute | solution.py:286
  39.4 14.0 %collective-permute-start.2 = (bf16[32,32,128]{2,1,0:T(8,128)(2,1)S(1)}, bf16[32,32,128]{2,1,0:T(8,128)(2,1)S(1)}, u32[]{:S(2)}, u32[]{:S(2)}) collective-permute-start(bf16[32,32,128]{2,1,0:T(8,128)(2,1)S(1)} %all_to_all.20.own), channel_id=1, source_target_pairs={{112,15},{240,112},{368,240},{496,368},{480,496},{352,480},{224,35... | collective-permute-start | bytes 786440 | tf_op jit(solution)/shard_map/ppermute | solution.py:286
  43.1 7.6 %collective-permute-start = (bf16[32,8,128]{2,1,0:T(8,128)(2,1)S(1)}, bf16[32,8,128]{2,1,0:T(8,128)(2,1)S(1)}, u32[]{:S(2)}, u32[]{:S(2)}) collective-permute-start(bf16[32,8,128]{2,1,0:T(8,128)(2,1)S(1)} %get-tuple-element.29), channel_id=1, source_target_pairs={{112,368},{240,496},{368,480},{496,352},{480,224},{352,96},{224,80... | collective-permute-start | bytes 196616 | tf_op jit(solution)/shard_map/ppermute | solution.py:286
  45.5 7.9 %collective-permute-start.3 = (bf16[32,8,128]{2,1,0:T(8,128)(2,1)S(1)}, bf16[32,8,128]{2,1,0:T(8,128)(2,1)S(1)}, u32[]{:S(2)}, u32[]{:S(2)}) collective-permute-start(bf16[32,8,128]{2,1,0:T(8,128)(2,1)S(1)} %get-tuple-element.28), channel_id=1, source_target_pairs={{112,143},{240,15},{368,112},{496,240},{480,368},{352,496},{224,48... | collective-permute-start | bytes 196616 | tf_op jit(solution)/shard_map/ppermute | solution.py:286
  48.7 4.7 %copy-start.2 = (bf16[128,128]{1,0:T(8,128)(2,1)S(1)}, bf16[128,128]{1,0:T(8,128)(2,1)}, u32[]{:S(2)}) copy-start(bf16[128,128]{1,0:T(8,128)(2,1)} %ker.1) | copy-start | bytes 98308
  48.8 4.7 %copy-start.3 = (f32[128]{0:T(128)S(1)}, f32[128]{0:T(128)}, u32[]{:S(2)}) copy-start(f32[128]{0:T(128)} %param.14) | copy-start | bytes 1540
  48.8 4.7 %copy-start.4 = (f32[128]{0:T(128)S(1)}, f32[128]{0:T(128)}, u32[]{:S(2)}) copy-start(f32[128]{0:T(128)} %param.16) | copy-start | bytes 1540
  48.8 4.7 %copy-start.5 = (bf16[128,384]{1,0:T(8,128)(2,1)S(1)}, bf16[128,384]{1,0:T(8,128)(2,1)}, u32[]{:S(2)}) copy-start(bf16[128,384]{1,0:T(8,128)(2,1)} %constant.17.clone.inv) | copy-start | bytes 294916
  48.8 4.7 %copy-start.6 = (bf16[128,384]{1,0:T(8,128)(2,1)S(1)}, bf16[128,384]{1,0:T(8,128)(2,1)}, u32[]{:S(2)}) copy-start(bf16[128,384]{1,0:T(8,128)(2,1)} %constant.19.clone.inv_nat) | copy-start | bytes 294916
  48.8 4.7 %copy-start.7 = (bf16[128,256]{1,0:T(8,128)(2,1)S(1)}, bf16[128,256]{1,0:T(8,128)(2,1)}, u32[]{:S(2)}) copy-start(bf16[128,256]{1,0:T(8,128)(2,1)} %constant.16.clone.fwd) | copy-start | bytes 196612
  48.8 4.6 %copy-start.8 = (bf16[128,256]{1,0:T(8,128)(2,1)S(1)}, bf16[128,256]{1,0:T(8,128)(2,1)}, u32[]{:S(2)}) copy-start(bf16[128,256]{1,0:T(8,128)(2,1)} %constant.18.clone.fwd_nat) | copy-start | bytes 196612
  80.3 22.4 %collective-permute-start.4 = (f32[80,128]{1,0:T(8,128)S(1)}, f32[80,128]{1,0:T(8,128)S(1)}, u32[]{:S(2)}, u32[]{:S(2)}) collective-permute-start(f32[80,128]{1,0:T(8,128)S(1)} %convert_reduce_fusion), channel_id=1, source_target_pairs={{0,2},{16,18},{32,34},{48,50},{64,66},{80,82},{96,98},{112,114},{2... | collective-permute-start | bytes 122888 | tf_op jit(solution)/shard_map/ppermute | solution.py:268
  89.6 13.1 %collective-permute-start.5 = (f32[80,128]{1,0:T(8,128)S(1)}, f32[80,128]{1,0:T(8,128)S(1)}, u32[]{:S(2)}, u32[]{:S(2)}) collective-permute-start(f32[80,128]{1,0:T(8,128)S(1)} %convert_reduce_fusion), channel_id=1, source_target_pairs={{0,64},{16,80},{32,96},{48,112},{64,2},{80,18},{96,34},{112,50},{2... | collective-permute-start | bytes 122888 | tf_op jit(solution)/shard_map/ppermute | solution.py:268
  91.5 11.2 %collective-permute-start.6 = (f32[80,128]{1,0:T(8,128)S(1)}, f32[80,128]{1,0:T(8,128)S(1)}, u32[]{:S(2)}, u32[]{:S(2)}) collective-permute-start(f32[80,128]{1,0:T(8,128)S(1)} %convert_reduce_fusion), channel_id=1, source_target_pairs={{0,66},{16,82},{32,98},{48,114},{64,0},{80,16},{96,32},{112,48},{2... | collective-permute-start | bytes 122888 | tf_op jit(solution)/shard_map/ppermute | solution.py:268
  98.8 17.8 %all-to-all-start.2 = ((bf16[32,16,128]{2,1,0:T(8,128)(2,1)}), bf16[32,16,128]{2,1,0:T(8,128)(2,1)S(1)}, u32[]{:S(2)}, u32[]{:S(2)}) async-start(bf16[32,16,128]{2,1,0:T(8,128)(2,1)} %get-tuple-element.20), calls=%async_computation.2 | async-start | bytes 262144 | tf_op jit(solution)/shard_map/all_to_all | solution.py:295
  102.8 9.3 %collective-permute-start.7 = (f32[80,128]{1,0:T(8,128)S(1)}, f32[80,128]{1,0:T(8,128)S(1)}, u32[]{:S(2)}, u32[]{:S(2)}) collective-permute-start(f32[80,128]{1,0:T(8,128)S(1)} %add_add_fusion), channel_id=1, source_target_pairs={{0,16},{16,0},{32,48},{48,32},{64,80},{80,64},{96,112},{112,96},{2... | collective-permute-start | bytes 122888 | tf_op jit(solution)/shard_map/ppermute | solution.py:268
  105.8 6.4 %collective-permute-start.8 = (f32[80,128]{1,0:T(8,128)S(1)}, f32[80,128]{1,0:T(8,128)S(1)}, u32[]{:S(2)}, u32[]{:S(2)}) collective-permute-start(f32[80,128]{1,0:T(8,128)S(1)} %add_add_fusion), channel_id=1, source_target_pairs={{0,32},{16,48},{32,0},{48,16},{64,96},{80,112},{96,64},{112,80},{2... | collective-permute-start | bytes 122888 | tf_op jit(solution)/shard_map/ppermute | solution.py:268
  109.8 6.8 %collective-permute-start.9 = (f32[80,128]{1,0:T(8,128)S(1)}, f32[80,128]{1,0:T(8,128)S(1)}, u32[]{:S(2)}, u32[]{:S(2)}) collective-permute-start(f32[80,128]{1,0:T(8,128)S(1)} %add_add_fusion), channel_id=1, source_target_pairs={{0,48},{16,32},{32,16},{48,0},{64,112},{80,96},{96,80},{112,64},{2... | collective-permute-start | bytes 122888 | tf_op jit(solution)/shard_map/ppermute | solution.py:268
  117.6 21.1 %all-to-all-start.3 = ((bf16[32,80,128]{2,1,0:T(8,128)(2,1)}), bf16[32,80,128]{2,1,0:T(8,128)(2,1)S(1)}, u32[]{:S(2)}, u32[]{:S(2)}) async-start(bf16[32,80,128]{2,1,0:T(8,128)(2,1)} %broadcast_in_dim.3), calls=%async_computation.3 | async-start | bytes 1310720 | tf_op jit(solution)/shard_map/all_to_all | solution.py:298

commit v4 on v3

--- a/solution.py
+++ b/solution.py
@@ -126,100 +126,87 @@
     return jnp.concatenate([ref[pl.ds(start + rr, 32, stride=stride), :] for rr in range(4)], axis=0)
 
 
-def step_kernel(far_left, left, own, right, far_right, ker, w1, b1, w2, b2, w1b, w2b, fwd, inv, fwd_nat, inv_nat,
+def step_kernel(left, own, right, ker, w1, b1, w2, b2, w1b, w2b, fwd, inv, fwd_nat, inv_nat,
                 pred, out,
-                gl, go, gr, gl2, gr2, latf, xw, parts, cots, hid, placed, spec, m3, h3, rise1, slope2, s3, z3, gm):
-    for ref, wide in ((left, gl), (own, go), (right, gr), (far_left, gl2), (far_right, gr2)):
+                gl, go, gr, latf, xw, parts, cots, hid, placed, spec, m3, h3, rise1, s3, z3, gh, gm):
+    for ref, wide in ((left, gl), (own, go), (right, gr)):
         wide[...] = ref[...].reshape(wide.shape).astype(F4)
-    lat_from = ([(gl2, 4, 8)] + [(gl, 4 * j, 32) for j in range(4)] + [(go, 4 * j, 32) for j in range(4)]
-                + [(gr, 4 * j, 32) for j in range(4)] + [(gr2, 0, 8)])
+    lat_from = ([(gl, 4 * j, 16) for j in (1, 2, 3)] + [(go, 4 * j, 32) for j in range(4)]
+                + [(gr, 4 * j, 16) for j in (0, 1, 2)])
     for j, (ref, start, stride) in enumerate(lat_from):
         x = column(ref, start, stride)
         latf[j] = x
         xb = x.astype(BF)
         xw[0:128, j * CH : (j + 1) * CH] = xb
         xw[128:256, j * CH : (j + 1) * CH] = xb
-    cot_from = [(gl, 24), (gl, 28)] + [(go, 16 + 4 * j) for j in range(4)] + [(gr, 16), (gr, 20)]
-    for u, (ref, start) in enumerate(cot_from):
-        cots[u] = column(ref, start, 32)
-    ker_two = jnp.concatenate([ker[...], ker[...]], axis=0)
-    ker_spec = dot(fwd_nat[...], ker_two)
-    for j in range(0, 14, 2):
+    for u in range(4):
+        cots[u] = column(go, 16 + 4 * u, 32)
+    ker_spec = dot(fwd_nat[...], jnp.concatenate([ker[...], ker[...]], axis=0))
+    for j in range(0, 10, 2):
         lanes = slice(j * CH, (j + 2) * CH)
         s = dot(fwd[...], xw[:, lanes])
-        if 4 <= j < 10:
-            spec[:, (j - 4) * CH : (j - 2) * CH] = s
+        spec[:, lanes] = s
         for i in range(2):
-            part = s[:, i * CH : (i + 1) * CH]
-            parts[:, i * CH : (i + 1) * CH] = three_parts(cross(ker_spec, part))
+            parts[:, i * CH : (i + 1) * CH] = three_parts(cross(ker_spec, s[:, i * CH : (i + 1) * CH]))
         corr = dot(inv[...], parts[...])
         for i in range(2):
             mixed = (latf[j + i] + corr[:, i * CH : (i + 1) * CH]).astype(BF).astype(F4)
             latf[j + i] = mixed
             put_turned(m3, j + i, mixed, (-1, 0, 1))
-    for j in range(0, 12, 4):
+    for j in range(0, 8, 4):
         v = b1[...]
         for q in range(3):
             v = v + dot(m3[j + q : j + q + 4].reshape(512, 384), w1[q])
         g = jax.nn.sigmoid(v)
-        if j == 4:
-            rise1[...] = (g * (1.0 + v * (1.0 - g))).reshape(4, N_ROWS, CH)
+        rise1[j * 128 : j * 128 + 512, :] = g * (1.0 + v * (1.0 - g))
         vg = v * g
         for i in range(4):
             h = (latf[j + i + 1] + vg[i * 128 : i * 128 + 128]).astype(BF).astype(F4)
             hid[j + i] = h
             put_turned(h3, j + i, h, (-2, 0, 2))
-    for j in range(0, 8, 4):
-        v = b2[...]
-        for q in range(3):
-            v = v + dot(h3[j + 2 * q : j + 2 * q + 4].reshape(512, 384), w2[q])
-        g = jax.nn.sigmoid(v)
-        vg = v * g
-        rise = g * (1.0 + v * (1.0 - g))
-        for i in range(4):
-            u = j + i
-            slope2[u] = (cots[u] * rise[i * 128 : i * 128 + 128]).astype(BF)
-            if 2 <= u < 6:
-                p = hid[u + 2] + vg[i * 128 : i * 128 + 128]
-                for rr in range(4):
-                    placed[pl.ds((u - 2) * 4 + rr, 32, stride=16), :] = p[rr * 32 : rr * 32 + 32]
+    v = b2[...]
+    for q in range(3):
+        v = v + dot(h3[2 * q : 2 * q + 4].reshape(512, 384), w2[q])
+    g = jax.nn.sigmoid(v)
+    p = hid[2:6].reshape(512, CH) + v * g
+    for u in range(4):
+        for rr in range(4):
+            placed[pl.ds(u * 4 + rr, 32, stride=16), :] = p[u * 128 + rr * 32 : u * 128 + rr * 32 + 32]
     pred[...] = placed[...].astype(BF).reshape(PEERS, 16, CH)
-
-    own2 = slope2[2:6].reshape(512, CH)
+    cot = cots[...].reshape(512, CH)
+    own2 = (cot * (g * (1.0 + v * (1.0 - g)))).astype(BF)
+    own2_wide = own2.astype(F4)
+    for u in range(4):
+        put_turned(s3, u, own2_wide[u * 128 : u * 128 + 128], (2, 0, -2))
+    gh[...] = jnp.zeros(gh.shape, F4)
+    gh[256:768, :] = cot
     for q in range(3):
-        d = dot_t(h3[2 + 2 * q : 6 + 2 * q].reshape(512, 384), own2)
+        gh[q * 256 : q * 256 + 512, :] += dot(s3[...].reshape(512, 384), w2b[q])
+    slope1 = (gh[...] * rise1[...]).astype(BF)
+    slope1_wide = slope1.astype(F4)
+    for u in range(8):
+        put_turned(z3, u, slope1_wide[u * 128 : u * 128 + 128], (1, 0, -1))
+    gm[...] = jnp.zeros(gm.shape, F4)
+    gm[128:1152, :] = gh[...]
+    for q in range(3):
+        gm[q * 128 : q * 128 + 1024, :] += dot(z3[...].reshape(1024, 384), w1b[q])
+    for q in range(3):
+        d = dot_t(m3[q : q + 8].reshape(1024, 384), slope1)
+        e = dot_t(h3[2 * q : 2 * q + 4].reshape(512, 384), own2)
         for p in range(3):
-            out[1152 + (p * 3 + q) * 128 : 1280 + (p * 3 + q) * 128, :] = d[p * 128 : p * 128 + 128].astype(BF)
-    for u in range(8):
-        put_turned(s3, u, slope2[u].astype(F4), (2, 0, -2))
-    gh = cots[2:6].reshape(512, CH)
-    for q in range(3):
-        gh = gh + dot(s3[4 - 2 * q : 8 - 2 * q].reshape(512, 384), w2b[q])
-    slope1 = (gh * rise1[...].reshape(512, CH)).astype(BF)
-    slope1_wide = slope1.astype(F4)
-    for i in range(4):
-        put_turned(z3, i, slope1_wide[i * 128 : i * 128 + 128], (1, 0, -1))
-    gm[0] = jnp.zeros((N_ROWS, CH), F4)
-    gm[5] = jnp.zeros((N_ROWS, CH), F4)
-    gm[1:5] = gh.reshape(4, N_ROWS, CH)
-    for q in range(3):
-        gm[q : q + 4] += dot(z3[...].reshape(512, 384), w1b[q]).reshape(4, N_ROWS, CH)
-    for q in range(3):
-        d = dot_t(m3[4 + q : 8 + q].reshape(512, 384), slope1)
-        for p in range(3):
-            out[(p * 3 + q) * 128 : (p * 3 + q) * 128 + 128, :] = d[p * 128 : p * 128 + 128].astype(BF)
+            at = (p * 3 + q) * 128
+            out[at : at + 128, :] = d[p * 128 : p * 128 + 128].astype(BF)
+            out[1152 + at : 1280 + at, :] = e[p * 128 : p * 128 + 128].astype(BF)
     both = jnp.zeros((N_ROWS, CH), F4)
-    for j in range(0, 6, 2):
-        two = jnp.concatenate([gm[j], gm[j + 1]], axis=1).astype(BF)
+    for j in range(0, 10, 2):
+        two = jnp.concatenate([gm[(j + i) * 128 : (j + i) * 128 + 128, :] for i in range(2)], axis=1).astype(BF)
         s = dot(fwd[...], jnp.concatenate([two, two], axis=0))
         for i in range(2):
             both = both + cross(s[:, i * CH : (i + 1) * CH], spec[:, (j + i) * CH : (j + i + 1) * CH])
-    dk = dot(inv_nat[...], three_parts(both))
-    out[2304:2432, :] = dk.astype(BF)
-    db1 = jnp.sum(slope1_wide, axis=0, keepdims=True)
-    db2 = jnp.sum(own2.astype(F4), axis=0, keepdims=True)
+    out[2304:2432, :] = dot(inv_nat[...], three_parts(both)).astype(BF)
     rows = []
-    for b in (db1, db2):
+    for wide in (slope1_wide, own2_wide):
+        b = jnp.sum(wide, axis=0, keepdims=True)
         high = b.astype(BF).astype(F4)
         rows += [high, b - high]
     tail = jnp.concatenate(rows + [jnp.zeros((GRAD_ROWS - 2436, CH), F4)], axis=0)
@@ -248,17 +235,16 @@
     )(*args)
 
 
-def local_step(far_left, left, own, right, far_right, ker, w1, b1, w2, b2):
+def local_step(left, own, right, ker, w1, b1, w2, b2):
     fwd, inv, fwd_nat, inv_nat = (jnp.asarray(t, BF) for t in tables())
     w1q, w2q = (w.transpose(1, 0, 2, 3).reshape(3, 384, CH) for w in (w1, w2))
     w1b, w2b = (w.transpose(1, 0, 3, 2).reshape(3, 384, CH) for w in (w1, w2))
     outs = [((PEERS, 16, CH), BF), ((GRAD_ROWS, CH), BF)]
-    scratch = [((1024, CH), F4)] * 3 + [((256, CH), F4)] * 2 + [
-        ((14, 128, CH), F4), ((256, 14 * CH), BF), ((384, 2 * CH), BF), ((8, 128, CH), F4), ((12, 128, CH), F4),
-        ((512, CH), F4),
-        ((128, 6 * CH), F4), ((14, 128, 384), BF), ((12, 128, 384), BF), ((4, 128, CH), F4), ((8, 128, CH), BF),
-        ((8, 128, 384), BF), ((4, 128, 384), BF), ((6, 128, CH), F4)]
-    return call(step_kernel, outs, scratch, 3 << 30, 24, far_left, left, own, right, far_right, ker,
+    scratch = [((512, CH), F4), ((1024, CH), F4), ((512, CH), F4),
+               ((10, 128, CH), F4), ((256, 10 * CH), BF), ((384, 2 * CH), BF), ((4, 128, CH), F4), ((8, 128, CH), F4),
+               ((512, CH), F4), ((128, 10 * CH), F4), ((10, 128, 384), BF), ((8, 128, 384), BF), ((1024, CH), F4),
+               ((4, 128, 384), BF), ((8, 128, 384), BF), ((1024, CH), F4), ((1280, CH), F4)]
+    return call(step_kernel, outs, scratch, 3 << 30, 24, left, own, right, ker,
                 w1q, b1.reshape(1, CH), w2q, b2.reshape(1, CH), w1b, w2b, fwd, inv, fwd_nat, inv_nat)
 
 
@@ -276,7 +262,16 @@
 def per_device(latent, corr_kernel, w1, b1, w2, b2, cotangent):
     row_count, col_count, _ = latent.shape
     flip = flipped(lax.axis_index("zh"), lax.axis_index("c"))
-    (send,) = call(send_kernel, [((PEERS, 32, CH), BF)], [((1024, CH), F4), ((1024, CH), F4)], 1 << 20, 4, latent, cotangent)
+    block = pl.BlockSpec(latent.shape, lambda i: (0, 0, 0))
+    send = pl.pallas_call(
+        send_kernel,
+        grid=(1,),
+        out_shape=jax.ShapeDtypeStruct((PEERS, 32, CH), BF),
+        in_specs=[block, block],
+        out_specs=pl.BlockSpec((PEERS, 32, CH), lambda i: (0, 0, 0)),
+        scratch_shapes=[pltpu.VMEM((1024, CH), F4), pltpu.VMEM((1024, CH), F4)],
+        compiler_params=pltpu.CompilerParams(vmem_limit_bytes=60 << 20),
+    )(latent, cotangent)
     own = lax.all_to_all(send, ROWS_AXES, 0, 0, tiled=True)
     ring = device_ring()
     n = len(ring)
@@ -285,9 +280,8 @@
     def shifted(block, by):
         return lax.ppermute(block, everywhere, [(ring[i], ring[(i + by) % n]) for i in range(n)])
 
-    left, right = shifted(own, 1), shifted(own, -1)
-    far_left, far_right = shifted(own[:, 8:16], 2), shifted(own[:, 0:8], -2)
-    pred_send, grads = local_step(far_left, left, own, right, far_right, corr_kernel, w1, b1, w2, b2)
+    left, right = shifted(own[:, 0:16], 1), shifted(own[:, 0:16], -1)
+    pred_send, grads = local_step(left, own, right, corr_kernel, w1, b1, w2, b2)
     n_plane = lax.axis_size(PLANE_AXES)
     share = GRAD_ROWS // n_plane
     part = lax.all_to_all(grads.reshape(n_plane, share, CH), PLANE_AXES, 0, 0, tiled=True)

time: 140 us -> 132 us (0.943)
  starting transfers between devices: 50.9 us -> 45.4 us
  local copies, waits for them, and re-layouts: 4.41 us -> 2.62 us
    ppermute x4 -> x2, starting transfers between devices: 11.1 us -> 5.58 us  [shifted(): lax.ppermute(block, everywhere, [(ring[i], ring[(i + by) % n]) for i in r...]
    pallas_call x0 -> x1, Pallas kernels: none -> 1.97 us  [per_device(): pl.pallas_call(send_kernel, grid=(1,), out_shape=jax.ShapeDtypeStruct((PE...]
    unnamed x22 -> x18, local copies, waits for them, and re-layouts: 1.86 us -> 0.05 us
    ppermute x4 -> x2, waiting for transfers between devices: 4.13 us -> 2.85 us  [shifted(): lax.ppermute(block, everywhere, [(ring[i], ring[(i + by) % n]) for i in r...]
    pallas_call x3 -> x2, Pallas kernels: 6.68 us -> 5.89 us  [call(): pl.pallas_call(kernel, out_shape=[jax.ShapeDtypeStruct(s, d) for s, d in...]
  transfers between devices with their start and end apart: 12 -> 10, of which waited for: 5 -> 4; matrix products, arithmetic and copies ran while one was open for 1% -> 1% of each run, Pallas kernels for 0% -> 0%
where the time goes in v4:
time: 132 us; the launch traced here: 131 us
  blocking collectives  55.1 us (42%)
  starting transfers between devices  45.4 us (34%)
  waiting for transfers between devices  19.1 us (14%)
  Pallas kernels  7.87 us (6%)
  local copies, waits for them, and re-layouts  2.62 us (2%)
    all_to_all x1, blocking collectives, per_device(): own = lax.all_to_all(send, ROWS_AXES, 0, 0, tiled=True)  35 us
    ppermute x6, starting transfers between devices, moved(): lax.ppermute(x, DEPTH_AXES, [(flat[z], flat[target(z)]) for z in range(16)])  26.6 us
    all_to_all x1, blocking collectives, per_device(): lax.all_to_all(grads.reshape(n_plane, share, CH), PLANE_AXES, 0, 0, tiled...  20.1 us
    all_to_all x1, waiting for transfers between devices, per_device(): lax.all_to_all(jnp.broadcast_to(part, (n_plane, share, CH)), PLANE_AXES,...  11.6 us
    all_to_all x1, starting transfers between devices, per_device(): lax.all_to_all(jnp.broadcast_to(part, (n_plane, share, CH)), PLANE_AXES,...  8.06 us
    pallas_call x2, Pallas kernels, call(): pl.pallas_call(kernel, out_shape=[jax.ShapeDtypeStruct(s, d) for s, d in...  5.89 us
    ppermute x2, starting transfers between devices, shifted(): lax.ppermute(block, everywhere, [(ring[i], ring[(i + by) % n]) for i in r...  5.58 us
    all_to_all x1, starting transfers between devices, per_device(): pred_got = lax.all_to_all(pred_send, ROWS_AXES, 0, 0, tiled=True)  5.21 us
  transfers between devices with their start and end apart: 10, of which 4 were waited for; matrix products, arithmetic and copies ran while one was open for 1% of the time, Pallas kernels for 0%

profile of v4, /device:TPU:1, one launch (start us, length us, event | category | flops | bytes accessed | tf_op | source)
XLA Modules:
  0.0 131.4 jit_solution(17610204818764265252)
XLA Ops:
  0.6 0.0 copy-start.7
  0.6 2.0 %shard_map.154 = bf16[32,32,128]{2,1,0:T(8,128)(2,1)} custom-call(bf16[4,128,128]{2,1,0:T(8,128)(2,1)} %lat.1, bf16[4,128,128]{2,1,0:T(8,128)(2,1)} %cot.1), custom_call_target="tpu_custom_call" | custom-call | tf_op jit(solution)/shard_map/pallas_call | solution.py:266
  2.6 35.0 %all_to_all.20.own = bf16[32,32,128]{2,1,0:T(8,128)(2,1)S(1)} all-to-all(bf16[32,32,128]{2,1,0:T(8,128)(2,1)} %shard_map.154), channel_id=1, replica_groups=mesh['y'=4,'zl'=8,'x'=4,'zh'=2,'c'=2] {'y','zl'}, dimensions={0} | all-to-all | bytes 524288 | tf_op jit(solution)/shard_map/all_to_all | solution.py:275
  37.6 1.9 %collective-permute-start = (bf16[32,16,128]{2,1,0:T(8,128)(2,1)S(1)}, bf16[32,16,128]{2,1,0:T(8,128)(2,1)S(1)}, u32[]{:S(2)}, u32[]{:S(2)}) collective-permute-start(bf16[32,16,128]{2,1,0:T(8,128)(2,1)S(1)} %slice.13), channel_id=1, source_target_pairs={{112,240},{240,368},{368,496},{496,480},{480,352},{352,224},{224,9... | collective-permute-start | bytes 393224 | tf_op jit(solution)/shard_map/ppermute | solution.py:281
  39.5 3.7 %collective-permute-start.1 = (bf16[32,16,128]{2,1,0:T(8,128)(2,1)S(1)}, bf16[32,16,128]{2,1,0:T(8,128)(2,1)S(1)}, u32[]{:S(2)}, u32[]{:S(2)}) collective-permute-start(bf16[32,16,128]{2,1,0:T(8,128)(2,1)S(1)} %slice.13), channel_id=1, source_target_pairs={{112,15},{240,112},{368,240},{496,368},{480,496},{352,480},{224,35... | collective-permute-start | bytes 393224 | tf_op jit(solution)/shard_map/ppermute | solution.py:281
  43.2 0.0 copy-done.7
  43.2 0.0 copy-done.8
  43.3 0.0 copy-start
  43.3 0.0 copy-start.1
  43.3 0.0 copy-start.2
  43.3 0.0 copy-start.3
  43.3 0.0 copy-start.4
  43.3 0.0 copy-start.5
  43.3 0.0 copy-start.6
  43.4 0.2 copy.35
  43.6 0.2 copy.36
  43.8 0.0 collective-permute-done.left
  43.8 2.8 %collective-permute-done.1.right = bf16[32,16,128]{2,1,0:T(8,128)(2,1)S(1)} collective-permute-done((bf16[32,16,128]{2,1,0:T(8,128)(2,1)S(1)}, bf16[32,16,128]{2,1,0:T(8,128)(2,1)S(1)}, u32[]{:S(2)}, u32[]{:S(2)}) %collective-permute-start.1) | collective-permute-done | bytes 131104 | tf_op jit(solution)/shard_map/ppermute | solution.py:281
  46.7 0.0 copy-done
  46.7 0.0 copy-done.1
  46.7 0.0 copy-done.2
  46.7 0.0 copy-done.3
  46.7 4.8 %shard_map.155 = (bf16[32,16,128]{2,1,0:T(8,128)(2,1)}, bf16[2560,128]{1,0:T(8,128)(2,1)S(1)}) custom-call(bf16[32,16,128]{2,1,0:T(8,128)(2,1)S(1)} %collective-permute-done.left, bf16[32,32,128]{2,1,0:T(8,128)(2,1)S(1)} %all_to_all.20.own, bf16[32,16,128]{2,1,0:T(8,128)(2,1)S(1)} %collective-permute-done.1.right, bf16[128,128]{1,0:T(8,128)(2,1)S(1)} %copy-done, ...), custom_call_target="tpu_custom_call" | custom-call | flops 3221225472 | bytes 4194304 | tf_op jit(solution)/shard_map/pallas_call | solution.py:227
  51.5 20.1 %all_to_all.21 = bf16[32,80,128]{2,1,0:T(8,128)(2,1)S(1)} all-to-all(bf16[32,80,128]{2,1,0:T(8,128)(2,1)S(1)} %bitcast.27), channel_id=1, replica_groups=mesh['y'=4,'zl'=8,'x'=4,'zh'=2,'c'=2] {'y','x','c'}, dimensions={0} | all-to-all | bytes 1310720 | tf_op jit(solution)/shard_map/all_to_all | solution.py:287
  71.7 0.1 convert_reduce_fusion
  71.8 8.1 %collective-permute-start.2 = (f32[80,128]{1,0:T(8,128)S(1)}, f32[80,128]{1,0:T(8,128)S(1)}, u32[]{:S(2)}, u32[]{:S(2)}) collective-permute-start(f32[80,128]{1,0:T(8,128)S(1)} %convert_reduce_fusion), channel_id=1, source_target_pairs={{0,2},{16,18},{32,34},{48,50},{64,66},{80,82},{96,98},{112,114},{2... | collective-permute-start | bytes 122888 | tf_op jit(solution)/shard_map/ppermute | solution.py:254
  79.9 2.4 %collective-permute-start.3 = (f32[80,128]{1,0:T(8,128)S(1)}, f32[80,128]{1,0:T(8,128)S(1)}, u32[]{:S(2)}, u32[]{:S(2)}) collective-permute-start(f32[80,128]{1,0:T(8,128)S(1)} %convert_reduce_fusion), channel_id=1, source_target_pairs={{0,64},{16,80},{32,96},{48,112},{64,2},{80,18},{96,34},{112,50},{2... | collective-permute-start | bytes 122888 | tf_op jit(solution)/shard_map/ppermute | solution.py:254
  82.3 6.8 %collective-permute-start.4 = (f32[80,128]{1,0:T(8,128)S(1)}, f32[80,128]{1,0:T(8,128)S(1)}, u32[]{:S(2)}, u32[]{:S(2)}) collective-permute-start(f32[80,128]{1,0:T(8,128)S(1)} %convert_reduce_fusion), channel_id=1, source_target_pairs={{0,66},{16,82},{32,98},{48,114},{64,0},{80,16},{96,32},{112,48},{2... | collective-permute-start | bytes 122888 | tf_op jit(solution)/shard_map/ppermute | solution.py:254
  89.1 5.2 %all-to-all-start.2 = ((bf16[32,16,128]{2,1,0:T(8,128)(2,1)}), bf16[32,16,128]{2,1,0:T(8,128)(2,1)S(1)}, u32[]{:S(2)}, u32[]{:S(2)}) async-start(bf16[32,16,128]{2,1,0:T(8,128)(2,1)} %get-tuple-element.20), calls=%async_computation.2 | async-start | bytes 262144 | tf_op jit(solution)/shard_map/all_to_all | solution.py:289
  94.3 0.0 collective-permute-done.2
  94.3 0.0 collective-permute-done.3
  94.4 0.0 collective-permute-done.4
  94.4 3.1 %collective-permute-start.5 = (f32[80,128]{1,0:T(8,128)S(1)}, f32[80,128]{1,0:T(8,128)S(1)}, u32[]{:S(2)}, u32[]{:S(2)}) collective-permute-start(f32[80,128]{1,0:T(8,128)S(1)} %add_add_fusion), channel_id=1, source_target_pairs={{0,16},{16,0},{32,48},{48,32},{64,80},{80,64},{96,112},{112,96},{2... | collective-permute-start | bytes 122888 | tf_op jit(solution)/shard_map/ppermute | solution.py:254
  97.5 4.0 %collective-permute-start.6 = (f32[80,128]{1,0:T(8,128)S(1)}, f32[80,128]{1,0:T(8,128)S(1)}, u32[]{:S(2)}, u32[]{:S(2)}) collective-permute-start(f32[80,128]{1,0:T(8,128)S(1)} %add_add_fusion), channel_id=1, source_target_pairs={{0,32},{16,48},{32,0},{48,16},{64,96},{80,112},{96,64},{112,80},{2... | collective-permute-start | bytes 122888 | tf_op jit(solution)/shard_map/ppermute | solution.py:254
  101.5 2.1 %collective-permute-start.7 = (f32[80,128]{1,0:T(8,128)S(1)}, f32[80,128]{1,0:T(8,128)S(1)}, u32[]{:S(2)}, u32[]{:S(2)}) collective-permute-start(f32[80,128]{1,0:T(8,128)S(1)} %add_add_fusion), channel_id=1, source_target_pairs={{0,48},{16,32},{32,16},{48,0},{64,112},{80,96},{96,80},{112,64},{2... | collective-permute-start | bytes 122888 | tf_op jit(solution)/shard_map/ppermute | solution.py:254
  103.7 0.0 collective-permute-done.5
  103.7 0.4 collective-permute-done.6
  104.1 4.3 %collective-permute-done.7 = f32[80,128]{1,0:T(8,128)S(1)} collective-permute-done((f32[80,128]{1,0:T(8,128)S(1)}, f32[80,128]{1,0:T(8,128)S(1)}, u32[]{:S(2)}, u32[]{:S(2)}) %collective-permute-start.7) | collective-permute-done | bytes 40992 | tf_op jit(solution)/shard_map/ppermute | solution.py:254
  108.4 0.0 all-to-all-done.2
  108.4 0.9 broadcast_in_dim.3
  109.3 8.1 %all-to-all-start.3 = ((bf16[32,80,128]{2,1,0:T(8,128)(2,1)}), bf16[32,80,128]{2,1,0:T(8,128)(2,1)S(1)}, u32[]{:S(2)}, u32[]{:S(2)}) async-start(bf16[32,80,128]{2,1,0:T(8,128)(2,1)} %broadcast_in_dim.3), calls=%async_computation.3 | async-start | bytes 1310720 | tf_op jit(solution)/shard_map/all_to_all | solution.py:292
  117.5 0.1 pad_maximum_fusion
  117.6 0.1 copy.37
  117.7 0.1 copy.38
  117.9 0.1 rev.7
  117.9 0.8 copy.39
  118.7 11.6 %all-to-all-done.3.whole = bf16[32,80,128]{2,1,0:T(8,128)(2,1)S(1)} async-done(((bf16[32,80,128]{2,1,0:T(8,128)(2,1)}), bf16[32,80,128]{2,1,0:T(8,128)(2,1)S(1)}, u32[]{:S(2)}, u32[]{:S(2)}) %all-to-all-start.3) | async-done | bytes 655392 | tf_op jit(solution)/shard_map/all_to_all | solution.py:292
  130.3 1.1 shard_map.156
  (12 shorter events, 0.2 us)
Async XLA Ops:
  0.6 42.6 %copy-start.7 = (bf16[3,3,128,128]{3,2,1,0:T(8,128)(2,1)S(1)}, bf16[3,3,128,128]{3,2,1,0:T(8,128)(2,1)}, u32[]{:S(2)}) copy-start(bf16[3,3,128,128]{3,2,1,0:T(8,128)(2,1)} %param.13) | copy-start | bytes 884740
  2.6 40.6 %copy-start.8 = (bf16[3,3,128,128]{3,2,1,0:T(8,128)(2,1)S(1)}, bf16[3,3,128,128]{3,2,1,0:T(8,128)(2,1)}, u32[]{:S(2)}) copy-start(bf16[3,3,128,128]{3,2,1,0:T(8,128)(2,1)} %param.15) | copy-start | bytes 884740
  37.6 6.2 %collective-permute-start = (bf16[32,16,128]{2,1,0:T(8,128)(2,1)S(1)}, bf16[32,16,128]{2,1,0:T(8,128)(2,1)S(1)}, u32[]{:S(2)}, u32[]{:S(2)}) collective-permute-start(bf16[32,16,128]{2,1,0:T(8,128)(2,1)S(1)} %slice.13), channel_id=1, source_target_pairs={{112,240},{240,368},{368,496},{496,480},{480,352},{352,224},{224,9... | collective-permute-start | bytes 393224 | tf_op jit(solution)/shard_map/ppermute | solution.py:281
  39.5 7.1 %collective-permute-start.1 = (bf16[32,16,128]{2,1,0:T(8,128)(2,1)S(1)}, bf16[32,16,128]{2,1,0:T(8,128)(2,1)S(1)}, u32[]{:S(2)}, u32[]{:S(2)}) collective-permute-start(bf16[32,16,128]{2,1,0:T(8,128)(2,1)S(1)} %slice.13), channel_id=1, source_target_pairs={{112,15},{240,112},{368,240},{496,368},{480,496},{352,480},{224,35... | collective-permute-start | bytes 393224 | tf_op jit(solution)/shard_map/ppermute | solution.py:281
  43.3 3.4 %copy-start = (bf16[128,128]{1,0:T(8,128)(2,1)S(1)}, bf16[128,128]{1,0:T(8,128)(2,1)}, u32[]{:S(2)}) copy-start(bf16[128,128]{1,0:T(8,128)(2,1)} %ker.1) | copy-start | bytes 98308
  43.3 3.4 %copy-start.1 = (f32[128]{0:T(128)S(1)}, f32[128]{0:T(128)}, u32[]{:S(2)}) copy-start(f32[128]{0:T(128)} %param.14) | copy-start | bytes 1540
  43.3 3.4 %copy-start.2 = (f32[128]{0:T(128)S(1)}, f32[128]{0:T(128)}, u32[]{:S(2)}) copy-start(f32[128]{0:T(128)} %param.16) | copy-start | bytes 1540
  43.3 3.4 %copy-start.3 = (bf16[128,384]{1,0:T(8,128)(2,1)S(1)}, bf16[128,384]{1,0:T(8,128)(2,1)}, u32[]{:S(2)}) copy-start(bf16[128,384]{1,0:T(8,128)(2,1)} %constant.17.clone.inv) | copy-start | bytes 294916
  43.3 3.4 %copy-start.4 = (bf16[128,384]{1,0:T(8,128)(2,1)S(1)}, bf16[128,384]{1,0:T(8,128)(2,1)}, u32[]{:S(2)}) copy-start(bf16[128,384]{1,0:T(8,128)(2,1)} %constant.19.clone.inv_nat) | copy-start | bytes 294916
  43.3 3.4 %copy-start.5 = (bf16[128,256]{1,0:T(8,128)(2,1)S(1)}, bf16[128,256]{1,0:T(8,128)(2,1)}, u32[]{:S(2)}) copy-start(bf16[128,256]{1,0:T(8,128)(2,1)} %constant.16.clone.fwd) | copy-start | bytes 196612
  43.3 3.4 %copy-start.6 = (bf16[128,256]{1,0:T(8,128)(2,1)S(1)}, bf16[128,256]{1,0:T(8,128)(2,1)}, u32[]{:S(2)}) copy-start(bf16[128,256]{1,0:T(8,128)(2,1)} %constant.18.clone.fwd_nat) | copy-start | bytes 196612
  71.8 22.6 %collective-permute-start.2 = (f32[80,128]{1,0:T(8,128)S(1)}, f32[80,128]{1,0:T(8,128)S(1)}, u32[]{:S(2)}, u32[]{:S(2)}) collective-permute-start(f32[80,128]{1,0:T(8,128)S(1)} %convert_reduce_fusion), channel_id=1, source_target_pairs={{0,2},{16,18},{32,34},{48,50},{64,66},{80,82},{96,98},{112,114},{2... | collective-permute-start | bytes 122888 | tf_op jit(solution)/shard_map/ppermute | solution.py:254
  79.9 14.4 %collective-permute-start.3 = (f32[80,128]{1,0:T(8,128)S(1)}, f32[80,128]{1,0:T(8,128)S(1)}, u32[]{:S(2)}, u32[]{:S(2)}) collective-permute-start(f32[80,128]{1,0:T(8,128)S(1)} %convert_reduce_fusion), channel_id=1, source_target_pairs={{0,64},{16,80},{32,96},{48,112},{64,2},{80,18},{96,34},{112,50},{2... | collective-permute-start | bytes 122888 | tf_op jit(solution)/shard_map/ppermute | solution.py:254
  82.3 12.0 %collective-permute-start.4 = (f32[80,128]{1,0:T(8,128)S(1)}, f32[80,128]{1,0:T(8,128)S(1)}, u32[]{:S(2)}, u32[]{:S(2)}) collective-permute-start(f32[80,128]{1,0:T(8,128)S(1)} %convert_reduce_fusion), channel_id=1, source_target_pairs={{0,66},{16,82},{32,98},{48,114},{64,0},{80,16},{96,32},{112,48},{2... | collective-permute-start | bytes 122888 | tf_op jit(solution)/shard_map/ppermute | solution.py:254
  89.1 19.3 %all-to-all-start.2 = ((bf16[32,16,128]{2,1,0:T(8,128)(2,1)}), bf16[32,16,128]{2,1,0:T(8,128)(2,1)S(1)}, u32[]{:S(2)}, u32[]{:S(2)}) async-start(bf16[32,16,128]{2,1,0:T(8,128)(2,1)} %get-tuple-element.20), calls=%async_computation.2 | async-start | bytes 262144 | tf_op jit(solution)/shard_map/all_to_all | solution.py:289
  94.4 9.3 %collective-permute-start.5 = (f32[80,128]{1,0:T(8,128)S(1)}, f32[80,128]{1,0:T(8,128)S(1)}, u32[]{:S(2)}, u32[]{:S(2)}) collective-permute-start(f32[80,128]{1,0:T(8,128)S(1)} %add_add_fusion), channel_id=1, source_target_pairs={{0,16},{16,0},{32,48},{48,32},{64,80},{80,64},{96,112},{112,96},{2... | collective-permute-start | bytes 122888 | tf_op jit(solution)/shard_map/ppermute | solution.py:254
  97.5 6.6 %collective-permute-start.6 = (f32[80,128]{1,0:T(8,128)S(1)}, f32[80,128]{1,0:T(8,128)S(1)}, u32[]{:S(2)}, u32[]{:S(2)}) collective-permute-start(f32[80,128]{1,0:T(8,128)S(1)} %add_add_fusion), channel_id=1, source_target_pairs={{0,32},{16,48},{32,0},{48,16},{64,96},{80,112},{96,64},{112,80},{2... | collective-permute-start | bytes 122888 | tf_op jit(solution)/shard_map/ppermute | solution.py:254
  101.5 6.8 %collective-permute-start.7 = (f32[80,128]{1,0:T(8,128)S(1)}, f32[80,128]{1,0:T(8,128)S(1)}, u32[]{:S(2)}, u32[]{:S(2)}) collective-permute-start(f32[80,128]{1,0:T(8,128)S(1)} %add_add_fusion), channel_id=1, source_target_pairs={{0,48},{16,32},{32,16},{48,0},{64,112},{80,96},{96,80},{112,64},{2... | collective-permute-start | bytes 122888 | tf_op jit(solution)/shard_map/ppermute | solution.py:254
  109.3 21.0 %all-to-all-start.3 = ((bf16[32,80,128]{2,1,0:T(8,128)(2,1)}), bf16[32,80,128]{2,1,0:T(8,128)(2,1)S(1)}, u32[]{:S(2)}, u32[]{:S(2)}) async-start(bf16[32,80,128]{2,1,0:T(8,128)(2,1)} %broadcast_in_dim.3), calls=%async_computation.3 | async-start | bytes 1310720 | tf_op jit(solution)/shard_map/all_to_all | solution.py:292

commit v5 on v4

--- a/solution.py
+++ b/solution.py
@@ -6,11 +6,11 @@
 from jax.experimental.pallas import tpu as pltpu
 from jax.sharding import Mesh, PartitionSpec as P
 
-ROWS_AXES = ("y", "zl")
+ROWS_AXES = ("y", "zb", "za")
 COLS_AXES = ("x", "zh", "c")
-PLANE_AXES = ("y", "x", "c")
-DEPTH_AXES = ("zl", "zh")
-SIZES = {"y": 4, "zl": 8, "x": 4, "zh": 2, "c": 2}
+PLANE_AXES = ("y", "za", "x", "c")
+DEPTH_AXES = ("zb", "zh")
+SIZES = {"y": 4, "zb": 4, "za": 2, "x": 4, "zh": 2, "c": 2}
 N_ROWS = 128
 CH = 128
 PEERS = 32
@@ -109,7 +109,7 @@
 
 
 def send_kernel(lat, cot, out, wide, packed):
-    y, zl, zh, c = (lax.axis_index(a) for a in ("y", "zl", "zh", "c"))
+    zh, c = lax.axis_index("zh"), lax.axis_index("c")
     flip = flipped(zh, c)
     for t, ref in enumerate((lat, cot)):
         wide[t * 512 : t * 512 + 512, :] = ref[...].reshape(512, CH).astype(F4)
@@ -214,11 +214,10 @@
 
 
 def finish_kernel(whole, dw1, dw2, dk, db1, db2):
-    rows = whole[...].reshape(GRAD_ROWS, CH)
-    dw1[...] = rows[0:1152].astype(F4)
-    dw2[...] = rows[1152:2304].astype(F4)
-    dk[...] = rows[2304:2432].astype(F4)
-    tail = rows[2432:2448].astype(F4)
+    dw1[...] = whole[0:1152].astype(F4)
+    dw2[...] = whole[1152:2304].astype(F4)
+    dk[...] = whole[2304:2432].astype(F4)
+    tail = whole[2432:2448].astype(F4)
     db1[...] = tail[0:1] + tail[1:2]
     db2[...] = tail[2:3] + tail[3:4]
 
@@ -248,15 +247,18 @@
                 w1q, b1.reshape(1, CH), w2q, b2.reshape(1, CH), w1b, w2b, fwd, inv, fwd_nat, inv_nat)
 
 
-def depth_sum(part):
-    def moved(x, target):
-        flat = [(z % 8) * 2 + z // 8 for z in range(16)]
-        return lax.ppermute(x, DEPTH_AXES, [(flat[z], flat[target(z)]) for z in range(16)])
-
-    opposite, ahead, behind = (moved(part, lambda z, d=d: (z + d) % 16) for d in (8, 4, 12))
-    part = (part + opposite) + (ahead + behind)
-    one, two, three = (moved(part, lambda z, d=d: z ^ d) for d in (1, 2, 3))
-    return (part + one) + (two + three)
+def sum_kernel(got, out):
+    total = got[0].astype(F4)
+    for i in range(1, got.shape[0]):
+        total = total + got[i].astype(F4)
+    total = total.astype(BF)
+    for i in range(out.shape[0]):
+        out[i] = total
+
+
+def summed(got, copies):
+    (out,) = call(sum_kernel, [((copies,) + got.shape[1:], BF)], [], 1 << 20, 8, got)
+    return out
 
 
 def per_device(latent, corr_kernel, w1, b1, w2, b2, cotangent):
@@ -282,14 +284,13 @@
 
     left, right = shifted(own[:, 0:16], 1), shifted(own[:, 0:16], -1)
     pred_send, grads = local_step(left, own, right, corr_kernel, w1, b1, w2, b2)
-    n_plane = lax.axis_size(PLANE_AXES)
-    share = GRAD_ROWS // n_plane
-    part = lax.all_to_all(grads.reshape(n_plane, share, CH), PLANE_AXES, 0, 0, tiled=True)
+    n_plane, n_depth = lax.axis_size(PLANE_AXES), lax.axis_size(DEPTH_AXES)
+    part = lax.all_to_all(grads.reshape(n_plane, GRAD_ROWS // n_plane, CH), PLANE_AXES, 0, 0, tiled=True)
+    part = lax.all_to_all(summed(part, n_depth), DEPTH_AXES, 0, 0, tiled=True)
     part, pred_send = lax.optimization_barrier((part, pred_send))
     pred_got = lax.all_to_all(pred_send, ROWS_AXES, 0, 0, tiled=True)
-    part = depth_sum(jnp.sum(part.astype(F4), axis=0)).astype(BF)
-    part, pred_got = lax.optimization_barrier((part, pred_got))
-    whole = lax.all_to_all(jnp.broadcast_to(part, (n_plane, share, CH)), PLANE_AXES, 0, 0, tiled=True)
+    part, pred_got = lax.optimization_barrier((summed(part, n_plane), pred_got))
+    whole = lax.all_to_all(part, PLANE_AXES, 0, 0, tiled=True).reshape(GRAD_ROWS, CH)
 
     got = pred_got.reshape(4, 8, 4, row_count, CH)
     even, odd = got[:, 0::2], got[::-1, 1::2]

time: 132 us -> 133 us (level)
  starting transfers between devices: 45.4 us -> 18.6 us
  blocking collectives: 55.1 us -> 75.2 us
  waiting for transfers between devices: 19.1 us -> 25.5 us
    ppermute x6 -> x0, starting transfers between devices: 26.6 us -> none  [moved(): lax.ppermute(x, DEPTH_AXES, [(flat[z], flat[target(z)]) for z in range(16)])]
    all_to_all x1 -> x2, blocking collectives: 20.1 us -> 40.2 us  [the longest x1 21.7 us: per_device(): lax.all_to_all(grads.reshape(n_plane, GRAD_ROWS // n_plane, CH), PLANE_AX...]
    all_to_all x1, waiting for transfers between devices: 0.01 us -> 10.9 us  [per_device(): pred_got = lax.all_to_all(pred_send, ROWS_AXES, 0, 0, tiled=True)]
    ppermute x6 -> x0, waiting for transfers between devices: 4.68 us -> none  [moved(): lax.ppermute(x, DEPTH_AXES, [(flat[z], flat[target(z)]) for z in range(16)])]
    unnamed x18, local copies, waits for them, and re-layouts: 0.05 us -> 1.59 us
    pallas_call x2 -> x4, Pallas kernels: 5.89 us -> 6.9 us  [call(): pl.pallas_call(kernel, out_shape=[jax.ShapeDtypeStruct(s, d) for s, d in...]
  transfers between devices with their start and end apart: 10 -> 4, of which waited for: 4 -> 3; matrix products, arithmetic and copies ran while one was open for 1% -> 1% of each run, Pallas kernels for 0% -> 1%
where the time goes in v5:
time: 133 us; the launch traced here: 132 us
  blocking collectives  75.2 us (57%)
  waiting for transfers between devices  25.5 us (19%)
  starting transfers between devices  18.6 us (14%)
  Pallas kernels  8.83 us (7%)
  local copies, waits for them, and re-layouts  3.2 us (2%)
    all_to_all x1, blocking collectives, per_device(): own = lax.all_to_all(send, ROWS_AXES, 0, 0, tiled=True)  35 us
    all_to_all x1, blocking collectives, per_device(): lax.all_to_all(grads.reshape(n_plane, GRAD_ROWS // n_plane, CH), PLANE_AX...  21.7 us
    all_to_all x1, blocking collectives, per_device(): part = lax.all_to_all(summed(part, n_depth), DEPTH_AXES, 0, 0, tiled=True)  18.6 us
    all_to_all x1, waiting for transfers between devices, per_device(): lax.all_to_all(part, PLANE_AXES, 0, 0, tiled=True).reshape(GRAD_ROWS, CH)  12.7 us
    all_to_all x1, waiting for transfers between devices, per_device(): pred_got = lax.all_to_all(pred_send, ROWS_AXES, 0, 0, tiled=True)  10.9 us
    all_to_all x1, starting transfers between devices, per_device(): lax.all_to_all(part, PLANE_AXES, 0, 0, tiled=True).reshape(GRAD_ROWS, CH)  7.72 us
    pallas_call x4, Pallas kernels, call(): pl.pallas_call(kernel, out_shape=[jax.ShapeDtypeStruct(s, d) for s, d in...  6.9 us
    ppermute x2, starting transfers between devices, shifted(): lax.ppermute(block, everywhere, [(ring[i], ring[(i + by) % n]) for i in r...  5.58 us
  transfers between devices with their start and end apart: 4, of which 3 were waited for; matrix products, arithmetic and copies ran while one was open for 1% of the time, Pallas kernels for 1%

profile of v5, /device:TPU:1, one launch (start us, length us, event | category | flops | bytes accessed | tf_op | source)
XLA Modules:
  0.0 132.3 jit_solution(14660378859016259950)
XLA Ops:
  0.6 1.9 %shard_map.154 = bf16[32,32,128]{2,1,0:T(8,128)(2,1)} custom-call(bf16[4,128,128]{2,1,0:T(8,128)(2,1)} %lat.1, bf16[4,128,128]{2,1,0:T(8,128)(2,1)} %cot.1), custom_call_target="tpu_custom_call" | custom-call | tf_op jit(solution)/shard_map/pallas_call | solution.py:268
  2.6 0.0 copy-start.7
  2.6 35.0 %all_to_all.25.own = bf16[32,32,128]{2,1,0:T(8,128)(2,1)S(1)} all-to-all(bf16[32,32,128]{2,1,0:T(8,128)(2,1)} %shard_map.154), channel_id=1, replica_groups=mesh['y'=4,'zb'=4,'za'=2,'x'=4,'zh'=2,'c'=2] {'y','zb','za'}, dimensions={0} | all-to-all | bytes 524288 | tf_op jit(solution)/shard_map/all_to_all | solution.py:277
  37.5 1.9 %collective-permute-start = (bf16[32,16,128]{2,1,0:T(8,128)(2,1)S(1)}, bf16[32,16,128]{2,1,0:T(8,128)(2,1)S(1)}, u32[]{:S(2)}, u32[]{:S(2)}) collective-permute-start(bf16[32,16,128]{2,1,0:T(8,128)(2,1)S(1)} %slice.13), channel_id=1, source_target_pairs={{112,240},{240,368},{368,496},{496,480},{480,352},{352,224},{224,9... | collective-permute-start | bytes 393224 | tf_op jit(solution)/shard_map/ppermute | solution.py:283
  39.5 3.7 %collective-permute-start.1 = (bf16[32,16,128]{2,1,0:T(8,128)(2,1)S(1)}, bf16[32,16,128]{2,1,0:T(8,128)(2,1)S(1)}, u32[]{:S(2)}, u32[]{:S(2)}) collective-permute-start(bf16[32,16,128]{2,1,0:T(8,128)(2,1)S(1)} %slice.13), channel_id=1, source_target_pairs={{112,15},{240,112},{368,240},{496,368},{480,496},{352,480},{224,35... | collective-permute-start | bytes 393224 | tf_op jit(solution)/shard_map/ppermute | solution.py:283
  43.1 0.0 copy-done.7
  43.1 0.0 copy-start.8
  43.2 0.9 copy-done.8
  44.1 0.2 copy.35
  44.4 0.0 copy-start
  44.4 0.0 copy-start.3
  44.4 0.0 copy-start.4
  44.4 0.0 copy-start.5
  44.4 0.0 copy-start.6
  44.4 0.2 copy.36
  44.6 0.0 collective-permute-done.left
  44.6 2.0 %collective-permute-done.1.right = bf16[32,16,128]{2,1,0:T(8,128)(2,1)S(1)} collective-permute-done((bf16[32,16,128]{2,1,0:T(8,128)(2,1)S(1)}, bf16[32,16,128]{2,1,0:T(8,128)(2,1)S(1)}, u32[]{:S(2)}, u32[]{:S(2)}) %collective-permute-start.1) | collective-permute-done | bytes 131104 | tf_op jit(solution)/shard_map/ppermute | solution.py:283
  46.6 0.0 copy-start.1
  46.6 0.0 copy-start.2
  46.6 0.0 copy-done
  46.6 0.0 copy-done.3
  46.6 0.0 copy-done.4
  46.6 0.0 copy-done.5
  46.6 0.0 copy-done.6
  46.6 0.6 copy-done.1
  47.3 0.0 copy-done.2
  47.3 4.8 %shard_map.155 = (bf16[32,16,128]{2,1,0:T(8,128)(2,1)}, bf16[2560,128]{1,0:T(8,128)(2,1)S(1)}) custom-call(bf16[32,16,128]{2,1,0:T(8,128)(2,1)S(1)} %collective-permute-done.left, bf16[32,32,128]{2,1,0:T(8,128)(2,1)S(1)} %all_to_all.25.own, bf16[32,16,128]{2,1,0:T(8,128)(2,1)S(1)} %collective-permute-done.1.right, bf16[128,128]{1,0:T(8,128)(2,1)S(1)} %copy-done, ...), custom_call_target="tpu_custom_call" | custom-call | flops 3221225472 | bytes 4194304 | tf_op jit(solution)/shard_map/pallas_call | solution.py:226
  52.1 21.7 %all_to_all.26.got = bf16[64,40,128]{2,1,0:T(8,128)(2,1)S(1)} all-to-all(bf16[64,40,128]{2,1,0:T(8,128)(2,1)S(1)} %bitcast.29), channel_id=1, replica_groups=mesh['y'=4,'zb'=4,'za'=2,'x'=4,'zh'=2,'c'=2] {'y','za','x','c'}, dimensions={0} | all-to-all | bytes 1310720 | tf_op jit(solution)/shard_map/all_to_all | solution.py:288
  73.8 0.1 shard_map.156
  73.9 18.6 %all_to_all.27.got = bf16[8,40,128]{2,1,0:T(8,128)(2,1)S(1)} all-to-all(bf16[8,40,128]{2,1,0:T(8,128)(2,1)S(1)} %shard_map.156), channel_id=1, replica_groups=mesh['y'=4,'zb'=4,'za'=2,'x'=4,'zh'=2,'c'=2] {'zb','zh'}, dimensions={0} | all-to-all | bytes 163840 | tf_op jit(solution)/shard_map/all_to_all | solution.py:289
  92.4 5.3 %all-to-all-start.3 = ((bf16[32,16,128]{2,1,0:T(8,128)(2,1)}), bf16[32,16,128]{2,1,0:T(8,128)(2,1)S(1)}, u32[]{:S(2)}, u32[]{:S(2)}) async-start(bf16[32,16,128]{2,1,0:T(8,128)(2,1)} %get-tuple-element.20), calls=%async_computation.3 | async-start | bytes 262144 | tf_op jit(solution)/shard_map/all_to_all | solution.py:291
  97.8 0.9 shard_map.157
  98.7 10.9 %all-to-all-done.3 = bf16[32,16,128]{2,1,0:T(8,128)(2,1)S(1)} async-done(((bf16[32,16,128]{2,1,0:T(8,128)(2,1)}), bf16[32,16,128]{2,1,0:T(8,128)(2,1)S(1)}, u32[]{:S(2)}, u32[]{:S(2)}) %all-to-all-start.3) | async-done | bytes 131104 | tf_op jit(solution)/shard_map/all_to_all | solution.py:291
  109.6 7.7 %all-to-all-start.4 = ((bf16[64,40,128]{2,1,0:T(8,128)(2,1)}), bf16[64,40,128]{2,1,0:T(8,128)(2,1)S(1)}, u32[]{:S(2)}, u32[]{:S(2)}) async-start(bf16[64,40,128]{2,1,0:T(8,128)(2,1)} %shard_map.157), calls=%async_computation.4 | async-start | bytes 1310720 | tf_op jit(solution)/shard_map/all_to_all | solution.py:293
  117.4 0.1 pad_maximum_fusion
  117.5 0.1 copy.37
  117.6 0.1 copy.38
  117.7 0.1 rev.7
  117.8 0.8 copy.39
  118.6 12.7 %all-to-all-done.4 = bf16[64,40,128]{2,1,0:T(8,128)(2,1)S(1)} async-done(((bf16[64,40,128]{2,1,0:T(8,128)(2,1)}), bf16[64,40,128]{2,1,0:T(8,128)(2,1)S(1)}, u32[]{:S(2)}, u32[]{:S(2)}) %all-to-all-start.4) | async-done | bytes 655392 | tf_op jit(solution)/shard_map/all_to_all | solution.py:293
  131.2 1.1 shard_map.158
  (6 shorter events, 0.1 us)
Async XLA Ops:
  2.6 40.6 %copy-start.7 = (bf16[3,3,128,128]{3,2,1,0:T(8,128)(2,1)S(1)}, bf16[3,3,128,128]{3,2,1,0:T(8,128)(2,1)}, u32[]{:S(2)}) copy-start(bf16[3,3,128,128]{3,2,1,0:T(8,128)(2,1)} %param.13) | copy-start | bytes 884740
  37.5 7.1 %collective-permute-start = (bf16[32,16,128]{2,1,0:T(8,128)(2,1)S(1)}, bf16[32,16,128]{2,1,0:T(8,128)(2,1)S(1)}, u32[]{:S(2)}, u32[]{:S(2)}) collective-permute-start(bf16[32,16,128]{2,1,0:T(8,128)(2,1)S(1)} %slice.13), channel_id=1, source_target_pairs={{112,240},{240,368},{368,496},{496,480},{480,352},{352,224},{224,9... | collective-permute-start | bytes 393224 | tf_op jit(solution)/shard_map/ppermute | solution.py:283
  39.5 7.1 %collective-permute-start.1 = (bf16[32,16,128]{2,1,0:T(8,128)(2,1)S(1)}, bf16[32,16,128]{2,1,0:T(8,128)(2,1)S(1)}, u32[]{:S(2)}, u32[]{:S(2)}) collective-permute-start(bf16[32,16,128]{2,1,0:T(8,128)(2,1)S(1)} %slice.13), channel_id=1, source_target_pairs={{112,15},{240,112},{368,240},{496,368},{480,496},{352,480},{224,35... | collective-permute-start | bytes 393224 | tf_op jit(solution)/shard_map/ppermute | solution.py:283
  43.1 1.0 copy-start.8
  44.4 2.3 %copy-start = (bf16[128,128]{1,0:T(8,128)(2,1)S(1)}, bf16[128,128]{1,0:T(8,128)(2,1)}, u32[]{:S(2)}) copy-start(bf16[128,128]{1,0:T(8,128)(2,1)} %ker.1) | copy-start | bytes 98308
  44.4 2.2 %copy-start.3 = (bf16[128,384]{1,0:T(8,128)(2,1)S(1)}, bf16[128,384]{1,0:T(8,128)(2,1)}, u32[]{:S(2)}) copy-start(bf16[128,384]{1,0:T(8,128)(2,1)} %constant.15.clone.inv) | copy-start | bytes 294916
  44.4 2.2 %copy-start.4 = (bf16[128,384]{1,0:T(8,128)(2,1)S(1)}, bf16[128,384]{1,0:T(8,128)(2,1)}, u32[]{:S(2)}) copy-start(bf16[128,384]{1,0:T(8,128)(2,1)} %constant.17.clone.inv_nat) | copy-start | bytes 294916
  44.4 2.2 %copy-start.5 = (bf16[128,256]{1,0:T(8,128)(2,1)S(1)}, bf16[128,256]{1,0:T(8,128)(2,1)}, u32[]{:S(2)}) copy-start(bf16[128,256]{1,0:T(8,128)(2,1)} %constant.14.clone.fwd) | copy-start | bytes 196612
  44.4 2.2 %copy-start.6 = (bf16[128,256]{1,0:T(8,128)(2,1)S(1)}, bf16[128,256]{1,0:T(8,128)(2,1)}, u32[]{:S(2)}) copy-start(bf16[128,256]{1,0:T(8,128)(2,1)} %constant.16.clone.fwd_nat) | copy-start | bytes 196612
  46.6 0.7 copy-start.1
  46.6 0.7 copy-start.2
  92.4 17.1 %all-to-all-start.3 = ((bf16[32,16,128]{2,1,0:T(8,128)(2,1)}), bf16[32,16,128]{2,1,0:T(8,128)(2,1)S(1)}, u32[]{:S(2)}, u32[]{:S(2)}) async-start(bf16[32,16,128]{2,1,0:T(8,128)(2,1)} %get-tuple-element.20), calls=%async_computation.3 | async-start | bytes 262144 | tf_op jit(solution)/shard_map/all_to_all | solution.py:291
  109.6 21.7 %all-to-all-start.4 = ((bf16[64,40,128]{2,1,0:T(8,128)(2,1)}), bf16[64,40,128]{2,1,0:T(8,128)(2,1)S(1)}, u32[]{:S(2)}, u32[]{:S(2)}) async-start(bf16[64,40,128]{2,1,0:T(8,128)(2,1)} %shard_map.157), calls=%async_computation.4 | async-start | bytes 1310720 | tf_op jit(solution)/shard_map/all_to_all | solution.py:293

commit v6 on v5

--- a/solution.py
+++ b/solution.py
@@ -8,7 +8,8 @@
 
 ROWS_AXES = ("y", "zb", "za")
 COLS_AXES = ("x", "zh", "c")
-PLANE_AXES = ("y", "za", "x", "c")
+NEAR_AXES = ("y", "za")
+PLANE_AXES = ("c", "x", "y", "za")
 DEPTH_AXES = ("zb", "zh")
 SIZES = {"y": 4, "zb": 4, "za": 2, "x": 4, "zh": 2, "c": 2}
 N_ROWS = 128
@@ -127,8 +128,8 @@
 
 
 def step_kernel(left, own, right, ker, w1, b1, w2, b2, w1b, w2b, fwd, inv, fwd_nat, inv_nat,
-                pred, out,
-                gl, go, gr, latf, xw, parts, cots, hid, placed, spec, m3, h3, rise1, s3, z3, gh, gm):
+                pred, keep, give,
+                gl, go, gr, latf, xw, parts, cots, hid, placed, spec, m3, h3, rise1, s3, z3, gh, gm, halves):
     for ref, wide in ((left, gl), (own, go), (right, gr)):
         wide[...] = ref[...].reshape(wide.shape).astype(F4)
     lat_from = ([(gl, 4 * j, 16) for j in (1, 2, 3)] + [(go, 4 * j, 32) for j in range(4)]
@@ -195,28 +196,31 @@
         e = dot_t(h3[2 * q : 2 * q + 4].reshape(512, 384), own2)
         for p in range(3):
             at = (p * 3 + q) * 128
-            out[at : at + 128, :] = d[p * 128 : p * 128 + 128].astype(BF)
-            out[1152 + at : 1280 + at, :] = e[p * 128 : p * 128 + 128].astype(BF)
+            halves[0, at : at + 128, :] = d[p * 128 : p * 128 + 128].astype(BF)
+            halves[1, at : at + 128, :] = e[p * 128 : p * 128 + 128].astype(BF)
     both = jnp.zeros((N_ROWS, CH), F4)
     for j in range(0, 10, 2):
         two = jnp.concatenate([gm[(j + i) * 128 : (j + i) * 128 + 128, :] for i in range(2)], axis=1).astype(BF)
         s = dot(fwd[...], jnp.concatenate([two, two], axis=0))
         for i in range(2):
             both = both + cross(s[:, i * CH : (i + 1) * CH], spec[:, (j + i) * CH : (j + i + 1) * CH])
-    out[2304:2432, :] = dot(inv_nat[...], three_parts(both)).astype(BF)
+    halves[0, 1152:1280, :] = dot(inv_nat[...], three_parts(both)).astype(BF)
     rows = []
     for wide in (slope1_wide, own2_wide):
         b = jnp.sum(wide, axis=0, keepdims=True)
         high = b.astype(BF).astype(F4)
         rows += [high, b - high]
-    tail = jnp.concatenate(rows + [jnp.zeros((GRAD_ROWS - 2436, CH), F4)], axis=0)
-    out[2432:GRAD_ROWS, :] = tail.astype(BF)
+    tail = jnp.concatenate(rows + [jnp.zeros((124, CH), F4)], axis=0)
+    halves[1, 1152:1280, :] = tail.astype(BF)
+    core = lax.axis_index("c")
+    keep[...] = halves[core]
+    give[...] = halves[1 - core]
 
 
 def finish_kernel(whole, dw1, dw2, dk, db1, db2):
     dw1[...] = whole[0:1152].astype(F4)
-    dw2[...] = whole[1152:2304].astype(F4)
-    dk[...] = whole[2304:2432].astype(F4)
+    dk[...] = whole[1152:1280].astype(F4)
+    dw2[...] = whole[1280:2432].astype(F4)
     tail = whole[2432:2448].astype(F4)
     db1[...] = tail[0:1] + tail[1:2]
     db2[...] = tail[2:3] + tail[3:4]
@@ -238,11 +242,11 @@
     fwd, inv, fwd_nat, inv_nat = (jnp.asarray(t, BF) for t in tables())
     w1q, w2q = (w.transpose(1, 0, 2, 3).reshape(3, 384, CH) for w in (w1, w2))
     w1b, w2b = (w.transpose(1, 0, 3, 2).reshape(3, 384, CH) for w in (w1, w2))
-    outs = [((PEERS, 16, CH), BF), ((GRAD_ROWS, CH), BF)]
+    outs = [((PEERS, 16, CH), BF), ((1280, CH), BF), ((1280, CH), BF)]
     scratch = [((512, CH), F4), ((1024, CH), F4), ((512, CH), F4),
                ((10, 128, CH), F4), ((256, 10 * CH), BF), ((384, 2 * CH), BF), ((4, 128, CH), F4), ((8, 128, CH), F4),
                ((512, CH), F4), ((128, 10 * CH), F4), ((10, 128, 384), BF), ((8, 128, 384), BF), ((1024, CH), F4),
-               ((4, 128, 384), BF), ((8, 128, 384), BF), ((1024, CH), F4), ((1280, CH), F4)]
+               ((4, 128, 384), BF), ((8, 128, 384), BF), ((1024, CH), F4), ((1280, CH), F4), ((2, 1280, CH), BF)]
     return call(step_kernel, outs, scratch, 3 << 30, 24, left, own, right, ker,
                 w1q, b1.reshape(1, CH), w2q, b2.reshape(1, CH), w1b, w2b, fwd, inv, fwd_nat, inv_nat)
 
@@ -254,6 +258,25 @@
     total = total.astype(BF)
     for i in range(out.shape[0]):
         out[i] = total
+
+
+def quarter_kernel(keep, got, mine, one, two, three, both):
+    both[...] = (keep[...].astype(F4) + got[...].astype(F4)).astype(BF)
+    x = lax.axis_index("x")
+    for d, ref in enumerate((mine, one, two, three)):
+        ref[...] = both[pl.ds(pl.multiple_of((x ^ d) * 320, 320), 320), :]
+
+
+def add_kernel(mine, one, two, three, out):
+    total = (mine[...].astype(F4) + one[...].astype(F4)) + (two[...].astype(F4) + three[...].astype(F4))
+    out[...] = total.astype(BF)
+
+
+def near_sums(keep, give):
+    got = lax.ppermute(give, "c", [(0, 1), (1, 0)])
+    mine, *given = call(quarter_kernel, [((320, CH), BF)] * 4, [((1280, CH), BF)], 1 << 20, 8, keep, got)
+    got = [lax.ppermute(g, "x", [(x, x ^ d) for x in range(4)]) for d, g in enumerate(given, 1)]
+    return call(add_kernel, [((320, CH), BF)], [], 1 << 20, 8, mine, *got)[0]
 
 
 def summed(got, copies):
@@ -283,14 +306,13 @@
         return lax.ppermute(block, everywhere, [(ring[i], ring[(i + by) % n]) for i in range(n)])
 
     left, right = shifted(own[:, 0:16], 1), shifted(own[:, 0:16], -1)
-    pred_send, grads = local_step(left, own, right, corr_kernel, w1, b1, w2, b2)
-    n_plane, n_depth = lax.axis_size(PLANE_AXES), lax.axis_size(DEPTH_AXES)
-    part = lax.all_to_all(grads.reshape(n_plane, GRAD_ROWS // n_plane, CH), PLANE_AXES, 0, 0, tiled=True)
+    pred_send, keep, give = local_step(left, own, right, corr_kernel, w1, b1, w2, b2)
+    pred_got = lax.all_to_all(pred_send, ROWS_AXES, 0, 0, tiled=True)
+    n_near, n_depth, n_plane = (lax.axis_size(axes) for axes in (NEAR_AXES, DEPTH_AXES, PLANE_AXES))
+    part, pred_got = lax.optimization_barrier((near_sums(keep, give), pred_got))
+    part = lax.all_to_all(part.reshape(n_near, 40, CH), NEAR_AXES, 0, 0, tiled=True)
     part = lax.all_to_all(summed(part, n_depth), DEPTH_AXES, 0, 0, tiled=True)
-    part, pred_send = lax.optimization_barrier((part, pred_send))
-    pred_got = lax.all_to_all(pred_send, ROWS_AXES, 0, 0, tiled=True)
-    part, pred_got = lax.optimization_barrier((summed(part, n_plane), pred_got))
-    whole = lax.all_to_all(part, PLANE_AXES, 0, 0, tiled=True).reshape(GRAD_ROWS, CH)
+    whole = lax.all_to_all(summed(part, n_plane), PLANE_AXES, 0, 0, tiled=True).reshape(GRAD_ROWS, CH)
 
     got = pred_got.reshape(4, 8, 4, row_count, CH)
     even, odd = got[:, 0::2], got[::-1, 1::2]

time: 133 us -> 135 us (1.015)
  starting transfers between devices: 18.6 us -> 36.1 us
  blocking collectives: 75.2 us -> 64.4 us
  waiting for transfers between devices: 25.5 us -> 19.7 us
    all_to_all x1, blocking collectives: 21.7 us -> 9.99 us  [per_device(): lax.all_to_all(part.reshape(n_near, 40, CH), NEAR_AXES, 0, 0, tiled=True)]
    ppermute x0 -> x4, starting transfers between devices: none -> 11.5 us  [the longest x3 9.58 us: near_sums(): lax.ppermute(g, 'x', [(x, x ^ d) for x in range(4)])]
    all_to_all x1, waiting for transfers between devices: 10.9 us -> 0.01 us  [per_device(): pred_got = lax.all_to_all(pred_send, ROWS_AXES, 0, 0, tiled=True)]
    ppermute x0 -> x4, waiting for transfers between devices: none -> 5.86 us  [the longest x3 4.27 us: near_sums(): lax.ppermute(g, 'x', [(x, x ^ d) for x in range(4)])]
    all_to_all x1, starting transfers between devices: 5.32 us -> 9.98 us  [per_device(): pred_got = lax.all_to_all(pred_send, ROWS_AXES, 0, 0, tiled=True)]
    pallas_call x4 -> x6, Pallas kernels: 6.9 us -> 7.64 us  [call(): pl.pallas_call(kernel, out_shape=[jax.ShapeDtypeStruct(s, d) for s, d in...]
  transfers between devices with their start and end apart: 4 -> 8, of which waited for: 3 -> 5; matrix products, arithmetic and copies ran while one was open for 1% -> 1% of each run, Pallas kernels for 1% -> 0%
where the time goes in v6:
time: 135 us; the launch traced here: 134 us
  blocking collectives  64.4 us (48%)
  starting transfers between devices  36.1 us (27%)
  waiting for transfers between devices  19.7 us (15%)
  Pallas kernels  9.57 us (7%)
  local copies, waits for them, and re-layouts  3.2 us (2%)
    all_to_all x1, blocking collectives, per_device(): own = lax.all_to_all(send, ROWS_AXES, 0, 0, tiled=True)  35 us
    all_to_all x1, blocking collectives, per_device(): part = lax.all_to_all(summed(part, n_depth), DEPTH_AXES, 0, 0, tiled=True)  19.4 us
    all_to_all x1, waiting for transfers between devices, per_device(): lax.all_to_all(summed(part, n_plane), PLANE_AXES, 0, 0, tiled=True)  11.9 us
    all_to_all x1, blocking collectives, per_device(): lax.all_to_all(part.reshape(n_near, 40, CH), NEAR_AXES, 0, 0, tiled=True)  9.99 us
    all_to_all x1, starting transfers between devices, per_device(): pred_got = lax.all_to_all(pred_send, ROWS_AXES, 0, 0, tiled=True)  9.98 us
    ppermute x3, starting transfers between devices, near_sums(): lax.ppermute(g, 'x', [(x, x ^ d) for x in range(4)])  9.58 us
    all_to_all x1, starting transfers between devices, per_device(): lax.all_to_all(summed(part, n_plane), PLANE_AXES, 0, 0, tiled=True)  9.01 us
    pallas_call x6, Pallas kernels, call(): pl.pallas_call(kernel, out_shape=[jax.ShapeDtypeStruct(s, d) for s, d in...  7.64 us
  transfers between devices with their start and end apart: 8, of which 5 were waited for; matrix products, arithmetic and copies ran while one was open for 1% of the time, Pallas kernels for 0%

profile of v6, /device:TPU:1, one launch (start us, length us, event | category | flops | bytes accessed | tf_op | source)
XLA Modules:
  0.0 134.0 jit_solution(11961365140709906974)
XLA Ops:
  0.6 1.9 %shard_map.154 = bf16[32,32,128]{2,1,0:T(8,128)(2,1)} custom-call(bf16[4,128,128]{2,1,0:T(8,128)(2,1)} %lat.1, bf16[4,128,128]{2,1,0:T(8,128)(2,1)} %cot.1), custom_call_target="tpu_custom_call" | custom-call | tf_op jit(solution)/shard_map/pallas_call | solution.py:291
  2.6 0.0 copy-start.7
  2.6 35.0 %all_to_all.25.own = bf16[32,32,128]{2,1,0:T(8,128)(2,1)S(1)} all-to-all(bf16[32,32,128]{2,1,0:T(8,128)(2,1)} %shard_map.154), channel_id=1, replica_groups=mesh['y'=4,'zb'=4,'za'=2,'x'=4,'zh'=2,'c'=2] {'y','zb','za'}, dimensions={0} | all-to-all | bytes 524288 | tf_op jit(solution)/shard_map/all_to_all | solution.py:300
  37.5 1.9 %collective-permute-start = (bf16[32,16,128]{2,1,0:T(8,128)(2,1)S(1)}, bf16[32,16,128]{2,1,0:T(8,128)(2,1)S(1)}, u32[]{:S(2)}, u32[]{:S(2)}) collective-permute-start(bf16[32,16,128]{2,1,0:T(8,128)(2,1)S(1)} %slice.13), channel_id=1, source_target_pairs={{112,240},{240,368},{368,496},{496,480},{480,352},{352,224},{224,9... | collective-permute-start | bytes 393224 | tf_op jit(solution)/shard_map/ppermute | solution.py:306
  39.5 3.7 %collective-permute-start.1 = (bf16[32,16,128]{2,1,0:T(8,128)(2,1)S(1)}, bf16[32,16,128]{2,1,0:T(8,128)(2,1)S(1)}, u32[]{:S(2)}, u32[]{:S(2)}) collective-permute-start(bf16[32,16,128]{2,1,0:T(8,128)(2,1)S(1)} %slice.13), channel_id=1, source_target_pairs={{112,15},{240,112},{368,240},{496,368},{480,496},{352,480},{224,35... | collective-permute-start | bytes 393224 | tf_op jit(solution)/shard_map/ppermute | solution.py:306
  43.1 0.0 copy-done.7
  43.1 0.0 copy-start.8
  43.2 0.9 copy-done.8
  44.1 0.2 copy.35
  44.4 0.0 copy-start
  44.4 0.0 copy-start.3
  44.4 0.0 copy-start.4
  44.4 0.0 copy-start.5
  44.4 0.0 copy-start.6
  44.4 0.2 copy.36
  44.6 0.0 collective-permute-done.left
  44.6 2.0 %collective-permute-done.1.right = bf16[32,16,128]{2,1,0:T(8,128)(2,1)S(1)} collective-permute-done((bf16[32,16,128]{2,1,0:T(8,128)(2,1)S(1)}, bf16[32,16,128]{2,1,0:T(8,128)(2,1)S(1)}, u32[]{:S(2)}, u32[]{:S(2)}) %collective-permute-start.1) | collective-permute-done | bytes 131104 | tf_op jit(solution)/shard_map/ppermute | solution.py:306
  46.6 0.0 copy-start.1
  46.6 0.0 copy-done
  46.6 0.0 copy-done.3
  46.6 0.0 copy-done.4
  46.6 0.0 copy-done.5
  46.6 0.0 copy-done.6
  46.6 0.6 copy-done.1
  47.3 0.0 copy-done.2
  47.3 5.4 %shard_map.155 = (bf16[32,16,128]{2,1,0:T(8,128)(2,1)}, bf16[1280,128]{1,0:T(8,128)(2,1)S(1)}, bf16[1280,128]{1,0:T(8,128)(2,1)S(1)}) custom-call(bf16[32,16,128]{2,1,0:T(8,128)(2,1)S(1)} %collective-permute-done.left, bf16[32,32,128]{2,1,0:T(8,128)(2,1)S(1)} %all_to_all.25.own, bf16[32,16,128]{2,1,0:T(8,128)(2,1)S(1)} %collective-permute-done.1.right, ...), custom_call_target="tpu_custom_call" | custom-call | flops 3221225472 | bytes 4194304 | tf_op jit(solution)/shard_map/pallas_call | solution.py:230
  52.7 10.0 %all-to-all-start.1 = ((bf16[32,16,128]{2,1,0:T(8,128)(2,1)}), bf16[32,16,128]{2,1,0:T(8,128)(2,1)S(1)}, u32[]{:S(2)}, u32[]{:S(2)}) async-start(bf16[32,16,128]{2,1,0:T(8,128)(2,1)} %get-tuple-element.26), calls=%async_computation.1 | async-start | bytes 262144 | tf_op jit(solution)/shard_map/all_to_all | solution.py:310
  62.7 1.9 %collective-permute-start.2 = (bf16[1280,128]{1,0:T(8,128)(2,1)S(1)}, bf16[1280,128]{1,0:T(8,128)(2,1)S(1)}, u32[]{:S(2)}, u32[]{:S(2)}) collective-permute-start(bf16[1280,128]{1,0:T(8,128)(2,1)S(1)} %get-tuple-element.21), channel_id=1, source_target_pairs={{0,1},{1,0},{2,3},{3,2},{4,5},{5,4},{6,7},{7,6},{8,9},{9,8},{10,11... | collective-permute-start | bytes 983048 | tf_op jit(solution)/shard_map/ppermute | solution.py:276
  64.6 1.6 %collective-permute-done.2.got = bf16[1280,128]{1,0:T(8,128)(2,1)S(1)} collective-permute-done((bf16[1280,128]{1,0:T(8,128)(2,1)S(1)}, bf16[1280,128]{1,0:T(8,128)(2,1)S(1)}, u32[]{:S(2)}, u32[]{:S(2)}) %collective-permute-start.2) | collective-permute-done | bytes 327712 | tf_op jit(solution)/shard_map/ppermute | solution.py:276
  66.2 0.2 shard_map.156
  66.4 3.1 %collective-permute-start.3 = (bf16[320,128]{1,0:T(8,128)(2,1)S(1)}, bf16[320,128]{1,0:T(8,128)(2,1)S(1)}, u32[]{:S(2)}, u32[]{:S(2)}) collective-permute-start(bf16[320,128]{1,0:T(8,128)(2,1)S(1)} %get-tuple-element.23), channel_id=1, source_target_pairs={{0,4},{4,0},{8,12},{12,8},{1,5},{5,1},{9,13},{13,9},{2,6},{6,2},{1... | collective-permute-start | bytes 245768 | tf_op jit(solution)/shard_map/ppermute | solution.py:278
  69.5 4.4 %collective-permute-start.4 = (bf16[320,128]{1,0:T(8,128)(2,1)S(1)}, bf16[320,128]{1,0:T(8,128)(2,1)S(1)}, u32[]{:S(2)}, u32[]{:S(2)}) collective-permute-start(bf16[320,128]{1,0:T(8,128)(2,1)S(1)} %get-tuple-element.24), channel_id=1, source_target_pairs={{0,8},{4,12},{8,0},{12,4},{1,9},{5,13},{9,1},{13,5},{2,10},{6,14},... | collective-permute-start | bytes 245768 | tf_op jit(solution)/shard_map/ppermute | solution.py:278
  73.9 2.1 %collective-permute-start.5 = (bf16[320,128]{1,0:T(8,128)(2,1)S(1)}, bf16[320,128]{1,0:T(8,128)(2,1)S(1)}, u32[]{:S(2)}, u32[]{:S(2)}) collective-permute-start(bf16[320,128]{1,0:T(8,128)(2,1)S(1)} %get-tuple-element.25), channel_id=1, source_target_pairs={{0,12},{4,8},{8,4},{12,0},{1,13},{5,9},{9,5},{13,1},{2,14},{6,10},... | collective-permute-start | bytes 245768 | tf_op jit(solution)/shard_map/ppermute | solution.py:278
  76.0 0.0 collective-permute-done.3.one
  76.0 0.2 collective-permute-done.4.two
  76.2 4.1 %collective-permute-done.5.three = bf16[320,128]{1,0:T(8,128)(2,1)S(1)} collective-permute-done((bf16[320,128]{1,0:T(8,128)(2,1)S(1)}, bf16[320,128]{1,0:T(8,128)(2,1)S(1)}, u32[]{:S(2)}, u32[]{:S(2)}) %collective-permute-start.5) | collective-permute-done | bytes 81952 | tf_op jit(solution)/shard_map/ppermute | solution.py:278
  80.3 0.0 all-to-all-done.1
  80.3 10.0 %all_to_all.26.got = bf16[8,40,128]{2,1,0:T(8,128)(2,1)S(1)} all-to-all(bf16[8,40,128]{2,1,0:T(8,128)(2,1)S(1)} %bitcast.29), channel_id=1, replica_groups=mesh['y'=4,'zb'=4,'za'=2,'x'=4,'zh'=2,'c'=2] {'y','za'}, dimensions={0} | all-to-all | bytes 163840 | tf_op jit(solution)/shard_map/all_to_all | solution.py:313
  90.3 19.4 %all_to_all.27.got = bf16[8,40,128]{2,1,0:T(8,128)(2,1)S(1)} all-to-all(bf16[8,40,128]{2,1,0:T(8,128)(2,1)S(1)} %shard_map.158), channel_id=1, replica_groups=mesh['y'=4,'zb'=4,'za'=2,'x'=4,'zh'=2,'c'=2] {'zb','zh'}, dimensions={0} | all-to-all | bytes 163840 | tf_op jit(solution)/shard_map/all_to_all | solution.py:314
  109.8 0.9 shard_map.159
  110.7 9.0 %all-to-all-start.4 = ((bf16[64,40,128]{2,1,0:T(8,128)(2,1)}), bf16[64,40,128]{2,1,0:T(8,128)(2,1)S(1)}, u32[]{:S(2)}, u32[]{:S(2)}) async-start(bf16[64,40,128]{2,1,0:T(8,128)(2,1)} %shard_map.159), calls=%async_computation.4 | async-start | bytes 1310720 | tf_op jit(solution)/shard_map/all_to_all | solution.py:315
  119.8 0.1 pad_maximum_fusion
  119.9 0.1 copy.37
  120.0 0.1 copy.38
  120.2 0.1 rev.7
  120.2 0.8 copy.39
  121.0 11.9 %all-to-all-done.4 = bf16[64,40,128]{2,1,0:T(8,128)(2,1)S(1)} async-done(((bf16[64,40,128]{2,1,0:T(8,128)(2,1)}), bf16[64,40,128]{2,1,0:T(8,128)(2,1)S(1)}, u32[]{:S(2)}, u32[]{:S(2)}) %all-to-all-start.4) | async-done | bytes 655392 | tf_op jit(solution)/shard_map/all_to_all | solution.py:315
  132.9 1.1 shard_map.160
  (9 shorter events, 0.2 us)
Async XLA Ops:
  2.6 40.6 %copy-start.7 = (bf16[3,3,128,128]{3,2,1,0:T(8,128)(2,1)S(1)}, bf16[3,3,128,128]{3,2,1,0:T(8,128)(2,1)}, u32[]{:S(2)}) copy-start(bf16[3,3,128,128]{3,2,1,0:T(8,128)(2,1)} %param.13) | copy-start | bytes 884740
  37.5 7.1 %collective-permute-start = (bf16[32,16,128]{2,1,0:T(8,128)(2,1)S(1)}, bf16[32,16,128]{2,1,0:T(8,128)(2,1)S(1)}, u32[]{:S(2)}, u32[]{:S(2)}) collective-permute-start(bf16[32,16,128]{2,1,0:T(8,128)(2,1)S(1)} %slice.13), channel_id=1, source_target_pairs={{112,240},{240,368},{368,496},{496,480},{480,352},{352,224},{224,9... | collective-permute-start | bytes 393224 | tf_op jit(solution)/shard_map/ppermute | solution.py:306
  39.5 7.1 %collective-permute-start.1 = (bf16[32,16,128]{2,1,0:T(8,128)(2,1)S(1)}, bf16[32,16,128]{2,1,0:T(8,128)(2,1)S(1)}, u32[]{:S(2)}, u32[]{:S(2)}) collective-permute-start(bf16[32,16,128]{2,1,0:T(8,128)(2,1)S(1)} %slice.13), channel_id=1, source_target_pairs={{112,15},{240,112},{368,240},{496,368},{480,496},{352,480},{224,35... | collective-permute-start | bytes 393224 | tf_op jit(solution)/shard_map/ppermute | solution.py:306
  43.1 1.0 copy-start.8
  44.4 2.3 %copy-start = (bf16[128,128]{1,0:T(8,128)(2,1)S(1)}, bf16[128,128]{1,0:T(8,128)(2,1)}, u32[]{:S(2)}) copy-start(bf16[128,128]{1,0:T(8,128)(2,1)} %ker.1) | copy-start | bytes 98308
  44.4 2.2 %copy-start.3 = (bf16[128,384]{1,0:T(8,128)(2,1)S(1)}, bf16[128,384]{1,0:T(8,128)(2,1)}, u32[]{:S(2)}) copy-start(bf16[128,384]{1,0:T(8,128)(2,1)} %constant.15.clone.inv) | copy-start | bytes 294916
  44.4 2.2 %copy-start.4 = (bf16[128,384]{1,0:T(8,128)(2,1)S(1)}, bf16[128,384]{1,0:T(8,128)(2,1)}, u32[]{:S(2)}) copy-start(bf16[128,384]{1,0:T(8,128)(2,1)} %constant.17.clone.inv_nat) | copy-start | bytes 294916
  44.4 2.2 %copy-start.5 = (bf16[128,256]{1,0:T(8,128)(2,1)S(1)}, bf16[128,256]{1,0:T(8,128)(2,1)}, u32[]{:S(2)}) copy-start(bf16[128,256]{1,0:T(8,128)(2,1)} %constant.14.clone.fwd) | copy-start | bytes 196612
  44.4 2.2 %copy-start.6 = (bf16[128,256]{1,0:T(8,128)(2,1)S(1)}, bf16[128,256]{1,0:T(8,128)(2,1)}, u32[]{:S(2)}) copy-start(bf16[128,256]{1,0:T(8,128)(2,1)} %constant.16.clone.fwd_nat) | copy-start | bytes 196612
  46.6 0.7 copy-start.1
  46.6 0.7 copy-start.2
  52.7 27.6 %all-to-all-start.1 = ((bf16[32,16,128]{2,1,0:T(8,128)(2,1)}), bf16[32,16,128]{2,1,0:T(8,128)(2,1)S(1)}, u32[]{:S(2)}, u32[]{:S(2)}) async-start(bf16[32,16,128]{2,1,0:T(8,128)(2,1)} %get-tuple-element.26), calls=%async_computation.1 | async-start | bytes 262144 | tf_op jit(solution)/shard_map/all_to_all | solution.py:310
  62.7 3.5 %collective-permute-start.2 = (bf16[1280,128]{1,0:T(8,128)(2,1)S(1)}, bf16[1280,128]{1,0:T(8,128)(2,1)S(1)}, u32[]{:S(2)}, u32[]{:S(2)}) collective-permute-start(bf16[1280,128]{1,0:T(8,128)(2,1)S(1)} %get-tuple-element.21), channel_id=1, source_target_pairs={{0,1},{1,0},{2,3},{3,2},{4,5},{5,4},{6,7},{7,6},{8,9},{9,8},{10,11... | collective-permute-start | bytes 983048 | tf_op jit(solution)/shard_map/ppermute | solution.py:276
  66.4 9.6 %collective-permute-start.3 = (bf16[320,128]{1,0:T(8,128)(2,1)S(1)}, bf16[320,128]{1,0:T(8,128)(2,1)S(1)}, u32[]{:S(2)}, u32[]{:S(2)}) collective-permute-start(bf16[320,128]{1,0:T(8,128)(2,1)S(1)} %get-tuple-element.23), channel_id=1, source_target_pairs={{0,4},{4,0},{8,12},{12,8},{1,5},{5,1},{9,13},{13,9},{2,6},{6,2},{1... | collective-permute-start | bytes 245768 | tf_op jit(solution)/shard_map/ppermute | solution.py:278
  69.5 6.7 %collective-permute-start.4 = (bf16[320,128]{1,0:T(8,128)(2,1)S(1)}, bf16[320,128]{1,0:T(8,128)(2,1)S(1)}, u32[]{:S(2)}, u32[]{:S(2)}) collective-permute-start(bf16[320,128]{1,0:T(8,128)(2,1)S(1)} %get-tuple-element.24), channel_id=1, source_target_pairs={{0,8},{4,12},{8,0},{12,4},{1,9},{5,13},{9,1},{13,5},{2,10},{6,14},... | collective-permute-start | bytes 245768 | tf_op jit(solution)/shard_map/ppermute | solution.py:278
  73.9 6.4 %collective-permute-start.5 = (bf16[320,128]{1,0:T(8,128)(2,1)S(1)}, bf16[320,128]{1,0:T(8,128)(2,1)S(1)}, u32[]{:S(2)}, u32[]{:S(2)}) collective-permute-start(bf16[320,128]{1,0:T(8,128)(2,1)S(1)} %get-tuple-element.25), channel_id=1, source_target_pairs={{0,12},{4,8},{8,4},{12,0},{1,13},{5,9},{9,5},{13,1},{2,14},{6,10},... | collective-permute-start | bytes 245768 | tf_op jit(solution)/shard_map/ppermute | solution.py:278
  110.7 22.2 %all-to-all-start.4 = ((bf16[64,40,128]{2,1,0:T(8,128)(2,1)}), bf16[64,40,128]{2,1,0:T(8,128)(2,1)S(1)}, u32[]{:S(2)}, u32[]{:S(2)}) async-start(bf16[64,40,128]{2,1,0:T(8,128)(2,1)} %shard_map.159), calls=%async_computation.4 | async-start | bytes 1310720 | tf_op jit(solution)/shard_map/all_to_all | solution.py:315

commit v7 on v6

--- a/solution.py
+++ b/solution.py
@@ -8,7 +8,7 @@
 
 ROWS_AXES = ("y", "zb", "za")
 COLS_AXES = ("x", "zh", "c")
-NEAR_AXES = ("y", "za")
+NEAR_AXES = ("x", "y", "za")
 PLANE_AXES = ("c", "x", "y", "za")
 DEPTH_AXES = ("zb", "zh")
 SIZES = {"y": 4, "zb": 4, "za": 2, "x": 4, "zh": 2, "c": 2}
@@ -260,23 +260,13 @@
         out[i] = total
 
 
-def quarter_kernel(keep, got, mine, one, two, three, both):
-    both[...] = (keep[...].astype(F4) + got[...].astype(F4)).astype(BF)
-    x = lax.axis_index("x")
-    for d, ref in enumerate((mine, one, two, three)):
-        ref[...] = both[pl.ds(pl.multiple_of((x ^ d) * 320, 320), 320), :]
-
-
-def add_kernel(mine, one, two, three, out):
-    total = (mine[...].astype(F4) + one[...].astype(F4)) + (two[...].astype(F4) + three[...].astype(F4))
-    out[...] = total.astype(BF)
-
-
-def near_sums(keep, give):
+def add_kernel(keep, got, out):
+    out[...] = (keep[...].astype(F4) + got[...].astype(F4)).astype(BF)
+
+
+def core_sum(keep, give):
     got = lax.ppermute(give, "c", [(0, 1), (1, 0)])
-    mine, *given = call(quarter_kernel, [((320, CH), BF)] * 4, [((1280, CH), BF)], 1 << 20, 8, keep, got)
-    got = [lax.ppermute(g, "x", [(x, x ^ d) for x in range(4)]) for d, g in enumerate(given, 1)]
-    return call(add_kernel, [((320, CH), BF)], [], 1 << 20, 8, mine, *got)[0]
+    return call(add_kernel, [((1280, CH), BF)], [], 1 << 20, 8, keep, got)[0]
 
 
 def summed(got, copies):
@@ -309,7 +299,7 @@
     pred_send, keep, give = local_step(left, own, right, corr_kernel, w1, b1, w2, b2)
     pred_got = lax.all_to_all(pred_send, ROWS_AXES, 0, 0, tiled=True)
     n_near, n_depth, n_plane = (lax.axis_size(axes) for axes in (NEAR_AXES, DEPTH_AXES, PLANE_AXES))
-    part, pred_got = lax.optimization_barrier((near_sums(keep, give), pred_got))
+    part, pred_got = lax.optimization_barrier((core_sum(keep, give), pred_got))
     part = lax.all_to_all(part.reshape(n_near, 40, CH), NEAR_AXES, 0, 0, tiled=True)
     part = lax.all_to_all(summed(part, n_depth), DEPTH_AXES, 0, 0, tiled=True)
     whole = lax.all_to_all(summed(part, n_plane), PLANE_AXES, 0, 0, tiled=True).reshape(GRAD_ROWS, CH)

time: 135 us -> 129 us (0.956)
  starting transfers between devices: 36.1 us -> 26 us
  waiting for transfers between devices: 19.7 us -> 25.2 us
    all_to_all x1, waiting for transfers between devices: 0.01 us -> 9.7 us  [per_device(): pred_got = lax.all_to_all(pred_send, ROWS_AXES, 0, 0, tiled=True)]
    ppermute x4 -> x1, starting transfers between devices: 11.5 us -> 1.92 us  [core_sum(): got = lax.ppermute(give, 'c', [(0, 1), (1, 0)])]
    all_to_all x1, blocking collectives: 19.4 us -> 15 us  [per_device(): part = lax.all_to_all(summed(part, n_depth), DEPTH_AXES, 0, 0, tiled=True)]
    ppermute x4 -> x1, waiting for transfers between devices: 5.86 us -> 1.59 us  [core_sum(): got = lax.ppermute(give, 'c', [(0, 1), (1, 0)])]
    all_to_all x1, blocking collectives: 9.99 us -> 14 us  [per_device(): lax.all_to_all(part.reshape(n_near, 40, CH), NEAR_AXES, 0, 0, tiled=True)]
    pallas_call x6 -> x5, Pallas kernels: 7.64 us -> 7.52 us  [call(): pl.pallas_call(kernel, out_shape=[jax.ShapeDtypeStruct(s, d) for s, d in...]
  transfers between devices with their start and end apart: 8 -> 5, of which waited for: 5 -> 4; matrix products, arithmetic and copies ran while one was open for 1% -> 1% of each run, Pallas kernels for 0% -> 0%
where the time goes in v7:
time: 129 us
  blocking collectives  63.9 us (50%)
  starting transfers between devices  26 us (20%)
  waiting for transfers between devices  25.2 us (20%)
  Pallas kernels  9.45 us (7%)
  local copies, waits for them, and re-layouts  3.2 us (2%)
    all_to_all x1, blocking collectives, per_device(): own = lax.all_to_all(send, ROWS_AXES, 0, 0, tiled=True)  35 us
    all_to_all x1, blocking collectives, per_device(): part = lax.all_to_all(summed(part, n_depth), DEPTH_AXES, 0, 0, tiled=True)  15 us
    all_to_all x1, blocking collectives, per_device(): lax.all_to_all(part.reshape(n_near, 40, CH), NEAR_AXES, 0, 0, tiled=True)  14 us
    all_to_all x1, waiting for transfers between devices, per_device(): lax.all_to_all(summed(part, n_plane), PLANE_AXES, 0, 0, tiled=True)  11.9 us
    all_to_all x1, starting transfers between devices, per_device(): pred_got = lax.all_to_all(pred_send, ROWS_AXES, 0, 0, tiled=True)  9.98 us
    all_to_all x1, waiting for transfers between devices, per_device(): pred_got = lax.all_to_all(pred_send, ROWS_AXES, 0, 0, tiled=True)  9.7 us
    all_to_all x1, starting transfers between devices, per_device(): lax.all_to_all(summed(part, n_plane), PLANE_AXES, 0, 0, tiled=True)  8.51 us
    pallas_call x5, Pallas kernels, call(): pl.pallas_call(kernel, out_shape=[jax.ShapeDtypeStruct(s, d) for s, d in...  7.52 us
  transfers between devices with their start and end apart: 5, of which 4 were waited for; matrix products, arithmetic and copies ran while one was open for 1% of the time, Pallas kernels for 0%

profile of v7, /device:TPU:1, one launch (start us, length us, event | category | flops | bytes accessed | tf_op | source)
XLA Modules:
  0.0 128.7 jit_solution(16866395096058727617)
XLA Ops:
  0.6 1.9 %shard_map.154 = bf16[32,32,128]{2,1,0:T(8,128)(2,1)} custom-call(bf16[4,128,128]{2,1,0:T(8,128)(2,1)} %lat.1, bf16[4,128,128]{2,1,0:T(8,128)(2,1)} %cot.1), custom_call_target="tpu_custom_call" | custom-call | tf_op jit(solution)/shard_map/pallas_call | solution.py:281
  2.6 0.0 copy-start.7
  2.6 35.0 %all_to_all.25.own = bf16[32,32,128]{2,1,0:T(8,128)(2,1)S(1)} all-to-all(bf16[32,32,128]{2,1,0:T(8,128)(2,1)} %shard_map.154), channel_id=1, replica_groups=mesh['y'=4,'zb'=4,'za'=2,'x'=4,'zh'=2,'c'=2] {'y','zb','za'}, dimensions={0} | all-to-all | bytes 524288 | tf_op jit(solution)/shard_map/all_to_all | solution.py:290
  37.5 1.9 %collective-permute-start = (bf16[32,16,128]{2,1,0:T(8,128)(2,1)S(1)}, bf16[32,16,128]{2,1,0:T(8,128)(2,1)S(1)}, u32[]{:S(2)}, u32[]{:S(2)}) collective-permute-start(bf16[32,16,128]{2,1,0:T(8,128)(2,1)S(1)} %slice.13), channel_id=1, source_target_pairs={{112,240},{240,368},{368,496},{496,480},{480,352},{352,224},{224,9... | collective-permute-start | bytes 393224 | tf_op jit(solution)/shard_map/ppermute | solution.py:296
  39.5 3.7 %collective-permute-start.1 = (bf16[32,16,128]{2,1,0:T(8,128)(2,1)S(1)}, bf16[32,16,128]{2,1,0:T(8,128)(2,1)S(1)}, u32[]{:S(2)}, u32[]{:S(2)}) collective-permute-start(bf16[32,16,128]{2,1,0:T(8,128)(2,1)S(1)} %slice.13), channel_id=1, source_target_pairs={{112,15},{240,112},{368,240},{496,368},{480,496},{352,480},{224,35... | collective-permute-start | bytes 393224 | tf_op jit(solution)/shard_map/ppermute | solution.py:296
  43.1 0.0 copy-done.7
  43.1 0.0 copy-start.8
  43.2 0.9 copy-done.8
  44.1 0.2 copy.35
  44.4 0.0 copy-start
  44.4 0.0 copy-start.3
  44.4 0.0 copy-start.4
  44.4 0.0 copy-start.5
  44.4 0.0 copy-start.6
  44.4 0.2 copy.36
  44.6 0.0 collective-permute-done.left
  44.6 2.0 %collective-permute-done.1.right = bf16[32,16,128]{2,1,0:T(8,128)(2,1)S(1)} collective-permute-done((bf16[32,16,128]{2,1,0:T(8,128)(2,1)S(1)}, bf16[32,16,128]{2,1,0:T(8,128)(2,1)S(1)}, u32[]{:S(2)}, u32[]{:S(2)}) %collective-permute-start.1) | collective-permute-done | bytes 131104 | tf_op jit(solution)/shard_map/ppermute | solution.py:296
  46.6 0.0 copy-start.1
  46.6 0.0 copy-start.2
  46.6 0.0 copy-done
  46.6 0.0 copy-done.3
  46.6 0.0 copy-done.4
  46.6 0.0 copy-done.5
  46.6 0.0 copy-done.6
  46.6 0.6 copy-done.1
  47.3 0.0 copy-done.2
  47.3 5.4 %shard_map.155 = (bf16[32,16,128]{2,1,0:T(8,128)(2,1)}, bf16[1280,128]{1,0:T(8,128)(2,1)S(1)}, bf16[1280,128]{1,0:T(8,128)(2,1)S(1)}) custom-call(bf16[32,16,128]{2,1,0:T(8,128)(2,1)S(1)} %collective-permute-done.left, bf16[32,32,128]{2,1,0:T(8,128)(2,1)S(1)} %all_to_all.25.own, bf16[32,16,128]{2,1,0:T(8,128)(2,1)S(1)} %collective-permute-done.1.right, ...), custom_call_target="tpu_custom_call" | custom-call | flops 3221225472 | bytes 4194304 | tf_op jit(solution)/shard_map/pallas_call | solution.py:230
  52.7 10.0 %all-to-all-start.1 = ((bf16[32,16,128]{2,1,0:T(8,128)(2,1)}), bf16[32,16,128]{2,1,0:T(8,128)(2,1)S(1)}, u32[]{:S(2)}, u32[]{:S(2)}) async-start(bf16[32,16,128]{2,1,0:T(8,128)(2,1)} %get-tuple-element.18), calls=%async_computation.1 | async-start | bytes 262144 | tf_op jit(solution)/shard_map/all_to_all | solution.py:300
  62.7 1.9 %collective-permute-start.2 = (bf16[1280,128]{1,0:T(8,128)(2,1)S(1)}, bf16[1280,128]{1,0:T(8,128)(2,1)S(1)}, u32[]{:S(2)}, u32[]{:S(2)}) collective-permute-start(bf16[1280,128]{1,0:T(8,128)(2,1)S(1)} %get-tuple-element.17), channel_id=1, source_target_pairs={{0,1},{1,0},{2,3},{3,2},{4,5},{5,4},{6,7},{7,6},{8,9},{9,8},{10,11... | collective-permute-start | bytes 983048 | tf_op jit(solution)/shard_map/ppermute | solution.py:268
  64.6 1.6 %collective-permute-done.2.got = bf16[1280,128]{1,0:T(8,128)(2,1)S(1)} collective-permute-done((bf16[1280,128]{1,0:T(8,128)(2,1)S(1)}, bf16[1280,128]{1,0:T(8,128)(2,1)S(1)}, u32[]{:S(2)}, u32[]{:S(2)}) %collective-permute-start.2) | collective-permute-done | bytes 327712 | tf_op jit(solution)/shard_map/ppermute | solution.py:268
  66.2 0.1 shard_map.156
  66.3 9.7 %all-to-all-done.1 = bf16[32,16,128]{2,1,0:T(8,128)(2,1)S(1)} async-done(((bf16[32,16,128]{2,1,0:T(8,128)(2,1)}), bf16[32,16,128]{2,1,0:T(8,128)(2,1)S(1)}, u32[]{:S(2)}, u32[]{:S(2)}) %all-to-all-start.1) | async-done | bytes 131104 | tf_op jit(solution)/shard_map/all_to_all | solution.py:300
  76.0 14.0 %all_to_all.26.got = bf16[32,40,128]{2,1,0:T(8,128)(2,1)S(1)} all-to-all(bf16[32,40,128]{2,1,0:T(8,128)(2,1)S(1)} %bitcast.29), channel_id=1, replica_groups=mesh['y'=4,'zb'=4,'za'=2,'x'=4,'zh'=2,'c'=2] {'x','y','za'}, dimensions={0} | all-to-all | bytes 655360 | tf_op jit(solution)/shard_map/all_to_all | solution.py:303
  89.9 0.1 shard_map.157
  90.0 15.0 %all_to_all.27.got = bf16[8,40,128]{2,1,0:T(8,128)(2,1)S(1)} all-to-all(bf16[8,40,128]{2,1,0:T(8,128)(2,1)S(1)} %shard_map.157), channel_id=1, replica_groups=mesh['y'=4,'zb'=4,'za'=2,'x'=4,'zh'=2,'c'=2] {'zb','zh'}, dimensions={0} | all-to-all | bytes 163840 | tf_op jit(solution)/shard_map/all_to_all | solution.py:304
  105.0 0.9 shard_map.158
  105.9 8.5 %all-to-all-start.4 = ((bf16[64,40,128]{2,1,0:T(8,128)(2,1)}), bf16[64,40,128]{2,1,0:T(8,128)(2,1)S(1)}, u32[]{:S(2)}, u32[]{:S(2)}) async-start(bf16[64,40,128]{2,1,0:T(8,128)(2,1)} %shard_map.158), calls=%async_computation.4 | async-start | bytes 1310720 | tf_op jit(solution)/shard_map/all_to_all | solution.py:305
  114.5 0.1 pad_maximum_fusion
  114.6 0.1 copy.37
  114.8 0.1 copy.38
  114.9 0.1 rev.7
  115.0 0.8 copy.39
  115.7 11.9 %all-to-all-done.4 = bf16[64,40,128]{2,1,0:T(8,128)(2,1)S(1)} async-done(((bf16[64,40,128]{2,1,0:T(8,128)(2,1)}), bf16[64,40,128]{2,1,0:T(8,128)(2,1)S(1)}, u32[]{:S(2)}, u32[]{:S(2)}) %all-to-all-start.4) | async-done | bytes 655392 | tf_op jit(solution)/shard_map/all_to_all | solution.py:305
  127.6 1.1 shard_map.159
  (6 shorter events, 0.1 us)
Async XLA Ops:
  2.6 40.6 %copy-start.7 = (bf16[3,3,128,128]{3,2,1,0:T(8,128)(2,1)S(1)}, bf16[3,3,128,128]{3,2,1,0:T(8,128)(2,1)}, u32[]{:S(2)}) copy-start(bf16[3,3,128,128]{3,2,1,0:T(8,128)(2,1)} %param.13) | copy-start | bytes 884740
  37.5 7.1 %collective-permute-start = (bf16[32,16,128]{2,1,0:T(8,128)(2,1)S(1)}, bf16[32,16,128]{2,1,0:T(8,128)(2,1)S(1)}, u32[]{:S(2)}, u32[]{:S(2)}) collective-permute-start(bf16[32,16,128]{2,1,0:T(8,128)(2,1)S(1)} %slice.13), channel_id=1, source_target_pairs={{112,240},{240,368},{368,496},{496,480},{480,352},{352,224},{224,9... | collective-permute-start | bytes 393224 | tf_op jit(solution)/shard_map/ppermute | solution.py:296
  39.5 7.1 %collective-permute-start.1 = (bf16[32,16,128]{2,1,0:T(8,128)(2,1)S(1)}, bf16[32,16,128]{2,1,0:T(8,128)(2,1)S(1)}, u32[]{:S(2)}, u32[]{:S(2)}) collective-permute-start(bf16[32,16,128]{2,1,0:T(8,128)(2,1)S(1)} %slice.13), channel_id=1, source_target_pairs={{112,15},{240,112},{368,240},{496,368},{480,496},{352,480},{224,35... | collective-permute-start | bytes 393224 | tf_op jit(solution)/shard_map/ppermute | solution.py:296
  43.1 1.0 copy-start.8
  44.4 2.3 %copy-start = (bf16[128,128]{1,0:T(8,128)(2,1)S(1)}, bf16[128,128]{1,0:T(8,128)(2,1)}, u32[]{:S(2)}) copy-start(bf16[128,128]{1,0:T(8,128)(2,1)} %ker.1) | copy-start | bytes 98308
  44.4 2.2 %copy-start.3 = (bf16[128,384]{1,0:T(8,128)(2,1)S(1)}, bf16[128,384]{1,0:T(8,128)(2,1)}, u32[]{:S(2)}) copy-start(bf16[128,384]{1,0:T(8,128)(2,1)} %constant.15.clone.inv) | copy-start | bytes 294916
  44.4 2.2 %copy-start.4 = (bf16[128,384]{1,0:T(8,128)(2,1)S(1)}, bf16[128,384]{1,0:T(8,128)(2,1)}, u32[]{:S(2)}) copy-start(bf16[128,384]{1,0:T(8,128)(2,1)} %constant.17.clone.inv_nat) | copy-start | bytes 294916
  44.4 2.2 %copy-start.5 = (bf16[128,256]{1,0:T(8,128)(2,1)S(1)}, bf16[128,256]{1,0:T(8,128)(2,1)}, u32[]{:S(2)}) copy-start(bf16[128,256]{1,0:T(8,128)(2,1)} %constant.14.clone.fwd) | copy-start | bytes 196612
  44.4 2.2 %copy-start.6 = (bf16[128,256]{1,0:T(8,128)(2,1)S(1)}, bf16[128,256]{1,0:T(8,128)(2,1)}, u32[]{:S(2)}) copy-start(bf16[128,256]{1,0:T(8,128)(2,1)} %constant.16.clone.fwd_nat) | copy-start | bytes 196612
  46.6 0.7 copy-start.1
  46.6 0.7 copy-start.2
  52.7 23.3 %all-to-all-start.1 = ((bf16[32,16,128]{2,1,0:T(8,128)(2,1)}), bf16[32,16,128]{2,1,0:T(8,128)(2,1)S(1)}, u32[]{:S(2)}, u32[]{:S(2)}) async-start(bf16[32,16,128]{2,1,0:T(8,128)(2,1)} %get-tuple-element.18), calls=%async_computation.1 | async-start | bytes 262144 | tf_op jit(solution)/shard_map/all_to_all | solution.py:300
  62.7 3.5 %collective-permute-start.2 = (bf16[1280,128]{1,0:T(8,128)(2,1)S(1)}, bf16[1280,128]{1,0:T(8,128)(2,1)S(1)}, u32[]{:S(2)}, u32[]{:S(2)}) collective-permute-start(bf16[1280,128]{1,0:T(8,128)(2,1)S(1)} %get-tuple-element.17), channel_id=1, source_target_pairs={{0,1},{1,0},{2,3},{3,2},{4,5},{5,4},{6,7},{7,6},{8,9},{9,8},{10,11... | collective-permute-start | bytes 983048 | tf_op jit(solution)/shard_map/ppermute | solution.py:268
  105.9 21.7 %all-to-all-start.4 = ((bf16[64,40,128]{2,1,0:T(8,128)(2,1)}), bf16[64,40,128]{2,1,0:T(8,128)(2,1)S(1)}, u32[]{:S(2)}, u32[]{:S(2)}) async-start(bf16[64,40,128]{2,1,0:T(8,128)(2,1)} %shard_map.158), calls=%async_computation.4 | async-start | bytes 1310720 | tf_op jit(solution)/shard_map/all_to_all | solution.py:305

commit v8 on v5

--- a/solution.py
+++ b/solution.py
@@ -8,7 +8,8 @@
 
 ROWS_AXES = ("y", "zb", "za")
 COLS_AXES = ("x", "zh", "c")
-PLANE_AXES = ("y", "za", "x", "c")
+NEAR_AXES = ("x", "y", "za")
+PLANE_AXES = ("c", "x", "y", "za")
 DEPTH_AXES = ("zb", "zh")
 SIZES = {"y": 4, "zb": 4, "za": 2, "x": 4, "zh": 2, "c": 2}
 N_ROWS = 128
@@ -108,11 +109,15 @@
     return jnp.concatenate([high, low, high], axis=0)
 
 
-def send_kernel(lat, cot, out, wide, packed):
+def send_kernel(lat, cot, out, staged, wide, packed, sems):
     zh, c = lax.axis_index("zh"), lax.axis_index("c")
     flip = flipped(zh, c)
-    for t, ref in enumerate((lat, cot)):
-        wide[t * 512 : t * 512 + 512, :] = ref[...].reshape(512, CH).astype(F4)
+    copies = [pltpu.make_async_copy(ref, staged.at[t], sems.at[t]) for t, ref in enumerate((lat, cot))]
+    for copy in copies:
+        copy.start()
+    for t, copy in enumerate(copies):
+        copy.wait()
+        wide[t * 512 : t * 512 + 512, :] = staged[t].reshape(512, CH).astype(F4)
     for k in range(PEERS):
         start = pl.multiple_of(4 * window_of(k // 8, jnp.int32(k % 8), flip), 4)
         for t in range(2):
@@ -196,27 +201,27 @@
         for p in range(3):
             at = (p * 3 + q) * 128
             out[at : at + 128, :] = d[p * 128 : p * 128 + 128].astype(BF)
-            out[1152 + at : 1280 + at, :] = e[p * 128 : p * 128 + 128].astype(BF)
+            out[1280 + at : 1408 + at, :] = e[p * 128 : p * 128 + 128].astype(BF)
     both = jnp.zeros((N_ROWS, CH), F4)
     for j in range(0, 10, 2):
         two = jnp.concatenate([gm[(j + i) * 128 : (j + i) * 128 + 128, :] for i in range(2)], axis=1).astype(BF)
         s = dot(fwd[...], jnp.concatenate([two, two], axis=0))
         for i in range(2):
             both = both + cross(s[:, i * CH : (i + 1) * CH], spec[:, (j + i) * CH : (j + i + 1) * CH])
-    out[2304:2432, :] = dot(inv_nat[...], three_parts(both)).astype(BF)
+    out[1152:1280, :] = dot(inv_nat[...], three_parts(both)).astype(BF)
     rows = []
     for wide in (slope1_wide, own2_wide):
         b = jnp.sum(wide, axis=0, keepdims=True)
         high = b.astype(BF).astype(F4)
         rows += [high, b - high]
-    tail = jnp.concatenate(rows + [jnp.zeros((GRAD_ROWS - 2436, CH), F4)], axis=0)
-    out[2432:GRAD_ROWS, :] = tail.astype(BF)
+    tail = jnp.concatenate(rows + [jnp.zeros((124, CH), F4)], axis=0)
+    out[2432:2560, :] = tail.astype(BF)
 
 
 def finish_kernel(whole, dw1, dw2, dk, db1, db2):
     dw1[...] = whole[0:1152].astype(F4)
-    dw2[...] = whole[1152:2304].astype(F4)
-    dk[...] = whole[2304:2432].astype(F4)
+    dk[...] = whole[1152:1280].astype(F4)
+    dw2[...] = whole[1280:2432].astype(F4)
     tail = whole[2432:2448].astype(F4)
     db1[...] = tail[0:1] + tail[1:2]
     db2[...] = tail[2:3] + tail[3:4]
@@ -256,6 +261,16 @@
         out[i] = total
 
 
+def half_kernel(grads, got, out):
+    rows = pl.ds(pl.multiple_of(lax.axis_index("c") * 1280, 1280), 1280)
+    out[...] = (grads[rows, :].astype(F4) + got[rows, :].astype(F4)).astype(BF)
+
+
+def core_sum(grads):
+    got = lax.ppermute(grads, "c", [(0, 1), (1, 0)])
+    return call(half_kernel, [((GRAD_ROWS // 2, CH), BF)], [], 1 << 20, 8, grads, got)[0]
+
+
 def summed(got, copies):
     (out,) = call(sum_kernel, [((copies,) + got.shape[1:], BF)], [], 1 << 20, 8, got)
     return out
@@ -264,16 +279,15 @@
 def per_device(latent, corr_kernel, w1, b1, w2, b2, cotangent):
     row_count, col_count, _ = latent.shape
     flip = flipped(lax.axis_index("zh"), lax.axis_index("c"))
-    block = pl.BlockSpec(latent.shape, lambda i: (0, 0, 0))
     send = pl.pallas_call(
         send_kernel,
-        grid=(1,),
         out_shape=jax.ShapeDtypeStruct((PEERS, 32, CH), BF),
-        in_specs=[block, block],
-        out_specs=pl.BlockSpec((PEERS, 32, CH), lambda i: (0, 0, 0)),
-        scratch_shapes=[pltpu.VMEM((1024, CH), F4), pltpu.VMEM((1024, CH), F4)],
-        compiler_params=pltpu.CompilerParams(vmem_limit_bytes=60 << 20),
-    )(latent, cotangent)
+        in_specs=[pl.BlockSpec(memory_space=pltpu.HBM)] * 2,
+        out_specs=VMEM,
+        scratch_shapes=[pltpu.VMEM((2, row_count, col_count, CH), BF), pltpu.VMEM((1024, CH), F4),
+                        pltpu.VMEM((1024, CH), F4), pltpu.SemaphoreType.DMA((2,))],
+        compiler_params=pltpu.CompilerParams(vmem_limit_bytes=8 << 20),
+    )(*(pltpu.with_memory_space_constraint(a, pltpu.HBM) for a in (latent, cotangent)))
     own = lax.all_to_all(send, ROWS_AXES, 0, 0, tiled=True)
     ring = device_ring()
     n = len(ring)
@@ -284,13 +298,12 @@
 
     left, right = shifted(own[:, 0:16], 1), shifted(own[:, 0:16], -1)
     pred_send, grads = local_step(left, own, right, corr_kernel, w1, b1, w2, b2)
-    n_plane, n_depth = lax.axis_size(PLANE_AXES), lax.axis_size(DEPTH_AXES)
-    part = lax.all_to_all(grads.reshape(n_plane, GRAD_ROWS // n_plane, CH), PLANE_AXES, 0, 0, tiled=True)
+    pred_got = lax.all_to_all(pred_send, ROWS_AXES, 0, 0, tiled=True)
+    n_near, n_depth, n_plane = (lax.axis_size(axes) for axes in (NEAR_AXES, DEPTH_AXES, PLANE_AXES))
+    part, pred_got = lax.optimization_barrier((core_sum(grads), pred_got))
+    part = lax.all_to_all(part.reshape(n_near, 40, CH), NEAR_AXES, 0, 0, tiled=True)
     part = lax.all_to_all(summed(part, n_depth), DEPTH_AXES, 0, 0, tiled=True)
-    part, pred_send = lax.optimization_barrier((part, pred_send))
-    pred_got = lax.all_to_all(pred_send, ROWS_AXES, 0, 0, tiled=True)
-    part, pred_got = lax.optimization_barrier((summed(part, n_plane), pred_got))
-    whole = lax.all_to_all(part, PLANE_AXES, 0, 0, tiled=True).reshape(GRAD_ROWS, CH)
+    whole = lax.all_to_all(summed(part, n_plane), PLANE_AXES, 0, 0, tiled=True).reshape(GRAD_ROWS, CH)
 
     got = pred_got.reshape(4, 8, 4, row_count, CH)
     even, odd = got[:, 0::2], got[::-1, 1::2]

time: 133 us -> 131 us (0.985)
  blocking collectives: 75.2 us -> 66.1 us
  starting transfers between devices: 18.6 us -> 26.3 us
    all_to_all x1, blocking collectives: 21.7 us -> 14.5 us  [per_device(): lax.all_to_all(part.reshape(n_near, 40, CH), NEAR_AXES, 0, 0, tiled=True)]
    all_to_all x1, starting transfers between devices: 5.32 us -> 8.94 us  [per_device(): pred_got = lax.all_to_all(pred_send, ROWS_AXES, 0, 0, tiled=True)]
    ppermute x0 -> x1, starting transfers between devices: none -> 2.96 us  [core_sum(): got = lax.ppermute(grads, 'c', [(0, 1), (1, 0)])]
    all_to_all x1, blocking collectives: 18.6 us -> 16.9 us  [per_device(): part = lax.all_to_all(summed(part, n_depth), DEPTH_AXES, 0, 0, tiled=True)]
    pallas_call x4 -> x5, Pallas kernels: 6.9 us -> 6.92 us  [call(): pl.pallas_call(kernel, out_shape=[jax.ShapeDtypeStruct(s, d) for s, d in...]
  transfers between devices with their start and end apart: 4 -> 5, of which waited for: 3 -> 3; matrix products, arithmetic and copies ran while one was open for 1% -> 1% of each run, Pallas kernels for 1% -> 0%
where the time goes in v8:
time: 131 us; the launch traced here: 130 us
  blocking collectives  66.1 us (50%)
  starting transfers between devices  26.3 us (20%)
  waiting for transfers between devices  25.5 us (19%)
  Pallas kernels  8.13 us (6%)
  local copies, waits for them, and re-layouts  3.21 us (2%)
    all_to_all x1, blocking collectives, per_device(): own = lax.all_to_all(send, ROWS_AXES, 0, 0, tiled=True)  34.8 us
    all_to_all x1, blocking collectives, per_device(): part = lax.all_to_all(summed(part, n_depth), DEPTH_AXES, 0, 0, tiled=True)  16.9 us
    all_to_all x1, blocking collectives, per_device(): lax.all_to_all(part.reshape(n_near, 40, CH), NEAR_AXES, 0, 0, tiled=True)  14.5 us
    all_to_all x1, waiting for transfers between devices, per_device(): lax.all_to_all(summed(part, n_plane), PLANE_AXES, 0, 0, tiled=True)  11.9 us
    all_to_all x1, waiting for transfers between devices, per_device(): pred_got = lax.all_to_all(pred_send, ROWS_AXES, 0, 0, tiled=True)  11.7 us
    all_to_all x1, starting transfers between devices, per_device(): pred_got = lax.all_to_all(pred_send, ROWS_AXES, 0, 0, tiled=True)  8.94 us
    all_to_all x1, starting transfers between devices, per_device(): lax.all_to_all(summed(part, n_plane), PLANE_AXES, 0, 0, tiled=True)  8.84 us
    pallas_call x5, Pallas kernels, call(): pl.pallas_call(kernel, out_shape=[jax.ShapeDtypeStruct(s, d) for s, d in...  6.92 us
  transfers between devices with their start and end apart: 5, of which 3 were waited for; matrix products, arithmetic and copies ran while one was open for 1% of the time, Pallas kernels for 0%

profile of v8, /device:TPU:1, one launch (start us, length us, event | category | flops | bytes accessed | tf_op | source)
XLA Modules:
  0.0 130.3 jit_solution(13837961577558223493)
XLA Ops:
  0.6 1.2 shard_map.154
  1.9 0.0 copy-start.7
  1.9 34.8 %all_to_all.25.own = bf16[32,32,128]{2,1,0:T(8,128)(2,1)S(1)} all-to-all(bf16[32,32,128]{2,1,0:T(8,128)(2,1)S(1)} %shard_map.154), channel_id=1, replica_groups=mesh['y'=4,'zb'=4,'za'=2,'x'=4,'zh'=2,'c'=2] {'y','zb','za'}, dimensions={0} | all-to-all | bytes 524288 | tf_op jit(solution)/shard_map/all_to_all | solution.py:291
  36.6 1.9 %collective-permute-start = (bf16[32,16,128]{2,1,0:T(8,128)(2,1)S(1)}, bf16[32,16,128]{2,1,0:T(8,128)(2,1)S(1)}, u32[]{:S(2)}, u32[]{:S(2)}) collective-permute-start(bf16[32,16,128]{2,1,0:T(8,128)(2,1)S(1)} %slice.13), channel_id=1, source_target_pairs={{112,240},{240,368},{368,496},{496,480},{480,352},{352,224},{224,9... | collective-permute-start | bytes 393224 | tf_op jit(solution)/shard_map/ppermute | solution.py:297
  38.6 3.7 %collective-permute-start.1 = (bf16[32,16,128]{2,1,0:T(8,128)(2,1)S(1)}, bf16[32,16,128]{2,1,0:T(8,128)(2,1)S(1)}, u32[]{:S(2)}, u32[]{:S(2)}) collective-permute-start(bf16[32,16,128]{2,1,0:T(8,128)(2,1)S(1)} %slice.13), channel_id=1, source_target_pairs={{112,15},{240,112},{368,240},{496,368},{480,496},{352,480},{224,35... | collective-permute-start | bytes 393224 | tf_op jit(solution)/shard_map/ppermute | solution.py:297
  42.2 0.0 copy-done.7
  42.3 0.0 copy-start.8
  42.3 0.9 copy-done.8
  43.2 0.2 copy.35
  43.5 0.0 copy-start
  43.5 0.0 copy-start.3
  43.5 0.0 copy-start.4
  43.5 0.0 copy-start.5
  43.5 0.0 copy-start.6
  43.5 0.2 copy.36
  43.7 0.0 collective-permute-done.left
  43.7 2.0 %collective-permute-done.1.right = bf16[32,16,128]{2,1,0:T(8,128)(2,1)S(1)} collective-permute-done((bf16[32,16,128]{2,1,0:T(8,128)(2,1)S(1)}, bf16[32,16,128]{2,1,0:T(8,128)(2,1)S(1)}, u32[]{:S(2)}, u32[]{:S(2)}) %collective-permute-start.1) | collective-permute-done | bytes 131104 | tf_op jit(solution)/shard_map/ppermute | solution.py:297
  45.7 0.0 copy-start.1
  45.7 0.0 copy-start.2
  45.7 0.0 copy-done
  45.7 0.0 copy-done.3
  45.7 0.0 copy-done.4
  45.7 0.0 copy-done.5
  45.7 0.0 copy-done.6
  45.7 0.6 copy-done.1
  46.4 0.0 copy-done.2
  46.4 4.8 %shard_map.155 = (bf16[32,16,128]{2,1,0:T(8,128)(2,1)}, bf16[2560,128]{1,0:T(8,128)(2,1)S(1)}) custom-call(bf16[32,16,128]{2,1,0:T(8,128)(2,1)S(1)} %collective-permute-done.left, bf16[32,32,128]{2,1,0:T(8,128)(2,1)S(1)} %all_to_all.25.own, bf16[32,16,128]{2,1,0:T(8,128)(2,1)S(1)} %collective-permute-done.1.right, bf16[128,128]{1,0:T(8,128)(2,1)S(1)} %copy-done, ...), custom_call_target="tpu_custom_call" | custom-call | flops 3221225472 | bytes 4194304 | tf_op jit(solution)/shard_map/pallas_call | solution.py:231
  51.2 3.0 %collective-permute-start.2 = (bf16[2560,128]{1,0:T(8,128)(2,1)S(1)}, bf16[2560,128]{1,0:T(8,128)(2,1)S(1)}, u32[]{:S(2)}, u32[]{:S(2)}) collective-permute-start(bf16[2560,128]{1,0:T(8,128)(2,1)S(1)} %get-tuple-element.15.grads), channel_id=1, source_target_pairs={{0,1},{1,0},{2,3},{3,2},{4,5},{5,4},{6,7},{7,6},{8,9},{9,8},{10,11... | collective-permute-start | bytes 1966088 | tf_op jit(solution)/shard_map/ppermute | solution.py:270
  54.2 8.9 %all-to-all-start.1 = ((bf16[32,16,128]{2,1,0:T(8,128)(2,1)}), bf16[32,16,128]{2,1,0:T(8,128)(2,1)S(1)}, u32[]{:S(2)}, u32[]{:S(2)}) async-start(bf16[32,16,128]{2,1,0:T(8,128)(2,1)} %get-tuple-element.16), calls=%async_computation.1 | async-start | bytes 262144 | tf_op jit(solution)/shard_map/all_to_all | solution.py:301
  63.1 0.0 collective-permute-done.2.got
  63.1 0.1 shard_map.156
  63.2 11.7 %all-to-all-done.1 = bf16[32,16,128]{2,1,0:T(8,128)(2,1)S(1)} async-done(((bf16[32,16,128]{2,1,0:T(8,128)(2,1)}), bf16[32,16,128]{2,1,0:T(8,128)(2,1)S(1)}, u32[]{:S(2)}, u32[]{:S(2)}) %all-to-all-start.1) | async-done | bytes 131104 | tf_op jit(solution)/shard_map/all_to_all | solution.py:301
  74.9 14.5 %all_to_all.26.got = bf16[32,40,128]{2,1,0:T(8,128)(2,1)S(1)} all-to-all(bf16[32,40,128]{2,1,0:T(8,128)(2,1)S(1)} %bitcast.29), channel_id=1, replica_groups=mesh['y'=4,'zb'=4,'za'=2,'x'=4,'zh'=2,'c'=2] {'x','y','za'}, dimensions={0} | all-to-all | bytes 655360 | tf_op jit(solution)/shard_map/all_to_all | solution.py:304
  89.4 0.1 shard_map.157
  89.5 16.9 %all_to_all.27.got = bf16[8,40,128]{2,1,0:T(8,128)(2,1)S(1)} all-to-all(bf16[8,40,128]{2,1,0:T(8,128)(2,1)S(1)} %shard_map.157), channel_id=1, replica_groups=mesh['y'=4,'zb'=4,'za'=2,'x'=4,'zh'=2,'c'=2] {'zb','zh'}, dimensions={0} | all-to-all | bytes 163840 | tf_op jit(solution)/shard_map/all_to_all | solution.py:305
  106.3 0.9 shard_map.158
  107.2 8.8 %all-to-all-start.4 = ((bf16[64,40,128]{2,1,0:T(8,128)(2,1)}), bf16[64,40,128]{2,1,0:T(8,128)(2,1)S(1)}, u32[]{:S(2)}, u32[]{:S(2)}) async-start(bf16[64,40,128]{2,1,0:T(8,128)(2,1)} %shard_map.158), calls=%async_computation.4 | async-start | bytes 1310720 | tf_op jit(solution)/shard_map/all_to_all | solution.py:306
  116.2 0.1 pad_maximum_fusion
  116.3 0.1 copy.37
  116.4 0.1 copy.38
  116.5 0.1 rev.7
  116.6 0.8 copy.39
  117.4 11.9 %all-to-all-done.4 = bf16[64,40,128]{2,1,0:T(8,128)(2,1)S(1)} async-done(((bf16[64,40,128]{2,1,0:T(8,128)(2,1)}), bf16[64,40,128]{2,1,0:T(8,128)(2,1)S(1)}, u32[]{:S(2)}, u32[]{:S(2)}) %all-to-all-start.4) | async-done | bytes 655392 | tf_op jit(solution)/shard_map/all_to_all | solution.py:306
  129.3 1.1 shard_map.159
  (6 shorter events, 0.1 us)
Async XLA Ops:
  1.9 40.4 %copy-start.7 = (bf16[3,3,128,128]{3,2,1,0:T(8,128)(2,1)S(1)}, bf16[3,3,128,128]{3,2,1,0:T(8,128)(2,1)}, u32[]{:S(2)}) copy-start(bf16[3,3,128,128]{3,2,1,0:T(8,128)(2,1)} %param.13) | copy-start | bytes 884740
  36.6 7.1 %collective-permute-start = (bf16[32,16,128]{2,1,0:T(8,128)(2,1)S(1)}, bf16[32,16,128]{2,1,0:T(8,128)(2,1)S(1)}, u32[]{:S(2)}, u32[]{:S(2)}) collective-permute-start(bf16[32,16,128]{2,1,0:T(8,128)(2,1)S(1)} %slice.13), channel_id=1, source_target_pairs={{112,240},{240,368},{368,496},{496,480},{480,352},{352,224},{224,9... | collective-permute-start | bytes 393224 | tf_op jit(solution)/shard_map/ppermute | solution.py:297
  38.6 7.1 %collective-permute-start.1 = (bf16[32,16,128]{2,1,0:T(8,128)(2,1)S(1)}, bf16[32,16,128]{2,1,0:T(8,128)(2,1)S(1)}, u32[]{:S(2)}, u32[]{:S(2)}) collective-permute-start(bf16[32,16,128]{2,1,0:T(8,128)(2,1)S(1)} %slice.13), channel_id=1, source_target_pairs={{112,15},{240,112},{368,240},{496,368},{480,496},{352,480},{224,35... | collective-permute-start | bytes 393224 | tf_op jit(solution)/shard_map/ppermute | solution.py:297
  42.3 1.0 copy-start.8
  43.5 2.3 %copy-start = (bf16[128,128]{1,0:T(8,128)(2,1)S(1)}, bf16[128,128]{1,0:T(8,128)(2,1)}, u32[]{:S(2)}) copy-start(bf16[128,128]{1,0:T(8,128)(2,1)} %ker.1) | copy-start | bytes 98308
  43.5 2.2 %copy-start.3 = (bf16[128,384]{1,0:T(8,128)(2,1)S(1)}, bf16[128,384]{1,0:T(8,128)(2,1)}, u32[]{:S(2)}) copy-start(bf16[128,384]{1,0:T(8,128)(2,1)} %constant.15.clone.inv) | copy-start | bytes 294916
  43.5 2.2 %copy-start.4 = (bf16[128,384]{1,0:T(8,128)(2,1)S(1)}, bf16[128,384]{1,0:T(8,128)(2,1)}, u32[]{:S(2)}) copy-start(bf16[128,384]{1,0:T(8,128)(2,1)} %constant.17.clone.inv_nat) | copy-start | bytes 294916
  43.5 2.2 %copy-start.5 = (bf16[128,256]{1,0:T(8,128)(2,1)S(1)}, bf16[128,256]{1,0:T(8,128)(2,1)}, u32[]{:S(2)}) copy-start(bf16[128,256]{1,0:T(8,128)(2,1)} %constant.14.clone.fwd) | copy-start | bytes 196612
  43.5 2.2 %copy-start.6 = (bf16[128,256]{1,0:T(8,128)(2,1)S(1)}, bf16[128,256]{1,0:T(8,128)(2,1)}, u32[]{:S(2)}) copy-start(bf16[128,256]{1,0:T(8,128)(2,1)} %constant.16.clone.fwd_nat) | copy-start | bytes 196612
  45.7 0.7 copy-start.1
  45.7 0.7 copy-start.2
  51.2 11.9 %collective-permute-start.2 = (bf16[2560,128]{1,0:T(8,128)(2,1)S(1)}, bf16[2560,128]{1,0:T(8,128)(2,1)S(1)}, u32[]{:S(2)}, u32[]{:S(2)}) collective-permute-start(bf16[2560,128]{1,0:T(8,128)(2,1)S(1)} %get-tuple-element.15.grads), channel_id=1, source_target_pairs={{0,1},{1,0},{2,3},{3,2},{4,5},{5,4},{6,7},{7,6},{8,9},{9,8},{10,11... | collective-permute-start | bytes 1966088 | tf_op jit(solution)/shard_map/ppermute | solution.py:270
  54.2 20.7 %all-to-all-start.1 = ((bf16[32,16,128]{2,1,0:T(8,128)(2,1)}), bf16[32,16,128]{2,1,0:T(8,128)(2,1)S(1)}, u32[]{:S(2)}, u32[]{:S(2)}) async-start(bf16[32,16,128]{2,1,0:T(8,128)(2,1)} %get-tuple-element.16), calls=%async_computation.1 | async-start | bytes 262144 | tf_op jit(solution)/shard_map/all_to_all | solution.py:301
  107.2 22.1 %all-to-all-start.4 = ((bf16[64,40,128]{2,1,0:T(8,128)(2,1)}), bf16[64,40,128]{2,1,0:T(8,128)(2,1)S(1)}, u32[]{:S(2)}, u32[]{:S(2)}) async-start(bf16[64,40,128]{2,1,0:T(8,128)(2,1)} %shard_map.158), calls=%async_computation.4 | async-start | bytes 1310720 | tf_op jit(solution)/shard_map/all_to_all | solution.py:306

commit v9 on v8

--- a/solution.py
+++ b/solution.py
@@ -132,7 +132,7 @@
 
 
 def step_kernel(left, own, right, ker, w1, b1, w2, b2, w1b, w2b, fwd, inv, fwd_nat, inv_nat,
-                pred, out,
+                pred, keep, give,
                 gl, go, gr, latf, xw, parts, cots, hid, placed, spec, m3, h3, rise1, s3, z3, gh, gm):
     for ref, wide in ((left, gl), (own, go), (right, gr)):
         wide[...] = ref[...].reshape(wide.shape).astype(F4)
@@ -195,27 +195,32 @@
     gm[128:1152, :] = gh[...]
     for q in range(3):
         gm[q * 128 : q * 128 + 1024, :] += dot(z3[...].reshape(1024, 384), w1b[q])
-    for q in range(3):
-        d = dot_t(m3[q : q + 8].reshape(1024, 384), slope1)
-        e = dot_t(h3[2 * q : 2 * q + 4].reshape(512, 384), own2)
-        for p in range(3):
-            at = (p * 3 + q) * 128
-            out[at : at + 128, :] = d[p * 128 : p * 128 + 128].astype(BF)
-            out[1280 + at : 1408 + at, :] = e[p * 128 : p * 128 + 128].astype(BF)
-    both = jnp.zeros((N_ROWS, CH), F4)
-    for j in range(0, 10, 2):
-        two = jnp.concatenate([gm[(j + i) * 128 : (j + i) * 128 + 128, :] for i in range(2)], axis=1).astype(BF)
-        s = dot(fwd[...], jnp.concatenate([two, two], axis=0))
-        for i in range(2):
-            both = both + cross(s[:, i * CH : (i + 1) * CH], spec[:, (j + i) * CH : (j + i + 1) * CH])
-    out[1152:1280, :] = dot(inv_nat[...], three_parts(both)).astype(BF)
-    rows = []
-    for wide in (slope1_wide, own2_wide):
-        b = jnp.sum(wide, axis=0, keepdims=True)
-        high = b.astype(BF).astype(F4)
-        rows += [high, b - high]
-    tail = jnp.concatenate(rows + [jnp.zeros((124, CH), F4)], axis=0)
-    out[2432:2560, :] = tail.astype(BF)
+    def write(first, second):
+        for q in range(3):
+            d = dot_t(m3[q : q + 8].reshape(1024, 384), slope1)
+            e = dot_t(h3[2 * q : 2 * q + 4].reshape(512, 384), own2)
+            for p in range(3):
+                at = (p * 3 + q) * 128
+                first[at : at + 128, :] = d[p * 128 : p * 128 + 128].astype(BF)
+                second[at : at + 128, :] = e[p * 128 : p * 128 + 128].astype(BF)
+        both = jnp.zeros((N_ROWS, CH), F4)
+        for j in range(0, 10, 2):
+            two = jnp.concatenate([gm[(j + i) * 128 : (j + i) * 128 + 128, :] for i in range(2)], axis=1).astype(BF)
+            s = dot(fwd[...], jnp.concatenate([two, two], axis=0))
+            for i in range(2):
+                both = both + cross(s[:, i * CH : (i + 1) * CH], spec[:, (j + i) * CH : (j + i + 1) * CH])
+        first[1152:1280, :] = dot(inv_nat[...], three_parts(both)).astype(BF)
+        rows = []
+        for wide in (slope1_wide, own2_wide):
+            b = jnp.sum(wide, axis=0, keepdims=True)
+            high = b.astype(BF).astype(F4)
+            rows += [high, b - high]
+        tail = jnp.concatenate(rows + [jnp.zeros((124, CH), F4)], axis=0)
+        second[1152:1280, :] = tail.astype(BF)
+
+    core = lax.axis_index("c")
+    pl.when(core == 0)(lambda: write(keep, give))
+    pl.when(core == 1)(lambda: write(give, keep))
 
 
 def finish_kernel(whole, dw1, dw2, dk, db1, db2):
@@ -243,7 +248,7 @@
     fwd, inv, fwd_nat, inv_nat = (jnp.asarray(t, BF) for t in tables())
     w1q, w2q = (w.transpose(1, 0, 2, 3).reshape(3, 384, CH) for w in (w1, w2))
     w1b, w2b = (w.transpose(1, 0, 3, 2).reshape(3, 384, CH) for w in (w1, w2))
-    outs = [((PEERS, 16, CH), BF), ((GRAD_ROWS, CH), BF)]
+    outs = [((PEERS, 16, CH), BF), ((GRAD_ROWS // 2, CH), BF), ((GRAD_ROWS // 2, CH), BF)]
     scratch = [((512, CH), F4), ((1024, CH), F4), ((512, CH), F4),
                ((10, 128, CH), F4), ((256, 10 * CH), BF), ((384, 2 * CH), BF), ((4, 128, CH), F4), ((8, 128, CH), F4),
                ((512, CH), F4), ((128, 10 * CH), F4), ((10, 128, 384), BF), ((8, 128, 384), BF), ((1024, CH), F4),
@@ -261,14 +266,13 @@
         out[i] = total
 
 
-def half_kernel(grads, got, out):
-    rows = pl.ds(pl.multiple_of(lax.axis_index("c") * 1280, 1280), 1280)
-    out[...] = (grads[rows, :].astype(F4) + got[rows, :].astype(F4)).astype(BF)
-
-
-def core_sum(grads):
-    got = lax.ppermute(grads, "c", [(0, 1), (1, 0)])
-    return call(half_kernel, [((GRAD_ROWS // 2, CH), BF)], [], 1 << 20, 8, grads, got)[0]
+def add_kernel(keep, got, out):
+    out[...] = (keep[...].astype(F4) + got[...].astype(F4)).astype(BF)
+
+
+def core_sum(keep, give):
+    got = lax.ppermute(give, "c", [(0, 1), (1, 0)])
+    return call(add_kernel, [((GRAD_ROWS // 2, CH), BF)], [], 1 << 20, 8, keep, got)[0]
 
 
 def summed(got, copies):
@@ -297,10 +301,10 @@
         return lax.ppermute(block, everywhere, [(ring[i], ring[(i + by) % n]) for i in range(n)])
 
     left, right = shifted(own[:, 0:16], 1), shifted(own[:, 0:16], -1)
-    pred_send, grads = local_step(left, own, right, corr_kernel, w1, b1, w2, b2)
+    pred_send, keep, give = local_step(left, own, right, corr_kernel, w1, b1, w2, b2)
     pred_got = lax.all_to_all(pred_send, ROWS_AXES, 0, 0, tiled=True)
     n_near, n_depth, n_plane = (lax.axis_size(axes) for axes in (NEAR_AXES, DEPTH_AXES, PLANE_AXES))
-    part, pred_got = lax.optimization_barrier((core_sum(grads), pred_got))
+    part, pred_got = lax.optimization_barrier((core_sum(keep, give), pred_got))
     part = lax.all_to_all(part.reshape(n_near, 40, CH), NEAR_AXES, 0, 0, tiled=True)
     part = lax.all_to_all(summed(part, n_depth), DEPTH_AXES, 0, 0, tiled=True)
     whole = lax.all_to_all(summed(part, n_plane), PLANE_AXES, 0, 0, tiled=True).reshape(GRAD_ROWS, CH)

time: 131 us -> 129 us (0.985)
  blocking collectives: 66.1 us -> 63.7 us
    all_to_all x1, waiting for transfers between devices: 11.7 us -> 9.7 us  [per_device(): pred_got = lax.all_to_all(pred_send, ROWS_AXES, 0, 0, tiled=True)]
    all_to_all x1, blocking collectives: 16.9 us -> 15 us  [per_device(): part = lax.all_to_all(summed(part, n_depth), DEPTH_AXES, 0, 0, tiled=True)]
    ppermute x1, waiting for transfers between devices: 0.01 us -> 1.59 us  [core_sum(): got = lax.ppermute(give, 'c', [(0, 1), (1, 0)])]
  transfers between devices with their start and end apart: 5 -> 5, of which waited for: 3 -> 4; matrix products, arithmetic and copies ran while one was open for 1% -> 1% of each run, Pallas kernels for 0% -> 0%
where the time goes in v9:
time: 129 us; the launch traced here: 128 us
  blocking collectives  63.7 us (49%)
  starting transfers between devices  26 us (20%)
  waiting for transfers between devices  25.2 us (20%)
  Pallas kernels  8.96 us (7%)
  local copies, waits for them, and re-layouts  3.21 us (2%)
    all_to_all x1, blocking collectives, per_device(): own = lax.all_to_all(send, ROWS_AXES, 0, 0, tiled=True)  34.8 us
    all_to_all x1, blocking collectives, per_device(): part = lax.all_to_all(summed(part, n_depth), DEPTH_AXES, 0, 0, tiled=True)  15 us
    all_to_all x1, blocking collectives, per_device(): lax.all_to_all(part.reshape(n_near, 40, CH), NEAR_AXES, 0, 0, tiled=True)  14 us
    all_to_all x1, waiting for transfers between devices, per_device(): lax.all_to_all(summed(part, n_plane), PLANE_AXES, 0, 0, tiled=True)  11.9 us
    all_to_all x1, starting transfers between devices, per_device(): pred_got = lax.all_to_all(pred_send, ROWS_AXES, 0, 0, tiled=True)  9.97 us
    all_to_all x1, waiting for transfers between devices, per_device(): pred_got = lax.all_to_all(pred_send, ROWS_AXES, 0, 0, tiled=True)  9.7 us
    all_to_all x1, starting transfers between devices, per_device(): lax.all_to_all(summed(part, n_plane), PLANE_AXES, 0, 0, tiled=True)  8.51 us
    pallas_call x5, Pallas kernels, call(): pl.pallas_call(kernel, out_shape=[jax.ShapeDtypeStruct(s, d) for s, d in...  7.75 us
  transfers between devices with their start and end apart: 5, of which 4 were waited for; matrix products, arithmetic and copies ran while one was open for 1% of the time, Pallas kernels for 0%

profile of v9, /device:TPU:1, one launch (start us, length us, event | category | flops | bytes accessed | tf_op | source)
XLA Modules:
  0.0 128.0 jit_solution(18304099240876210975)
XLA Ops:
  0.6 1.2 shard_map.154
  1.9 0.0 copy-start.7
  1.9 34.8 %all_to_all.25.own = bf16[32,32,128]{2,1,0:T(8,128)(2,1)S(1)} all-to-all(bf16[32,32,128]{2,1,0:T(8,128)(2,1)S(1)} %shard_map.154), channel_id=1, replica_groups=mesh['y'=4,'zb'=4,'za'=2,'x'=4,'zh'=2,'c'=2] {'y','zb','za'}, dimensions={0} | all-to-all | bytes 524288 | tf_op jit(solution)/shard_map/all_to_all | solution.py:295
  36.6 1.9 %collective-permute-start = (bf16[32,16,128]{2,1,0:T(8,128)(2,1)S(1)}, bf16[32,16,128]{2,1,0:T(8,128)(2,1)S(1)}, u32[]{:S(2)}, u32[]{:S(2)}) collective-permute-start(bf16[32,16,128]{2,1,0:T(8,128)(2,1)S(1)} %slice.13), channel_id=1, source_target_pairs={{112,240},{240,368},{368,496},{496,480},{480,352},{352,224},{224,9... | collective-permute-start | bytes 393224 | tf_op jit(solution)/shard_map/ppermute | solution.py:301
  38.6 3.7 %collective-permute-start.1 = (bf16[32,16,128]{2,1,0:T(8,128)(2,1)S(1)}, bf16[32,16,128]{2,1,0:T(8,128)(2,1)S(1)}, u32[]{:S(2)}, u32[]{:S(2)}) collective-permute-start(bf16[32,16,128]{2,1,0:T(8,128)(2,1)S(1)} %slice.13), channel_id=1, source_target_pairs={{112,15},{240,112},{368,240},{496,368},{480,496},{352,480},{224,35... | collective-permute-start | bytes 393224 | tf_op jit(solution)/shard_map/ppermute | solution.py:301
  42.2 0.0 copy-done.7
  42.3 0.0 copy-start.8
  42.3 0.9 copy-done.8
  43.2 0.2 copy.35
  43.5 0.0 copy-start
  43.5 0.0 copy-start.3
  43.5 0.0 copy-start.4
  43.5 0.0 copy-start.5
  43.5 0.0 copy-start.6
  43.5 0.2 copy.36
  43.7 0.0 collective-permute-done.left
  43.7 2.0 %collective-permute-done.1.right = bf16[32,16,128]{2,1,0:T(8,128)(2,1)S(1)} collective-permute-done((bf16[32,16,128]{2,1,0:T(8,128)(2,1)S(1)}, bf16[32,16,128]{2,1,0:T(8,128)(2,1)S(1)}, u32[]{:S(2)}, u32[]{:S(2)}) %collective-permute-start.1) | collective-permute-done | bytes 131104 | tf_op jit(solution)/shard_map/ppermute | solution.py:301
  45.7 0.0 copy-start.1
  45.7 0.0 copy-start.2
  45.7 0.0 copy-done
  45.7 0.0 copy-done.3
  45.7 0.0 copy-done.4
  45.7 0.0 copy-done.5
  45.7 0.0 copy-done.6
  45.7 0.6 copy-done.1
  46.4 0.0 copy-done.2
  46.4 5.6 %shard_map.155 = (bf16[32,16,128]{2,1,0:T(8,128)(2,1)}, bf16[1280,128]{1,0:T(8,128)(2,1)S(1)}, bf16[1280,128]{1,0:T(8,128)(2,1)S(1)}) custom-call(bf16[32,16,128]{2,1,0:T(8,128)(2,1)S(1)} %collective-permute-done.left, bf16[32,32,128]{2,1,0:T(8,128)(2,1)S(1)} %all_to_all.25.own, bf16[32,16,128]{2,1,0:T(8,128)(2,1)S(1)} %collective-permute-done.1.right, ...), custom_call_target="tpu_custom_call" | custom-call | flops 3221225472 | bytes 4194304 | tf_op jit(solution)/shard_map/pallas_call | solution.py:236
  52.0 10.0 %all-to-all-start.1 = ((bf16[32,16,128]{2,1,0:T(8,128)(2,1)}), bf16[32,16,128]{2,1,0:T(8,128)(2,1)S(1)}, u32[]{:S(2)}, u32[]{:S(2)}) async-start(bf16[32,16,128]{2,1,0:T(8,128)(2,1)} %get-tuple-element.18), calls=%async_computation.1 | async-start | bytes 262144 | tf_op jit(solution)/shard_map/all_to_all | solution.py:305
  62.0 1.9 %collective-permute-start.2 = (bf16[1280,128]{1,0:T(8,128)(2,1)S(1)}, bf16[1280,128]{1,0:T(8,128)(2,1)S(1)}, u32[]{:S(2)}, u32[]{:S(2)}) collective-permute-start(bf16[1280,128]{1,0:T(8,128)(2,1)S(1)} %get-tuple-element.17), channel_id=1, source_target_pairs={{0,1},{1,0},{2,3},{3,2},{4,5},{5,4},{6,7},{7,6},{8,9},{9,8},{10,11... | collective-permute-start | bytes 983048 | tf_op jit(solution)/shard_map/ppermute | solution.py:274
  63.9 1.6 %collective-permute-done.2.got = bf16[1280,128]{1,0:T(8,128)(2,1)S(1)} collective-permute-done((bf16[1280,128]{1,0:T(8,128)(2,1)S(1)}, bf16[1280,128]{1,0:T(8,128)(2,1)S(1)}, u32[]{:S(2)}, u32[]{:S(2)}) %collective-permute-start.2) | collective-permute-done | bytes 327712 | tf_op jit(solution)/shard_map/ppermute | solution.py:274
  65.5 0.1 shard_map.156
  65.6 9.7 %all-to-all-done.1 = bf16[32,16,128]{2,1,0:T(8,128)(2,1)S(1)} async-done(((bf16[32,16,128]{2,1,0:T(8,128)(2,1)}), bf16[32,16,128]{2,1,0:T(8,128)(2,1)S(1)}, u32[]{:S(2)}, u32[]{:S(2)}) %all-to-all-start.1) | async-done | bytes 131104 | tf_op jit(solution)/shard_map/all_to_all | solution.py:305
  75.3 14.0 %all_to_all.26.got = bf16[32,40,128]{2,1,0:T(8,128)(2,1)S(1)} all-to-all(bf16[32,40,128]{2,1,0:T(8,128)(2,1)S(1)} %bitcast.29), channel_id=1, replica_groups=mesh['y'=4,'zb'=4,'za'=2,'x'=4,'zh'=2,'c'=2] {'x','y','za'}, dimensions={0} | all-to-all | bytes 655360 | tf_op jit(solution)/shard_map/all_to_all | solution.py:308
  89.3 0.1 shard_map.157
  89.3 15.0 %all_to_all.27.got = bf16[8,40,128]{2,1,0:T(8,128)(2,1)S(1)} all-to-all(bf16[8,40,128]{2,1,0:T(8,128)(2,1)S(1)} %shard_map.157), channel_id=1, replica_groups=mesh['y'=4,'zb'=4,'za'=2,'x'=4,'zh'=2,'c'=2] {'zb','zh'}, dimensions={0} | all-to-all | bytes 163840 | tf_op jit(solution)/shard_map/all_to_all | solution.py:309
  104.3 0.9 shard_map.158
  105.2 8.5 %all-to-all-start.4 = ((bf16[64,40,128]{2,1,0:T(8,128)(2,1)}), bf16[64,40,128]{2,1,0:T(8,128)(2,1)S(1)}, u32[]{:S(2)}, u32[]{:S(2)}) async-start(bf16[64,40,128]{2,1,0:T(8,128)(2,1)} %shard_map.158), calls=%async_computation.4 | async-start | bytes 1310720 | tf_op jit(solution)/shard_map/all_to_all | solution.py:310
  113.8 0.1 pad_maximum_fusion
  113.9 0.1 copy.37
  114.1 0.1 copy.38
  114.2 0.1 rev.7
  114.3 0.8 copy.39
  115.0 11.9 %all-to-all-done.4 = bf16[64,40,128]{2,1,0:T(8,128)(2,1)S(1)} async-done(((bf16[64,40,128]{2,1,0:T(8,128)(2,1)}), bf16[64,40,128]{2,1,0:T(8,128)(2,1)S(1)}, u32[]{:S(2)}, u32[]{:S(2)}) %all-to-all-start.4) | async-done | bytes 655392 | tf_op jit(solution)/shard_map/all_to_all | solution.py:310
  127.0 1.1 shard_map.159
  (6 shorter events, 0.1 us)
Async XLA Ops:
  1.9 40.4 %copy-start.7 = (bf16[3,3,128,128]{3,2,1,0:T(8,128)(2,1)S(1)}, bf16[3,3,128,128]{3,2,1,0:T(8,128)(2,1)}, u32[]{:S(2)}) copy-start(bf16[3,3,128,128]{3,2,1,0:T(8,128)(2,1)} %param.13) | copy-start | bytes 884740
  36.6 7.1 %collective-permute-start = (bf16[32,16,128]{2,1,0:T(8,128)(2,1)S(1)}, bf16[32,16,128]{2,1,0:T(8,128)(2,1)S(1)}, u32[]{:S(2)}, u32[]{:S(2)}) collective-permute-start(bf16[32,16,128]{2,1,0:T(8,128)(2,1)S(1)} %slice.13), channel_id=1, source_target_pairs={{112,240},{240,368},{368,496},{496,480},{480,352},{352,224},{224,9... | collective-permute-start | bytes 393224 | tf_op jit(solution)/shard_map/ppermute | solution.py:301
  38.6 7.1 %collective-permute-start.1 = (bf16[32,16,128]{2,1,0:T(8,128)(2,1)S(1)}, bf16[32,16,128]{2,1,0:T(8,128)(2,1)S(1)}, u32[]{:S(2)}, u32[]{:S(2)}) collective-permute-start(bf16[32,16,128]{2,1,0:T(8,128)(2,1)S(1)} %slice.13), channel_id=1, source_target_pairs={{112,15},{240,112},{368,240},{496,368},{480,496},{352,480},{224,35... | collective-permute-start | bytes 393224 | tf_op jit(solution)/shard_map/ppermute | solution.py:301
  42.3 1.0 copy-start.8
  43.5 2.3 %copy-start = (bf16[128,128]{1,0:T(8,128)(2,1)S(1)}, bf16[128,128]{1,0:T(8,128)(2,1)}, u32[]{:S(2)}) copy-start(bf16[128,128]{1,0:T(8,128)(2,1)} %ker.1) | copy-start | bytes 98308
  43.5 2.2 %copy-start.3 = (bf16[128,384]{1,0:T(8,128)(2,1)S(1)}, bf16[128,384]{1,0:T(8,128)(2,1)}, u32[]{:S(2)}) copy-start(bf16[128,384]{1,0:T(8,128)(2,1)} %constant.15.clone.inv) | copy-start | bytes 294916
  43.5 2.2 %copy-start.4 = (bf16[128,384]{1,0:T(8,128)(2,1)S(1)}, bf16[128,384]{1,0:T(8,128)(2,1)}, u32[]{:S(2)}) copy-start(bf16[128,384]{1,0:T(8,128)(2,1)} %constant.17.clone.inv_nat) | copy-start | bytes 294916
  43.5 2.2 %copy-start.5 = (bf16[128,256]{1,0:T(8,128)(2,1)S(1)}, bf16[128,256]{1,0:T(8,128)(2,1)}, u32[]{:S(2)}) copy-start(bf16[128,256]{1,0:T(8,128)(2,1)} %constant.14.clone.fwd) | copy-start | bytes 196612
  43.5 2.2 %copy-start.6 = (bf16[128,256]{1,0:T(8,128)(2,1)S(1)}, bf16[128,256]{1,0:T(8,128)(2,1)}, u32[]{:S(2)}) copy-start(bf16[128,256]{1,0:T(8,128)(2,1)} %constant.16.clone.fwd_nat) | copy-start | bytes 196612
  45.7 0.7 copy-start.1
  45.7 0.7 copy-start.2
  52.0 23.3 %all-to-all-start.1 = ((bf16[32,16,128]{2,1,0:T(8,128)(2,1)}), bf16[32,16,128]{2,1,0:T(8,128)(2,1)S(1)}, u32[]{:S(2)}, u32[]{:S(2)}) async-start(bf16[32,16,128]{2,1,0:T(8,128)(2,1)} %get-tuple-element.18), calls=%async_computation.1 | async-start | bytes 262144 | tf_op jit(solution)/shard_map/all_to_all | solution.py:305
  62.0 3.5 %collective-permute-start.2 = (bf16[1280,128]{1,0:T(8,128)(2,1)S(1)}, bf16[1280,128]{1,0:T(8,128)(2,1)S(1)}, u32[]{:S(2)}, u32[]{:S(2)}) collective-permute-start(bf16[1280,128]{1,0:T(8,128)(2,1)S(1)} %get-tuple-element.17), channel_id=1, source_target_pairs={{0,1},{1,0},{2,3},{3,2},{4,5},{5,4},{6,7},{7,6},{8,9},{9,8},{10,11... | collective-permute-start | bytes 983048 | tf_op jit(solution)/shard_map/ppermute | solution.py:274
  105.2 21.7 %all-to-all-start.4 = ((bf16[64,40,128]{2,1,0:T(8,128)(2,1)}), bf16[64,40,128]{2,1,0:T(8,128)(2,1)S(1)}, u32[]{:S(2)}, u32[]{:S(2)}) async-start(bf16[64,40,128]{2,1,0:T(8,128)(2,1)} %shard_map.158), calls=%async_computation.4 | async-start | bytes 1310720 | tf_op jit(solution)/shard_map/all_to_all | solution.py:310

commit v10 on v8

--- a/solution.py
+++ b/solution.py
@@ -133,7 +133,10 @@
 
 def step_kernel(left, own, right, ker, w1, b1, w2, b2, w1b, w2b, fwd, inv, fwd_nat, inv_nat,
                 pred, out,
-                gl, go, gr, latf, xw, parts, cots, hid, placed, spec, m3, h3, rise1, s3, z3, gh, gm):
+                gl, go, gr, latf, xw, parts, cots, hid, placed, spec, m3, h3, rise1, s3, z3, gh, gm, biases, sems):
+    copies = [pltpu.make_async_copy(b, biases.at[i], sems.at[i]) for i, b in enumerate((b1, b2))]
+    for copy in copies:
+        copy.start()
     for ref, wide in ((left, gl), (own, go), (right, gr)):
         wide[...] = ref[...].reshape(wide.shape).astype(F4)
     lat_from = ([(gl, 4 * j, 16) for j in (1, 2, 3)] + [(go, 4 * j, 32) for j in range(4)]
@@ -158,8 +161,10 @@
             mixed = (latf[j + i] + corr[:, i * CH : (i + 1) * CH]).astype(BF).astype(F4)
             latf[j + i] = mixed
             put_turned(m3, j + i, mixed, (-1, 0, 1))
+    for copy in copies:
+        copy.wait()
     for j in range(0, 8, 4):
-        v = b1[...]
+        v = biases[0]
         for q in range(3):
             v = v + dot(m3[j + q : j + q + 4].reshape(512, 384), w1[q])
         g = jax.nn.sigmoid(v)
@@ -169,7 +174,7 @@
             h = (latf[j + i + 1] + vg[i * 128 : i * 128 + 128]).astype(BF).astype(F4)
             hid[j + i] = h
             put_turned(h3, j + i, h, (-2, 0, 2))
-    v = b2[...]
+    v = biases[1]
     for q in range(3):
         v = v + dot(h3[2 * q : 2 * q + 4].reshape(512, 384), w2[q])
     g = jax.nn.sigmoid(v)
@@ -227,13 +232,13 @@
     db2[...] = tail[2:3] + tail[3:4]
 
 
-def call(kernel, outs, scratch, flops, mib, *args):
+def call(kernel, outs, scratch, flops, mib, *args, hbm=(), sems=0):
     return pl.pallas_call(
         kernel,
         out_shape=[jax.ShapeDtypeStruct(s, d) for s, d in outs],
-        in_specs=[VMEM] * len(args),
+        in_specs=[pl.BlockSpec(memory_space=pltpu.HBM) if i in hbm else VMEM for i in range(len(args))],
         out_specs=[VMEM] * len(outs),
-        scratch_shapes=[pltpu.VMEM(s, d) for s, d in scratch],
+        scratch_shapes=[pltpu.VMEM(s, d) for s, d in scratch] + [pltpu.SemaphoreType.DMA((sems,))] * (sems > 0),
         compiler_params=pltpu.CompilerParams(vmem_limit_bytes=mib << 20),
         cost_estimate=pl.CostEstimate(flops=flops, bytes_accessed=4 << 20, transcendentals=0),
     )(*args)
@@ -247,9 +252,10 @@
     scratch = [((512, CH), F4), ((1024, CH), F4), ((512, CH), F4),
                ((10, 128, CH), F4), ((256, 10 * CH), BF), ((384, 2 * CH), BF), ((4, 128, CH), F4), ((8, 128, CH), F4),
                ((512, CH), F4), ((128, 10 * CH), F4), ((10, 128, 384), BF), ((8, 128, 384), BF), ((1024, CH), F4),
-               ((4, 128, 384), BF), ((8, 128, 384), BF), ((1024, CH), F4), ((1280, CH), F4)]
+               ((4, 128, 384), BF), ((8, 128, 384), BF), ((1024, CH), F4), ((1280, CH), F4), ((2, 1, CH), F4)]
+    b1, b2 = (pltpu.with_memory_space_constraint(b.reshape(1, CH), pltpu.HBM) for b in (b1, b2))
     return call(step_kernel, outs, scratch, 3 << 30, 24, left, own, right, ker,
-                w1q, b1.reshape(1, CH), w2q, b2.reshape(1, CH), w1b, w2b, fwd, inv, fwd_nat, inv_nat)
+                w1q, b1, w2q, b2, w1b, w2b, fwd, inv, fwd_nat, inv_nat, hbm=(5, 7), sems=2)
 
 
 def sum_kernel(got, out):
@@ -263,12 +269,14 @@
 
 def half_kernel(grads, got, out):
     rows = pl.ds(pl.multiple_of(lax.axis_index("c") * 1280, 1280), 1280)
-    out[...] = (grads[rows, :].astype(F4) + got[rows, :].astype(F4)).astype(BF)
+    out[...] = (grads[rows, :].astype(F4) + got[...].astype(F4)).astype(BF)
 
 
 def core_sum(grads):
-    got = lax.ppermute(grads, "c", [(0, 1), (1, 0)])
-    return call(half_kernel, [((GRAD_ROWS // 2, CH), BF)], [], 1 << 20, 8, grads, got)[0]
+    half = GRAD_ROWS // 2
+    give = lax.dynamic_slice_in_dim(grads, (1 - lax.axis_index("c")) * half, half)
+    got = lax.ppermute(give, "c", [(0, 1), (1, 0)])
+    return call(half_kernel, [((half, CH), BF)], [], 1 << 20, 8, grads, got)[0]
 
 
 def summed(got, copies):

time: 131 us -> 128 us (0.977)
  blocking collectives: 66.1 us -> 63.8 us
    all_to_all x1, waiting for transfers between devices: 11.7 us -> 9.65 us  [per_device(): pred_got = lax.all_to_all(pred_send, ROWS_AXES, 0, 0, tiled=True)]
    all_to_all x1, blocking collectives: 16.9 us -> 15 us  [per_device(): part = lax.all_to_all(summed(part, n_depth), DEPTH_AXES, 0, 0, tiled=True)]
    ppermute x1, waiting for transfers between devices: 0.01 us -> 1.59 us  [core_sum(): got = lax.ppermute(give, 'c', [(0, 1), (1, 0)])]
  transfers between devices with their start and end apart: 5 -> 5, of which waited for: 3 -> 4; matrix products, arithmetic and copies ran while one was open for 1% -> 1% of each run, Pallas kernels for 0% -> 0%
where the time goes in v10:
time: 128 us; the launch traced here: 127 us
  blocking collectives  63.8 us (50%)
  starting transfers between devices  25.8 us (20%)
  waiting for transfers between devices  25.1 us (20%)
  Pallas kernels  8.86 us (7%)
  local copies, waits for them, and re-layouts  2.61 us (2%)
    all_to_all x1, blocking collectives, per_device(): own = lax.all_to_all(send, ROWS_AXES, 0, 0, tiled=True)  34.8 us
    all_to_all x1, blocking collectives, per_device(): part = lax.all_to_all(summed(part, n_depth), DEPTH_AXES, 0, 0, tiled=True)  15 us
    all_to_all x1, blocking collectives, per_device(): lax.all_to_all(part.reshape(n_near, 40, CH), NEAR_AXES, 0, 0, tiled=True)  14 us
    all_to_all x1, waiting for transfers between devices, per_device(): lax.all_to_all(summed(part, n_plane), PLANE_AXES, 0, 0, tiled=True)  11.9 us
    all_to_all x1, starting transfers between devices, per_device(): pred_got = lax.all_to_all(pred_send, ROWS_AXES, 0, 0, tiled=True)  9.99 us
    all_to_all x1, waiting for transfers between devices, per_device(): pred_got = lax.all_to_all(pred_send, ROWS_AXES, 0, 0, tiled=True)  9.65 us
    all_to_all x1, starting transfers between devices, per_device(): lax.all_to_all(summed(part, n_plane), PLANE_AXES, 0, 0, tiled=True)  8.3 us
    pallas_call x5, Pallas kernels, call(): pl.pallas_call(kernel, out_shape=[jax.ShapeDtypeStruct(s, d) for s, d in...  7.65 us
  transfers between devices with their start and end apart: 5, of which 4 were waited for; matrix products, arithmetic and copies ran while one was open for 1% of the time, Pallas kernels for 0%

profile of v10, /device:TPU:1, one launch (start us, length us, event | category | flops | bytes accessed | tf_op | source)
XLA Modules:
  0.0 127.1 jit_solution(874704219370051524)
XLA Ops:
  0.6 1.2 shard_map.154
  1.9 0.0 copy-start.5
  1.9 34.8 %all_to_all.25.own = bf16[32,32,128]{2,1,0:T(8,128)(2,1)S(1)} all-to-all(bf16[32,32,128]{2,1,0:T(8,128)(2,1)S(1)} %shard_map.154), channel_id=1, replica_groups=mesh['y'=4,'zb'=4,'za'=2,'x'=4,'zh'=2,'c'=2] {'y','zb','za'}, dimensions={0} | all-to-all | bytes 524288 | tf_op jit(solution)/shard_map/all_to_all | solution.py:299
  36.6 1.9 %collective-permute-start = (bf16[32,16,128]{2,1,0:T(8,128)(2,1)S(1)}, bf16[32,16,128]{2,1,0:T(8,128)(2,1)S(1)}, u32[]{:S(2)}, u32[]{:S(2)}) collective-permute-start(bf16[32,16,128]{2,1,0:T(8,128)(2,1)S(1)} %slice.13), channel_id=1, source_target_pairs={{112,240},{240,368},{368,496},{496,480},{480,352},{352,224},{224,9... | collective-permute-start | bytes 393224 | tf_op jit(solution)/shard_map/ppermute | solution.py:305
  38.6 3.7 %collective-permute-start.1 = (bf16[32,16,128]{2,1,0:T(8,128)(2,1)S(1)}, bf16[32,16,128]{2,1,0:T(8,128)(2,1)S(1)}, u32[]{:S(2)}, u32[]{:S(2)}) collective-permute-start(bf16[32,16,128]{2,1,0:T(8,128)(2,1)S(1)} %slice.13), channel_id=1, source_target_pairs={{112,15},{240,112},{368,240},{496,368},{480,496},{352,480},{224,35... | collective-permute-start | bytes 393224 | tf_op jit(solution)/shard_map/ppermute | solution.py:305
  42.2 0.0 copy-done.5
  42.3 0.0 copy-start.6
  42.3 0.9 copy-done.6
  43.2 0.2 copy.35
  43.5 0.0 copy-start
  43.5 0.0 copy-start.1
  43.5 0.0 copy-start.2
  43.5 0.0 copy-start.3
  43.5 0.0 copy-start.4
  43.5 0.2 copy.36
  43.7 0.0 collective-permute-done.left
  43.8 2.0 %collective-permute-done.1.right = bf16[32,16,128]{2,1,0:T(8,128)(2,1)S(1)} collective-permute-done((bf16[32,16,128]{2,1,0:T(8,128)(2,1)S(1)}, bf16[32,16,128]{2,1,0:T(8,128)(2,1)S(1)}, u32[]{:S(2)}, u32[]{:S(2)}) %collective-permute-start.1) | collective-permute-done | bytes 131104 | tf_op jit(solution)/shard_map/ppermute | solution.py:305
  45.7 0.0 copy-done
  45.7 0.0 copy-done.1
  45.7 0.0 copy-done.2
  45.7 0.0 copy-done.3
  45.7 0.0 copy-done.4
  45.7 5.5 %shard_map.155 = (bf16[32,16,128]{2,1,0:T(8,128)(2,1)}, bf16[2560,128]{1,0:T(8,128)(2,1)S(1)}) custom-call(bf16[32,16,128]{2,1,0:T(8,128)(2,1)S(1)} %collective-permute-done.left, bf16[32,32,128]{2,1,0:T(8,128)(2,1)S(1)} %all_to_all.25.own, bf16[32,16,128]{2,1,0:T(8,128)(2,1)S(1)} %collective-permute-done.1.right, bf16[128,128]{1,0:T(8,128)(2,1)S(1)} %copy-done, ...), custom_call_target="tpu_custom_call" | custom-call | flops 3221225472 | bytes 4194304 | tf_op jit(solution)/shard_map/pallas_call | solution.py:236
  51.3 10.0 %all-to-all-start.1 = ((bf16[32,16,128]{2,1,0:T(8,128)(2,1)}), bf16[32,16,128]{2,1,0:T(8,128)(2,1)S(1)}, u32[]{:S(2)}, u32[]{:S(2)}) async-start(bf16[32,16,128]{2,1,0:T(8,128)(2,1)} %get-tuple-element.16), calls=%async_computation.1 | async-start | bytes 262144 | tf_op jit(solution)/shard_map/all_to_all | solution.py:309
  61.3 1.9 %collective-permute-start.2 = (bf16[1280,128]{1,0:T(8,128)(2,1)S(1)}, bf16[1280,128]{1,0:T(8,128)(2,1)S(1)}, u32[]{:S(2)}, u32[]{:S(2)}) collective-permute-start(bf16[1280,128]{1,0:T(8,128)(2,1)S(1)} %constant_dynamic-slice_fusion), channel_id=1, source_target_pairs={{0,1},{1,0},{2,3},{3,2},{4,5},{5,4},{6,7},{7,6},{8,9},{9,8},{10,11... | collective-permute-start | bytes 983048 | tf_op jit(solution)/shard_map/ppermute | solution.py:278
  63.2 1.6 %collective-permute-done.2.got = bf16[1280,128]{1,0:T(8,128)(2,1)S(1)} collective-permute-done((bf16[1280,128]{1,0:T(8,128)(2,1)S(1)}, bf16[1280,128]{1,0:T(8,128)(2,1)S(1)}, u32[]{:S(2)}, u32[]{:S(2)}) %collective-permute-start.2) | collective-permute-done | bytes 327712 | tf_op jit(solution)/shard_map/ppermute | solution.py:278
  64.8 0.1 shard_map.156
  64.9 9.6 %all-to-all-done.1 = bf16[32,16,128]{2,1,0:T(8,128)(2,1)S(1)} async-done(((bf16[32,16,128]{2,1,0:T(8,128)(2,1)}), bf16[32,16,128]{2,1,0:T(8,128)(2,1)S(1)}, u32[]{:S(2)}, u32[]{:S(2)}) %all-to-all-start.1) | async-done | bytes 131104 | tf_op jit(solution)/shard_map/all_to_all | solution.py:309
  74.6 14.0 %all_to_all.26.got = bf16[32,40,128]{2,1,0:T(8,128)(2,1)S(1)} all-to-all(bf16[32,40,128]{2,1,0:T(8,128)(2,1)S(1)} %bitcast.29), channel_id=1, replica_groups=mesh['y'=4,'zb'=4,'za'=2,'x'=4,'zh'=2,'c'=2] {'x','y','za'}, dimensions={0} | all-to-all | bytes 655360 | tf_op jit(solution)/shard_map/all_to_all | solution.py:312
  88.5 0.1 shard_map.157
  88.6 15.0 %all_to_all.27.got = bf16[8,40,128]{2,1,0:T(8,128)(2,1)S(1)} all-to-all(bf16[8,40,128]{2,1,0:T(8,128)(2,1)S(1)} %shard_map.157), channel_id=1, replica_groups=mesh['y'=4,'zb'=4,'za'=2,'x'=4,'zh'=2,'c'=2] {'zb','zh'}, dimensions={0} | all-to-all | bytes 163840 | tf_op jit(solution)/shard_map/all_to_all | solution.py:313
  103.6 0.9 shard_map.158
  104.5 8.3 %all-to-all-start.4 = ((bf16[64,40,128]{2,1,0:T(8,128)(2,1)}), bf16[64,40,128]{2,1,0:T(8,128)(2,1)S(1)}, u32[]{:S(2)}, u32[]{:S(2)}) async-start(bf16[64,40,128]{2,1,0:T(8,128)(2,1)} %shard_map.158), calls=%async_computation.4 | async-start | bytes 1310720 | tf_op jit(solution)/shard_map/all_to_all | solution.py:314
  112.9 0.1 pad_maximum_fusion
  113.0 0.1 copy.37
  113.2 0.1 copy.38
  113.3 0.1 rev.7
  113.4 0.8 copy.39
  114.1 11.9 %all-to-all-done.4 = bf16[64,40,128]{2,1,0:T(8,128)(2,1)S(1)} async-done(((bf16[64,40,128]{2,1,0:T(8,128)(2,1)}), bf16[64,40,128]{2,1,0:T(8,128)(2,1)S(1)}, u32[]{:S(2)}, u32[]{:S(2)}) %all-to-all-start.4) | async-done | bytes 655392 | tf_op jit(solution)/shard_map/all_to_all | solution.py:314
  126.0 1.1 shard_map.159
  (7 shorter events, 0.2 us)
Async XLA Ops:
  1.9 40.4 %copy-start.5 = (bf16[3,3,128,128]{3,2,1,0:T(8,128)(2,1)S(1)}, bf16[3,3,128,128]{3,2,1,0:T(8,128)(2,1)}, u32[]{:S(2)}) copy-start(bf16[3,3,128,128]{3,2,1,0:T(8,128)(2,1)} %param.13) | copy-start | bytes 884740
  36.6 7.1 %collective-permute-start = (bf16[32,16,128]{2,1,0:T(8,128)(2,1)S(1)}, bf16[32,16,128]{2,1,0:T(8,128)(2,1)S(1)}, u32[]{:S(2)}, u32[]{:S(2)}) collective-permute-start(bf16[32,16,128]{2,1,0:T(8,128)(2,1)S(1)} %slice.13), channel_id=1, source_target_pairs={{112,240},{240,368},{368,496},{496,480},{480,352},{352,224},{224,9... | collective-permute-start | bytes 393224 | tf_op jit(solution)/shard_map/ppermute | solution.py:305
  38.6 7.1 %collective-permute-start.1 = (bf16[32,16,128]{2,1,0:T(8,128)(2,1)S(1)}, bf16[32,16,128]{2,1,0:T(8,128)(2,1)S(1)}, u32[]{:S(2)}, u32[]{:S(2)}) collective-permute-start(bf16[32,16,128]{2,1,0:T(8,128)(2,1)S(1)} %slice.13), channel_id=1, source_target_pairs={{112,15},{240,112},{368,240},{496,368},{480,496},{352,480},{224,35... | collective-permute-start | bytes 393224 | tf_op jit(solution)/shard_map/ppermute | solution.py:305
  42.3 1.0 copy-start.6
  43.5 2.2 %copy-start = (bf16[128,128]{1,0:T(8,128)(2,1)S(1)}, bf16[128,128]{1,0:T(8,128)(2,1)}, u32[]{:S(2)}) copy-start(bf16[128,128]{1,0:T(8,128)(2,1)} %ker.1) | copy-start | bytes 98308
  43.5 2.2 %copy-start.1 = (bf16[128,384]{1,0:T(8,128)(2,1)S(1)}, bf16[128,384]{1,0:T(8,128)(2,1)}, u32[]{:S(2)}) copy-start(bf16[128,384]{1,0:T(8,128)(2,1)} %constant.23.clone.inv) | copy-start | bytes 294916
  43.5 2.2 %copy-start.2 = (bf16[128,384]{1,0:T(8,128)(2,1)S(1)}, bf16[128,384]{1,0:T(8,128)(2,1)}, u32[]{:S(2)}) copy-start(bf16[128,384]{1,0:T(8,128)(2,1)} %constant.25.clone.inv_nat) | copy-start | bytes 294916
  43.5 2.2 %copy-start.3 = (bf16[128,256]{1,0:T(8,128)(2,1)S(1)}, bf16[128,256]{1,0:T(8,128)(2,1)}, u32[]{:S(2)}) copy-start(bf16[128,256]{1,0:T(8,128)(2,1)} %constant.22.clone.fwd) | copy-start | bytes 196612
  43.5 2.2 %copy-start.4 = (bf16[128,256]{1,0:T(8,128)(2,1)S(1)}, bf16[128,256]{1,0:T(8,128)(2,1)}, u32[]{:S(2)}) copy-start(bf16[128,256]{1,0:T(8,128)(2,1)} %constant.24.clone.fwd_nat) | copy-start | bytes 196612
  51.3 23.3 %all-to-all-start.1 = ((bf16[32,16,128]{2,1,0:T(8,128)(2,1)}), bf16[32,16,128]{2,1,0:T(8,128)(2,1)S(1)}, u32[]{:S(2)}, u32[]{:S(2)}) async-start(bf16[32,16,128]{2,1,0:T(8,128)(2,1)} %get-tuple-element.16), calls=%async_computation.1 | async-start | bytes 262144 | tf_op jit(solution)/shard_map/all_to_all | solution.py:309
  61.3 3.5 %collective-permute-start.2 = (bf16[1280,128]{1,0:T(8,128)(2,1)S(1)}, bf16[1280,128]{1,0:T(8,128)(2,1)S(1)}, u32[]{:S(2)}, u32[]{:S(2)}) collective-permute-start(bf16[1280,128]{1,0:T(8,128)(2,1)S(1)} %constant_dynamic-slice_fusion), channel_id=1, source_target_pairs={{0,1},{1,0},{2,3},{3,2},{4,5},{5,4},{6,7},{7,6},{8,9},{9,8},{10,11... | collective-permute-start | bytes 983048 | tf_op jit(solution)/shard_map/ppermute | solution.py:278
  104.5 21.5 %all-to-all-start.4 = ((bf16[64,40,128]{2,1,0:T(8,128)(2,1)}), bf16[64,40,128]{2,1,0:T(8,128)(2,1)S(1)}, u32[]{:S(2)}, u32[]{:S(2)}) async-start(bf16[64,40,128]{2,1,0:T(8,128)(2,1)} %shard_map.158), calls=%async_computation.4 | async-start | bytes 1310720 | tf_op jit(solution)/shard_map/all_to_all | solution.py:314

commit v11 on v8

--- a/solution.py
+++ b/solution.py
@@ -131,7 +131,7 @@
     return jnp.concatenate([ref[pl.ds(start + rr, 32, stride=stride), :] for rr in range(4)], axis=0)
 
 
-def step_kernel(left, own, right, ker, w1, b1, w2, b2, w1b, w2b, fwd, inv, fwd_nat, inv_nat,
+def step_kernel(left, own, right, ker, biases, w1, w2, w1b, w2b, fwd, inv, fwd_nat, inv_nat,
                 pred, out,
                 gl, go, gr, latf, xw, parts, cots, hid, placed, spec, m3, h3, rise1, s3, z3, gh, gm):
     for ref, wide in ((left, gl), (own, go), (right, gr)):
@@ -159,7 +159,7 @@
             latf[j + i] = mixed
             put_turned(m3, j + i, mixed, (-1, 0, 1))
     for j in range(0, 8, 4):
-        v = b1[...]
+        v = biases[0:1, :]
         for q in range(3):
             v = v + dot(m3[j + q : j + q + 4].reshape(512, 384), w1[q])
         g = jax.nn.sigmoid(v)
@@ -169,7 +169,7 @@
             h = (latf[j + i + 1] + vg[i * 128 : i * 128 + 128]).astype(BF).astype(F4)
             hid[j + i] = h
             put_turned(h3, j + i, h, (-2, 0, 2))
-    v = b2[...]
+    v = biases[1:2, :]
     for q in range(3):
         v = v + dot(h3[2 * q : 2 * q + 4].reshape(512, 384), w2[q])
     g = jax.nn.sigmoid(v)
@@ -249,7 +249,7 @@
                ((512, CH), F4), ((128, 10 * CH), F4), ((10, 128, 384), BF), ((8, 128, 384), BF), ((1024, CH), F4),
                ((4, 128, 384), BF), ((8, 128, 384), BF), ((1024, CH), F4), ((1280, CH), F4)]
     return call(step_kernel, outs, scratch, 3 << 30, 24, left, own, right, ker,
-                w1q, b1.reshape(1, CH), w2q, b2.reshape(1, CH), w1b, w2b, fwd, inv, fwd_nat, inv_nat)
+                jnp.stack([b1, b2]), w1q, w2q, w1b, w2b, fwd, inv, fwd_nat, inv_nat)
 
 
 def sum_kernel(got, out):
@@ -263,12 +263,14 @@
 
 def half_kernel(grads, got, out):
     rows = pl.ds(pl.multiple_of(lax.axis_index("c") * 1280, 1280), 1280)
-    out[...] = (grads[rows, :].astype(F4) + got[rows, :].astype(F4)).astype(BF)
+    out[...] = (grads[rows, :].astype(F4) + got[...].astype(F4)).astype(BF)
 
 
 def core_sum(grads):
-    got = lax.ppermute(grads, "c", [(0, 1), (1, 0)])
-    return call(half_kernel, [((GRAD_ROWS // 2, CH), BF)], [], 1 << 20, 8, grads, got)[0]
+    half = GRAD_ROWS // 2
+    give = lax.dynamic_slice_in_dim(grads, (1 - lax.axis_index("c")) * half, half)
+    got = lax.ppermute(give, "c", [(0, 1), (1, 0)])
+    return call(half_kernel, [((half, CH), BF)], [], 1 << 20, 8, grads, got)[0]
 
 
 def summed(got, copies):

time: 131 us -> 127 us (0.969)
  blocking collectives: 66.1 us -> 63.8 us
    all_to_all x1, waiting for transfers between devices: 11.7 us -> 9.65 us  [per_device(): pred_got = lax.all_to_all(pred_send, ROWS_AXES, 0, 0, tiled=True)]
    all_to_all x1, blocking collectives: 16.9 us -> 15 us  [per_device(): part = lax.all_to_all(summed(part, n_depth), DEPTH_AXES, 0, 0, tiled=True)]
    ppermute x1, waiting for transfers between devices: 0.01 us -> 1.59 us  [core_sum(): got = lax.ppermute(give, 'c', [(0, 1), (1, 0)])]
  transfers between devices with their start and end apart: 5 -> 5, of which waited for: 3 -> 4; matrix products, arithmetic and copies ran while one was open for 1% -> 1% of each run, Pallas kernels for 0% -> 0%
where the time goes in v11:
time: 127 us; the launch traced here: 126 us
  blocking collectives  63.8 us (50%)
  starting transfers between devices  25.8 us (20%)
  waiting for transfers between devices  24.4 us (19%)
  Pallas kernels  8.13 us (6%)
  local copies, waits for them, and re-layouts  3.27 us (3%)
    all_to_all x1, blocking collectives, per_device(): own = lax.all_to_all(send, ROWS_AXES, 0, 0, tiled=True)  34.8 us
    all_to_all x1, blocking collectives, per_device(): part = lax.all_to_all(summed(part, n_depth), DEPTH_AXES, 0, 0, tiled=True)  15 us
    all_to_all x1, blocking collectives, per_device(): lax.all_to_all(part.reshape(n_near, 40, CH), NEAR_AXES, 0, 0, tiled=True)  14 us
    all_to_all x1, waiting for transfers between devices, per_device(): lax.all_to_all(summed(part, n_plane), PLANE_AXES, 0, 0, tiled=True)  11.9 us
    all_to_all x1, starting transfers between devices, per_device(): pred_got = lax.all_to_all(pred_send, ROWS_AXES, 0, 0, tiled=True)  9.99 us
    all_to_all x1, waiting for transfers between devices, per_device(): pred_got = lax.all_to_all(pred_send, ROWS_AXES, 0, 0, tiled=True)  9.65 us
    all_to_all x1, starting transfers between devices, per_device(): lax.all_to_all(summed(part, n_plane), PLANE_AXES, 0, 0, tiled=True)  8.3 us
    pallas_call x5, Pallas kernels, call(): pl.pallas_call(kernel, out_shape=[jax.ShapeDtypeStruct(s, d) for s, d in...  6.91 us
  transfers between devices with their start and end apart: 5, of which 4 were waited for; matrix products, arithmetic and copies ran while one was open for 1% of the time, Pallas kernels for 0%

profile of v11, /device:TPU:1, one launch (start us, length us, event | category | flops | bytes accessed | tf_op | source)
XLA Modules:
  0.0 126.4 jit_solution(17556940085688602172)
XLA Ops:
  0.6 1.2 shard_map.154
  1.9 0.0 copy-start.5
  1.9 34.8 %all_to_all.25.own = bf16[32,32,128]{2,1,0:T(8,128)(2,1)S(1)} all-to-all(bf16[32,32,128]{2,1,0:T(8,128)(2,1)S(1)} %shard_map.154), channel_id=1, replica_groups=mesh['y'=4,'zb'=4,'za'=2,'x'=4,'zh'=2,'c'=2] {'y','zb','za'}, dimensions={0} | all-to-all | bytes 524288 | tf_op jit(solution)/shard_map/all_to_all | solution.py:293
  36.6 1.9 %collective-permute-start = (bf16[32,16,128]{2,1,0:T(8,128)(2,1)S(1)}, bf16[32,16,128]{2,1,0:T(8,128)(2,1)S(1)}, u32[]{:S(2)}, u32[]{:S(2)}) collective-permute-start(bf16[32,16,128]{2,1,0:T(8,128)(2,1)S(1)} %slice.13), channel_id=1, source_target_pairs={{112,240},{240,368},{368,496},{496,480},{480,352},{352,224},{224,9... | collective-permute-start | bytes 393224 | tf_op jit(solution)/shard_map/ppermute | solution.py:299
  38.6 3.7 %collective-permute-start.1 = (bf16[32,16,128]{2,1,0:T(8,128)(2,1)S(1)}, bf16[32,16,128]{2,1,0:T(8,128)(2,1)S(1)}, u32[]{:S(2)}, u32[]{:S(2)}) collective-permute-start(bf16[32,16,128]{2,1,0:T(8,128)(2,1)S(1)} %slice.13), channel_id=1, source_target_pairs={{112,15},{240,112},{368,240},{496,368},{480,496},{352,480},{224,35... | collective-permute-start | bytes 393224 | tf_op jit(solution)/shard_map/ppermute | solution.py:299
  42.2 0.0 copy-done.5
  42.3 0.0 copy-start.6
  42.3 0.9 copy-done.6
  43.2 0.2 copy.35
  43.5 0.0 copy-start
  43.5 0.0 copy-start.1
  43.5 0.0 copy-start.2
  43.5 0.0 copy-start.3
  43.5 0.0 copy-start.4
  43.5 0.2 copy.36
  43.7 0.0 copy-start.7
  43.8 0.0 copy-start.8
  43.8 0.6 copy-done.7
  44.4 0.0 copy-done.8
  44.4 0.0 collective-permute-done.left
  44.4 1.3 %collective-permute-done.1.right = bf16[32,16,128]{2,1,0:T(8,128)(2,1)S(1)} collective-permute-done((bf16[32,16,128]{2,1,0:T(8,128)(2,1)S(1)}, bf16[32,16,128]{2,1,0:T(8,128)(2,1)S(1)}, u32[]{:S(2)}, u32[]{:S(2)}) %collective-permute-start.1) | collective-permute-done | bytes 131104 | tf_op jit(solution)/shard_map/ppermute | solution.py:299
  45.7 0.0 copy-done
  45.7 0.0 copy-done.1
  45.7 0.0 copy-done.2
  45.7 0.0 copy-done.3
  45.7 0.0 copy-done.4
  45.7 4.8 %shard_map.155 = (bf16[32,16,128]{2,1,0:T(8,128)(2,1)}, bf16[2560,128]{1,0:T(8,128)(2,1)S(1)}) custom-call(bf16[32,16,128]{2,1,0:T(8,128)(2,1)S(1)} %collective-permute-done.left, bf16[32,32,128]{2,1,0:T(8,128)(2,1)S(1)} %all_to_all.25.own, bf16[32,16,128]{2,1,0:T(8,128)(2,1)S(1)} %collective-permute-done.1.right, bf16[128,128]{1,0:T(8,128)(2,1)S(1)} %copy-done, ...), custom_call_target="tpu_custom_call" | custom-call | flops 3221225472 | bytes 4194304 | tf_op jit(solution)/shard_map/pallas_call | solution.py:231
  50.5 10.0 %all-to-all-start.1 = ((bf16[32,16,128]{2,1,0:T(8,128)(2,1)}), bf16[32,16,128]{2,1,0:T(8,128)(2,1)S(1)}, u32[]{:S(2)}, u32[]{:S(2)}) async-start(bf16[32,16,128]{2,1,0:T(8,128)(2,1)} %get-tuple-element.16), calls=%async_computation.1 | async-start | bytes 262144 | tf_op jit(solution)/shard_map/all_to_all | solution.py:303
  60.6 1.9 %collective-permute-start.2 = (bf16[1280,128]{1,0:T(8,128)(2,1)S(1)}, bf16[1280,128]{1,0:T(8,128)(2,1)S(1)}, u32[]{:S(2)}, u32[]{:S(2)}) collective-permute-start(bf16[1280,128]{1,0:T(8,128)(2,1)S(1)} %constant_dynamic-slice_fusion), channel_id=1, source_target_pairs={{0,1},{1,0},{2,3},{3,2},{4,5},{5,4},{6,7},{7,6},{8,9},{9,8},{10,11... | collective-permute-start | bytes 983048 | tf_op jit(solution)/shard_map/ppermute | solution.py:272
  62.5 1.6 %collective-permute-done.2.got = bf16[1280,128]{1,0:T(8,128)(2,1)S(1)} collective-permute-done((bf16[1280,128]{1,0:T(8,128)(2,1)S(1)}, bf16[1280,128]{1,0:T(8,128)(2,1)S(1)}, u32[]{:S(2)}, u32[]{:S(2)}) %collective-permute-start.2) | collective-permute-done | bytes 327712 | tf_op jit(solution)/shard_map/ppermute | solution.py:272
  64.1 0.1 shard_map.156
  64.2 9.6 %all-to-all-done.1 = bf16[32,16,128]{2,1,0:T(8,128)(2,1)S(1)} async-done(((bf16[32,16,128]{2,1,0:T(8,128)(2,1)}), bf16[32,16,128]{2,1,0:T(8,128)(2,1)S(1)}, u32[]{:S(2)}, u32[]{:S(2)}) %all-to-all-start.1) | async-done | bytes 131104 | tf_op jit(solution)/shard_map/all_to_all | solution.py:303
  73.8 14.0 %all_to_all.26.got = bf16[32,40,128]{2,1,0:T(8,128)(2,1)S(1)} all-to-all(bf16[32,40,128]{2,1,0:T(8,128)(2,1)S(1)} %bitcast.29), channel_id=1, replica_groups=mesh['y'=4,'zb'=4,'za'=2,'x'=4,'zh'=2,'c'=2] {'x','y','za'}, dimensions={0} | all-to-all | bytes 655360 | tf_op jit(solution)/shard_map/all_to_all | solution.py:306
  87.8 0.1 shard_map.157
  87.9 15.0 %all_to_all.27.got = bf16[8,40,128]{2,1,0:T(8,128)(2,1)S(1)} all-to-all(bf16[8,40,128]{2,1,0:T(8,128)(2,1)S(1)} %shard_map.157), channel_id=1, replica_groups=mesh['y'=4,'zb'=4,'za'=2,'x'=4,'zh'=2,'c'=2] {'zb','zh'}, dimensions={0} | all-to-all | bytes 163840 | tf_op jit(solution)/shard_map/all_to_all | solution.py:307
  102.9 0.9 shard_map.158
  103.8 8.3 %all-to-all-start.4 = ((bf16[64,40,128]{2,1,0:T(8,128)(2,1)}), bf16[64,40,128]{2,1,0:T(8,128)(2,1)S(1)}, u32[]{:S(2)}, u32[]{:S(2)}) async-start(bf16[64,40,128]{2,1,0:T(8,128)(2,1)} %shard_map.158), calls=%async_computation.4 | async-start | bytes 1310720 | tf_op jit(solution)/shard_map/all_to_all | solution.py:308
  112.2 0.1 pad_maximum_fusion
  112.3 0.1 copy.37
  112.4 0.1 copy.38
  112.5 0.1 rev.7
  112.6 0.8 copy.39
  113.4 11.9 %all-to-all-done.4 = bf16[64,40,128]{2,1,0:T(8,128)(2,1)S(1)} async-done(((bf16[64,40,128]{2,1,0:T(8,128)(2,1)}), bf16[64,40,128]{2,1,0:T(8,128)(2,1)S(1)}, u32[]{:S(2)}, u32[]{:S(2)}) %all-to-all-start.4) | async-done | bytes 655392 | tf_op jit(solution)/shard_map/all_to_all | solution.py:308
  125.3 1.1 shard_map.159
  (8 shorter events, 0.2 us)
Async XLA Ops:
  1.9 40.4 %copy-start.5 = (bf16[3,3,128,128]{3,2,1,0:T(8,128)(2,1)S(1)}, bf16[3,3,128,128]{3,2,1,0:T(8,128)(2,1)}, u32[]{:S(2)}) copy-start(bf16[3,3,128,128]{3,2,1,0:T(8,128)(2,1)} %param.13) | copy-start | bytes 884740
  36.6 7.8 %collective-permute-start = (bf16[32,16,128]{2,1,0:T(8,128)(2,1)S(1)}, bf16[32,16,128]{2,1,0:T(8,128)(2,1)S(1)}, u32[]{:S(2)}, u32[]{:S(2)}) collective-permute-start(bf16[32,16,128]{2,1,0:T(8,128)(2,1)S(1)} %slice.13), channel_id=1, source_target_pairs={{112,240},{240,368},{368,496},{496,480},{480,352},{352,224},{224,9... | collective-permute-start | bytes 393224 | tf_op jit(solution)/shard_map/ppermute | solution.py:299
  38.6 7.1 %collective-permute-start.1 = (bf16[32,16,128]{2,1,0:T(8,128)(2,1)S(1)}, bf16[32,16,128]{2,1,0:T(8,128)(2,1)S(1)}, u32[]{:S(2)}, u32[]{:S(2)}) collective-permute-start(bf16[32,16,128]{2,1,0:T(8,128)(2,1)S(1)} %slice.13), channel_id=1, source_target_pairs={{112,15},{240,112},{368,240},{496,368},{480,496},{352,480},{224,35... | collective-permute-start | bytes 393224 | tf_op jit(solution)/shard_map/ppermute | solution.py:299
  42.3 1.0 copy-start.6
  43.5 2.2 %copy-start = (bf16[128,128]{1,0:T(8,128)(2,1)S(1)}, bf16[128,128]{1,0:T(8,128)(2,1)}, u32[]{:S(2)}) copy-start(bf16[128,128]{1,0:T(8,128)(2,1)} %ker.1) | copy-start | bytes 98308
  43.5 2.2 %copy-start.1 = (bf16[128,384]{1,0:T(8,128)(2,1)S(1)}, bf16[128,384]{1,0:T(8,128)(2,1)}, u32[]{:S(2)}) copy-start(bf16[128,384]{1,0:T(8,128)(2,1)} %constant.23.clone.inv) | copy-start | bytes 294916
  43.5 2.2 %copy-start.2 = (bf16[128,384]{1,0:T(8,128)(2,1)S(1)}, bf16[128,384]{1,0:T(8,128)(2,1)}, u32[]{:S(2)}) copy-start(bf16[128,384]{1,0:T(8,128)(2,1)} %constant.25.clone.inv_nat) | copy-start | bytes 294916
  43.5 2.2 %copy-start.3 = (bf16[128,256]{1,0:T(8,128)(2,1)S(1)}, bf16[128,256]{1,0:T(8,128)(2,1)}, u32[]{:S(2)}) copy-start(bf16[128,256]{1,0:T(8,128)(2,1)} %constant.22.clone.fwd) | copy-start | bytes 196612
  43.5 2.2 %copy-start.4 = (bf16[128,256]{1,0:T(8,128)(2,1)S(1)}, bf16[128,256]{1,0:T(8,128)(2,1)}, u32[]{:S(2)}) copy-start(bf16[128,256]{1,0:T(8,128)(2,1)} %constant.24.clone.fwd_nat) | copy-start | bytes 196612
  43.7 0.7 copy-start.7
  43.8 0.7 copy-start.8
  50.5 23.3 %all-to-all-start.1 = ((bf16[32,16,128]{2,1,0:T(8,128)(2,1)}), bf16[32,16,128]{2,1,0:T(8,128)(2,1)S(1)}, u32[]{:S(2)}, u32[]{:S(2)}) async-start(bf16[32,16,128]{2,1,0:T(8,128)(2,1)} %get-tuple-element.16), calls=%async_computation.1 | async-start | bytes 262144 | tf_op jit(solution)/shard_map/all_to_all | solution.py:303
  60.6 3.5 %collective-permute-start.2 = (bf16[1280,128]{1,0:T(8,128)(2,1)S(1)}, bf16[1280,128]{1,0:T(8,128)(2,1)S(1)}, u32[]{:S(2)}, u32[]{:S(2)}) collective-permute-start(bf16[1280,128]{1,0:T(8,128)(2,1)S(1)} %constant_dynamic-slice_fusion), channel_id=1, source_target_pairs={{0,1},{1,0},{2,3},{3,2},{4,5},{5,4},{6,7},{7,6},{8,9},{9,8},{10,11... | collective-permute-start | bytes 983048 | tf_op jit(solution)/shard_map/ppermute | solution.py:272
  103.8 21.5 %all-to-all-start.4 = ((bf16[64,40,128]{2,1,0:T(8,128)(2,1)}), bf16[64,40,128]{2,1,0:T(8,128)(2,1)S(1)}, u32[]{:S(2)}, u32[]{:S(2)}) async-start(bf16[64,40,128]{2,1,0:T(8,128)(2,1)} %shard_map.158), calls=%async_computation.4 | async-start | bytes 1310720 | tf_op jit(solution)/shard_map/all_to_all | solution.py:308
